TPU v7x, 32 devices: a whole 2x2x4 slice. The times are simulated.
32 devices in a mesh: seq: 8 (over z, y), ch: 4 (over x, core).
Axes of the slice: x: 2, y: 2, z: 4, core: 2. Of those that a mesh axis runs over, the one named last changes fastest.
Arguments:
- tokens: bfloat16 [32768, 1024], P('seq', 'ch'), may hold values from -6 to 6
- cotangent: bfloat16 [32768, 1024], P('seq', 'ch'), may hold values from -6 to 6
- first_factor: bfloat16 [16, 64, 64], replicated, may hold values from -0.75 to 0.75
- second_factor: bfloat16 [64, 16, 16], replicated, may hold values from -1.5 to 1.5
- third_factor: bfloat16 [64, 32, 32], replicated, may hold values from -1 to 1
- gate_weight: bfloat16 [1024, 1024], P(None, 'ch'), may hold values from -0.1875 to 0.1875
Outputs:
- output: bfloat16 [32768, 1024], P('seq', 'ch')
- input_grad: bfloat16 [32768, 1024], P('seq', 'ch')
- first_grad: bfloat16 [16, 64, 64], replicated
- second_grad: bfloat16 [64, 16, 16], replicated
- third_grad: bfloat16 [64, 32, 32], replicated
- gate_grad: float32 [1024, 1024], P('seq', 'ch')
All inputs are finite; a program needn't handle non-finite values.
Results may differ from a plain program's by a relative error of at most 0.0068.
Values may be sent and summed in bfloat16 or wider, within the bound.
No kernel may reach another device: no remote copies, remote signals or barrier semaphores. Data moves between devices by JAX's collectives and lax.ppermute only.
A program may use at most 64 MiB of HBM per device.

v0:
```python
import functools

import jax
import jax.numpy as jnp
from jax import lax
from jax.experimental import pallas as pl
from jax.experimental.pallas import tpu as pltpu
from jax.sharding import PartitionSpec as P

A = 32
B = 16
C = 64
PER = 8
F32 = jnp.float32
BF16 = jnp.bfloat16
VMEM_BYTES = 56 * 1024 * 1024


def swap(values, axis, step):
    count = lax.axis_size(axis)
    return lax.ppermute(values, axis, [(i, i ^ step) for i in range(count)])


def flip_blocks(values, dim, index):
    count = values.shape[dim]
    bit = 1
    while bit < count:
        shape = values.shape[:dim] + (count // (2 * bit), 2, bit) + values.shape[dim + 1 :]
        split = values.reshape(shape)
        turned = jnp.flip(split, dim + 1)
        values = jnp.where((index // bit) % 2 == 1, turned, split).reshape(values.shape)
        bit *= 2
    return values


def exchange(pieces):
    moved = {}
    for j in range(len(pieces) - 1, 0, -1):
        moved[j] = swap(pieces[j], "seq", j)
    return [pieces[0]] + [moved[j] for j in range(1, len(pieces))]


def dot(left, right, dims=((1,), (0,))):
    return lax.dot_general(left, right, (dims, ((), ())), preferred_element_type=F32)


def rows_of(block, count):
    return pl.ds(pl.multiple_of(block * count, count), count)


def call(kernel, grid, index, ins, in_specs, outs, out_specs, scratch=(), flops=0):
    moved = sum(x.size * x.dtype.itemsize for x in list(ins) + list(outs))
    return pl.pallas_call(
        kernel,
        grid_spec=pltpu.PrefetchScalarGridSpec(
            num_scalar_prefetch=1,
            grid=grid,
            in_specs=in_specs,
            out_specs=out_specs,
            scratch_shapes=scratch,
        ),
        out_shape=outs,
        compiler_params=pltpu.CompilerParams(
            dimension_semantics=("arbitrary",) * len(grid), vmem_limit_bytes=VMEM_BYTES
        ),
        cost_estimate=pl.CostEstimate(flops=flops, transcendentals=0, bytes_accessed=moved),
    )(index, *ins)


def shape(dims, dtype):
    return jax.ShapeDtypeStruct(dims, dtype)


def whole(x):
    dims = x.shape
    return pl.BlockSpec(dims, lambda *_: (0,) * len(dims))


def by_row(x, parts):
    dims = (x.shape[0] // parts,) + tuple(x.shape[1:])
    return pl.BlockSpec(dims, lambda i, *_: (i,) + (0,) * (len(dims) - 1))


def scatter_rows(source, pieces, me, pair):
    for j, piece in enumerate(pieces):
        low = source[0, rows_of(me ^ j, PER), :]
        high = source[1, rows_of(me ^ j, PER), :]
        piece[0, pair] = jnp.concatenate([low, high], 0).astype(BF16)


def gather_rows(target, pieces, me, pair):
    for j, piece in enumerate(pieces):
        both = piece[0, pair].astype(F32)
        target[0, rows_of(me ^ j, PER), :] = both[:PER]
        target[1, rows_of(me ^ j, PER), :] = both[PER:]


def first_kernel(index, tokens, factor, *rest):
    pieces, held = rest[:-1], rest[-1]
    for pair in range(B // 2):
        for side in range(2):
            b = 2 * pair + side
            held[pair % 2, side] = dot(factor[b], tokens[b * C : (b + 1) * C, :])
        scatter_rows(held.at[pair % 2], pieces, index[0], pair)


def far_kernel(n, own_a, index, *refs):
    first, (second_big, third_big), second_out, pieces = (
        refs[:n], refs[n : n + 2], refs[n + 2], refs[n + 3 :]
    )
    for j in range(n):
        for i in range(own_a):
            block = first[j][i].reshape(B * PER, -1)
            mixed = dot(second_big[...], block).astype(BF16)
            second_out[j * own_a + i] = mixed.reshape(second_out.shape[1:])
    for pair in range(B // 2):
        block = second_out[:, pair].reshape(2 * A * PER, -1)
        mixed = dot(third_big[...], block).astype(BF16).reshape(A, 2 * PER, -1)
        for j in range(n):
            pieces[j][:, pair] = mixed[j * own_a : (j + 1) * own_a]


def gate_kernel(m, index, *refs):
    gathered, (weight, upstream, gate_out), pieces, held = (
        refs[:m], refs[m : m + 3], refs[m + 3 : -1], refs[-1]
    )
    width = weight.shape[1]
    for pair in range(B // 2):
        rows = slice(pair * 2 * C, (pair + 1) * 2 * C)
        gate = 0.0
        for j in range(m):
            gate += dot(gathered[j][rows, :], weight[rows_of(index[1] ^ j, width), :])
        gate_out[rows, :] = gate
        grad = upstream[rows, :].astype(F32) * (gate * jax.nn.sigmoid(gate))
        held[pair % 2] = grad.reshape(2, C, width)
        scatter_rows(held.at[pair % 2], pieces, index[0], pair)


def output_kernel(n, index, *refs):
    pieces, (gate_in, tokens, upstream, output, pre_grad, held) = refs[:n], refs[n:]
    for pair in range(B // 2):
        rows = slice(pair * 2 * C, (pair + 1) * 2 * C)
        gather_rows(held.at[pair % 2], pieces, index[0], pair)
        mixed = held[pair % 2].reshape(2 * C, -1)
        gate = gate_in[rows, :]
        sig = jax.nn.sigmoid(gate)
        output[rows, :] = (tokens[rows, :].astype(F32) + mixed * (gate * sig)).astype(BF16)
        pre_grad[rows, :] = (
            upstream[rows, :].astype(F32) * mixed * sig * (1.0 + gate * (1.0 - sig))
        ).astype(BF16)


def split_dot(values, selector):
    top = values.astype(BF16)
    rest = values - top.astype(F32)
    middle = rest.astype(BF16)
    low = (rest - middle.astype(F32)).astype(BF16)
    return dot(top, selector) + dot(middle, selector) + dot(low, selector)


def back_kernel(n, own_a, index, *refs):
    grads, (second_big, third_big, back_second), pieces = refs[:n], refs[n : n + 3], refs[n + 3 :]
    for pair in range(B // 2):
        block = jnp.concatenate([g[:, pair].reshape(own_a * 2 * PER, -1) for g in grads], 0)
        back = dot(third_big[...], block).astype(BF16)
        back_second[:, pair] = back.reshape(A, 2 * PER, -1)
    for j in range(n):
        for i in range(own_a):
            block = back_second[j * own_a + i].reshape(B * PER, -1)
            pieces[j][i] = dot(second_big[...], block).astype(BF16).reshape(pieces[j].shape[1:])


def far_grad_kernel(n, own_a, index, *refs):
    grads, first = refs[:n], refs[n : 2 * n]
    second_val, back_second, sums, third_acc, second_acc = refs[2 * n :]
    big = 2 * A * PER
    small = B * PER
    for pair in range(B // 2):
        block = jnp.concatenate([g[:, pair].reshape(own_a * 2 * PER, -1) for g in grads], 0)
        part = dot(block, second_val[:, pair].reshape(big, -1), ((1,), (1,)))
        third_acc[...] = part if pair == 0 else third_acc[...] + part
    for j in range(n):
        for i in range(own_a):
            block = back_second[j * own_a + i].reshape(small, -1)
            part = dot(block, first[j][i].reshape(small, -1), ((1,), (1,)))
            second_acc[...] = part if j + i == 0 else second_acc[...] + part
    tall = own_a * 2 * PER
    row = lax.broadcasted_iota(jnp.int32, (tall, big), 0)
    col = lax.broadcasted_iota(jnp.int32, (tall, big), 1)
    keep = row % (2 * PER) == col % (2 * PER)
    source = lax.broadcasted_iota(jnp.int32, (big, 128), 0) // (2 * PER)
    source = ((source // own_a) ^ index[0]) * own_a + source % own_a
    lane = lax.broadcasted_iota(jnp.int32, (big, 128), 1)
    selector = (lane == source).astype(BF16)
    for block in range(n):
        picked = jnp.where(keep, third_acc[rows_of(index[0] ^ block, tall), :], 0.0)
        found = split_dot(picked, selector)
        total = found[: 2 * PER]
        for i in range(1, own_a):
            total += pltpu.roll(found[i * 2 * PER : (i + 1) * 2 * PER], i * A, 1)
        sums[block * PER : (block + 1) * PER, :] = total[:PER] + total[PER:]
    row = lax.broadcasted_iota(jnp.int32, (2 * PER, small), 0)
    col = lax.broadcasted_iota(jnp.int32, (2 * PER, small), 1)
    keep = row % PER == col % PER
    expand = lax.broadcasted_iota(jnp.int32, (small, 128), 0) // PER
    lane = lax.broadcasted_iota(jnp.int32, (small, 128), 1)
    total = 0.0
    for g in range(small // (2 * PER)):
        picked = jnp.where(keep, second_acc[g * 2 * PER : (g + 1) * 2 * PER, :], 0.0)
        total += split_dot(picked, (lane == expand + g * B).astype(BF16))
    sums[n * PER :, :] = total


def gate_grad_kernel(m, index, *refs):
    gathered, pre_grad, out = refs[:m], refs[m], refs[m + 1]
    width = pre_grad.shape[1]

    @pl.when(pl.program_id(0) == 0)
    def _():
        out[...] = jnp.zeros_like(out)

    for j in range(m):
        out[rows_of(index[1] ^ j, width), :] += dot(
            gathered[j][...], pre_grad[...], ((0,), (0,))
        )


def gate_input_kernel(m, index, *refs):
    grads, weights, upstream, out = refs[:m], refs[m : 2 * m], refs[2 * m], refs[2 * m + 1]
    total = upstream[...].astype(F32)
    for j in range(m):
        total += dot(grads[j][...], weights[j][...], ((1,), (1,)))
    out[...] = total


def first_grad_kernel(n, index, *refs):
    pieces, (tokens, back, out, held) = refs[:n], refs[n:]

    @pl.when(pl.program_id(0) == 0)
    def _():
        out[...] = jnp.zeros_like(out)

    for pair in range(B // 2):
        gather_rows(held.at[pair % 2], pieces, index[0], pair)
        sides = []
        for side in range(2):
            rows = slice((2 * pair + side) * C, (2 * pair + side + 1) * C)
            value = held[pair % 2, side].astype(BF16)
            back[rows, :] = value
            sides.append(dot(value, tokens[rows, :], ((1,), (1,))))
        both = jnp.concatenate(sides, 1).reshape(C // PER, PER, 2 * C)
        out[:, pair] += both


def input_grad_kernel(index, back, factor, partial, out):
    for b in range(B):
        rows = slice(b * C, (b + 1) * C)
        mixed = dot(factor[b], back[rows, :], ((0,), (0,)))
        out[rows, :] = (partial[rows, :] + mixed).astype(BF16)


def spread_diagonal(values, copies):
    rows, c, cols = values.shape
    tall = jnp.broadcast_to(values[:, None], (rows, copies, c, cols))
    tall = tall.reshape(rows * copies * c, cols)
    wide = cols * copies * c
    expand = (
        lax.broadcasted_iota(jnp.int32, (cols, wide), 1) // (copies * c)
        == lax.broadcasted_iota(jnp.int32, (cols, wide), 0)
    ).astype(BF16)
    dims = (tall.shape[0], wide)
    keep = (
        lax.broadcasted_iota(jnp.int32, dims, 0) % (copies * c)
        == lax.broadcasted_iota(jnp.int32, dims, 1) % (copies * c)
    )
    return jnp.where(keep, dot(tall, expand), 0.0).astype(BF16)


def resident(tokens, cotangent, first_factor, second_factor, third_factor, gate_weight):
    n = lax.axis_size("seq")
    s = lax.axis_index("seq")
    m = lax.axis_size("ch")
    q = lax.axis_index("ch")
    rows, width = tokens.shape
    own_a = rows // (B * C)
    index = jnp.stack([s, q]).astype(jnp.int32)
    piece = shape((own_a, B // 2, 2 * PER, width), BF16)
    piece_rows = [by_row(piece, own_a)] * n
    row_blocks = by_row(tokens, own_a)
    pair_rows = pltpu.VMEM((2, 2, C, width), F32)

    far_tokens = swap(tokens, "ch", 2)
    sent = call(
        first_kernel, (own_a,), index, (tokens, first_factor),
        [row_blocks, whole(first_factor)], [piece] * n, piece_rows, [pair_rows],
        2 * rows * width * C,
    )
    first_far = exchange(sent)
    gathered = [tokens, swap(tokens, "ch", 1), far_tokens, swap(far_tokens, "ch", 1)]
    weight_rows = [
        lax.dynamic_slice_in_dim(gate_weight, (q ^ j) * width, width, 0) for j in range(m)
    ]
    back_weight = [weight_rows[0]] + [swap(weight_rows[j], "ch", j) for j in range(1, m)]

    second_own = lax.dynamic_slice_in_dim(second_factor, s * PER, PER, 0)
    third_own = lax.dynamic_slice_in_dim(third_factor, s * PER, PER, 0)
    third_own = third_own.reshape(PER, n, own_a, n, own_a)
    third_own = flip_blocks(flip_blocks(third_own, 1, s), 3, s).reshape(PER, A, A)
    second_big = spread_diagonal(second_own.transpose(1, 0, 2), 1)
    third_big = spread_diagonal(third_own.transpose(1, 0, 2), 2)
    second_back = spread_diagonal(second_own.transpose(2, 0, 1), 1)
    third_back = spread_diagonal(third_own.transpose(2, 0, 1), 2)

    far = shape((A, B // 2, 2 * PER, width), BF16)
    ins = (*first_far, second_big, third_big)
    outs = [far] + [piece] * n
    second_far, *sent = call(
        functools.partial(far_kernel, n, own_a), (1,), index, ins,
        [whole(x) for x in ins], outs, [whole(x) for x in outs],
        (), 2 * rows * width * 6 * C,
    )
    mixed_home = exchange(sent)

    gate_shape = shape((rows, width), F32)
    ins = (*gathered, gate_weight, cotangent)
    gate_pre, *sent = call(
        functools.partial(gate_kernel, m), (own_a,), index, ins,
        [row_blocks] * m + [whole(gate_weight), row_blocks],
        [gate_shape] + [piece] * n, [row_blocks] + piece_rows, [pair_rows],
        2 * rows * width * m * width,
    )
    grad_far = exchange(sent)

    ins = (*mixed_home, gate_pre, tokens, cotangent)
    output, pre_grad = call(
        functools.partial(output_kernel, n), (own_a,), index, ins,
        piece_rows + [row_blocks] * 3, [shape((rows, width), BF16)] * 2, [row_blocks] * 2,
        [pair_rows], rows * width * 16,
    )
    far_pre = swap(pre_grad, "ch", 2)
    all_pre = [pre_grad, swap(pre_grad, "ch", 1), far_pre, swap(far_pre, "ch", 1)]

    ins = (*grad_far, second_back, third_back)
    outs = [far] + [piece] * n
    back_second, *sent = call(
        functools.partial(back_kernel, n, own_a), (1,), index, ins,
        [whole(x) for x in ins], outs, [whole(x) for x in outs], (),
        2 * rows * width * 6 * C,
    )
    back_home = exchange(sent)
    ins = (*grad_far, *first_far, second_far, back_second)
    outs = [shape((n * PER + 2 * PER, 128), F32)]
    sums = call(
        functools.partial(far_grad_kernel, n, own_a), (1,), index, ins,
        [whole(x) for x in ins], outs, [whole(x) for x in outs],
        [
            pltpu.VMEM((2 * A * PER, 2 * A * PER), F32),
            pltpu.VMEM((B * PER, B * PER), F32),
        ],
        2 * rows * width * 10 * C,
    )[0]

    out = shape((m * width, width), F32)
    gate_part = call(
        functools.partial(gate_grad_kernel, m), (own_a,), index, (*gathered, pre_grad),
        [row_blocks] * (m + 1), [out], [whole(out)], (),
        2 * rows * width * m * width,
    )[0].reshape(n, m * width // n, width)
    bit = 1
    while bit < n:
        mine = (s // bit) % 2
        split = gate_part.reshape(n // (2 * bit), 2, *gate_part.shape[1:])
        keep = lax.dynamic_index_in_dim(split, mine, 1, False)
        send = lax.dynamic_index_in_dim(split, 1 - mine, 1, False)
        gate_part = keep + swap(send, "seq", bit)
        bit *= 2
    gate_grad = gate_part.reshape(m * width // n, width)

    ins = (*all_pre, *back_weight, cotangent)
    partial = call(
        functools.partial(gate_input_kernel, m), (own_a,), index, ins,
        [row_blocks] * m + [whole(w) for w in back_weight] + [row_blocks],
        [gate_shape], [row_blocks], (), 2 * rows * width * m * width,
    )[0]

    bit = m // 2
    while bit:
        sums = sums + swap(sums, "ch", bit)
        bit //= 2
    every = sums.astype(BF16)[None]
    bit = 1
    while bit < n:
        other = swap(every, "seq", bit)
        every = jnp.where(
            (s // bit) % 2 == 1,
            jnp.concatenate([other, every], 0),
            jnp.concatenate([every, other], 0),
        )
        bit *= 2
    third_all = every[:, : n * PER].reshape(n, n, PER, 128).transpose(0, 2, 1, 3)
    third_grad = third_all.reshape(C, A, A)
    second_all = every[:, n * PER :].reshape(n, 2, PER, B // 2, B)
    second_grad = second_all.transpose(0, 2, 3, 1, 4).reshape(C, B, B)

    ins = (*back_home, tokens)
    first_out = shape((n, B // 2, PER, 2 * C), F32)
    back_rows, first_part = call(
        functools.partial(first_grad_kernel, n), (own_a,), index, ins,
        piece_rows + [row_blocks], [shape((rows, width), BF16), first_out],
        [row_blocks, whole(first_out)], [pair_rows], 2 * rows * width * C,
    )
    parts = first_part.reshape(n * m, -1, 128)
    parts = lax.all_to_all(parts, ("seq", "ch"), split_axis=0, concat_axis=0, tiled=True)
    first_sum = parts.sum(0).astype(BF16)
    first_sum = lax.all_to_all(
        jnp.broadcast_to(first_sum[None], (n * m, *first_sum.shape)),
        ("seq", "ch"), split_axis=0, concat_axis=0, tiled=True,
    )
    first_grad = first_sum.reshape(n, B // 2, PER, 2, C).transpose(1, 3, 0, 2, 4)
    first_grad = first_grad.reshape(B, C, C)

    ins = (back_rows, first_factor, partial)
    input_grad = call(
        input_grad_kernel, (own_a,), index, ins,
        [row_blocks, whole(first_factor), row_blocks],
        [shape((rows, width), BF16)], [row_blocks], (), 2 * rows * width * C,
    )[0]
    return output, input_grad, first_grad, second_grad, third_grad, gate_grad


def spread_out(tokens, cotangent, first_factor, second_factor, third_factor, gate_weight):
    seq_count = lax.axis_size("seq")
    seq_index = lax.axis_index("seq")
    per_device_c = max(1, C // seq_count)
    splits = max(1, seq_count // C)
    local_rows, width = tokens.shape
    narrow = width // splits
    blocks = local_rows // C
    batch_b = min(blocks, B)
    start_b = seq_index * blocks % B
    if blocks >= B:
        first_sel = first_factor
    else:
        first_sel = lax.dynamic_slice_in_dim(first_factor, start_b, blocks, 0)
    column = seq_index // splits * per_device_c
    second_sel = lax.dynamic_slice_in_dim(second_factor, column, per_device_c, 0)
    third_sel = lax.dynamic_slice_in_dim(third_factor, column, per_device_c, 0)
    grid_view = tokens.reshape(blocks // batch_b, batch_b, C, width)
    mixed_first = jnp.einsum(
        "bcd,ibdh->ibch", first_sel, grid_view, preferred_element_type=jnp.float32
    ).astype(jnp.bfloat16)

    def spread(values):
        return values.reshape(blocks, seq_count, per_device_c, narrow)

    received = lax.all_to_all(spread(mixed_first), "seq", split_axis=1, concat_axis=0, tiled=True)
    item_count = received.shape[3]
    far_view = received.reshape(A, B, per_device_c, item_count)
    second_val = jnp.einsum(
        "kbe,aekh->abkh", second_sel, far_view, preferred_element_type=jnp.float32
    ).astype(jnp.bfloat16)
    third_val = jnp.einsum(
        "kae,ebkh->abkh", third_sel, second_val, preferred_element_type=jnp.float32
    ).astype(jnp.bfloat16)
    first_far = received
    second_far = second_val.reshape(A * B, 1, per_device_c, item_count)
    mixed_far = third_val.reshape(A * B, 1, per_device_c, item_count)
    mixed_back = lax.all_to_all(mixed_far, "seq", split_axis=0, concat_axis=1, tiled=True).reshape(
        local_rows, width
    )
    full_tokens, full_weight = (
        lax.all_gather(tokens, "ch", axis=1, tiled=True),
        lax.all_gather(gate_weight, "ch", axis=1, tiled=True),
    )
    own_rows = lax.dynamic_slice_in_dim(full_weight, lax.axis_index("ch") * width, width, 0)
    gate_pre = jnp.dot(full_tokens, gate_weight, preferred_element_type=jnp.float32)
    sigmoid_gate = jax.nn.sigmoid(gate_pre)
    activation = gate_pre * sigmoid_gate
    mixed_float = mixed_back.astype(jnp.float32)
    output = (tokens.astype(jnp.float32) + mixed_float * activation).astype(jnp.bfloat16)
    upstream = cotangent.astype(jnp.float32)
    mix_grad = (upstream * activation).astype(jnp.bfloat16)
    pre_grad = (
        upstream * mixed_float * sigmoid_gate * (1.0 + gate_pre * (1.0 - sigmoid_gate))
    ).astype(jnp.bfloat16)
    received = lax.all_to_all(spread(mix_grad), "seq", split_axis=1, concat_axis=0, tiled=True)
    item_count = received.shape[3]
    far_view = received.reshape(A, B, per_device_c, item_count)
    back_second = jnp.einsum(
        "kae,abkh->ebkh", third_sel, far_view, preferred_element_type=jnp.float32
    ).astype(jnp.bfloat16)
    back_first = jnp.einsum(
        "kbe,abkh->aekh", second_sel, back_second, preferred_element_type=jnp.float32
    ).astype(jnp.bfloat16)
    second_back = back_second.reshape(A * B, 1, per_device_c, item_count)
    first_back = back_first.reshape(A * B, 1, per_device_c, item_count)
    third_part = jnp.einsum(
        "abkh,ebkh->kae",
        received.reshape(A, B, per_device_c, narrow),
        second_far.reshape(A, B, per_device_c, narrow),
        preferred_element_type=jnp.float32,
    )
    second_part = jnp.einsum(
        "abkh,aekh->kbe",
        second_back.reshape(A, B, per_device_c, narrow),
        first_far.reshape(A, B, per_device_c, narrow),
        preferred_element_type=jnp.float32,
    )
    first_home = lax.all_to_all(first_back, "seq", split_axis=0, concat_axis=1, tiled=True).reshape(
        blocks // batch_b, batch_b, C, width
    )
    mix_input = jnp.einsum(
        "bcd,ibch->ibdh", first_sel, first_home, preferred_element_type=jnp.float32
    ).reshape(local_rows, width)
    first_part = jnp.einsum(
        "ibch,ibdh->bcd", first_home, grid_view, preferred_element_type=jnp.float32
    )
    if blocks >= B:
        first_full = first_part
    else:
        first_full = lax.dynamic_update_slice_in_dim(
            jnp.zeros((B, C, C), jnp.float32), first_part, start_b, 0
        )
    second_full = lax.dynamic_update_slice_in_dim(
        jnp.zeros((C, B, B), jnp.float32), second_part, column, 0
    )
    third_full = lax.dynamic_update_slice_in_dim(
        jnp.zeros((C, A, A), jnp.float32), third_part, column, 0
    )
    first_sum, second_sum, third_sum = lax.psum(
        (first_full, second_full, third_full), ("seq", "ch")
    )
    gate_input = lax.dot_general(
        lax.all_gather(pre_grad, "ch", axis=1, tiled=True),
        own_rows,
        (((1,), (1,)), ((), ())),
        preferred_element_type=jnp.float32,
    )
    gate_grad = lax.psum_scatter(
        lax.dot_general(
            full_tokens, pre_grad, (((0,), (0,)), ((), ())), preferred_element_type=jnp.float32
        ),
        "seq",
        scatter_dimension=0,
        tiled=True,
    )
    input_grad = (upstream + mix_input + gate_input).astype(jnp.bfloat16)
    return (
        output,
        input_grad,
        first_sum.astype(jnp.bfloat16),
        second_sum.astype(jnp.bfloat16),
        third_sum.astype(jnp.bfloat16),
        gate_grad,
    )


def on_device(*arrays):
    n = lax.axis_size("seq")
    rows = arrays[0].shape[0]
    square = lax.axis_size("ch") == 4 and n * PER == C
    if square and rows % (B * C) == 0 and rows * n == A * B * C:
        return resident(*arrays)
    return spread_out(*arrays)


def solution(mesh):
    placed = (P("seq", "ch"), P("seq", "ch"), P(), P(), P(), P(None, "ch"))
    return jax.shard_map(
        on_device,
        mesh=mesh,
        in_specs=placed,
        out_specs=(P("seq", "ch"), P("seq", "ch"), P(), P(), P(), P("seq", "ch")),
        check_vma=False,
    )
```

profile of v0, /device:TPU:0, one launch (start us, length us, event | category | flops | bytes accessed | tf_op | source)
XLA Modules:
  0.0 363.5 jit_solution(2506900685494760963)
XLA Ops:
  0.7 3.0 collective-permute-start.15
  4.3 5.0 %shard_map.109 = (bf16[4,8,16,256]{3,2,1,0:T(8,128)(2,1)}, bf16[4,8,16,256]{3,2,1,0:T(8,128)(2,1)}, bf16[4,8,16,256]{3,2,1,0:T(8,128)(2,1)}, bf16[4,8,16,256]{3,...) custom-call(s32[2]{0:T(128)} %pad_add_fusion.index, ...), custom_call_target="tpu_custom_call" | custom-call | flops 134217728 | bytes 4325376 | tf_op jit(solution)/shard_map/pallas_call | solution.py:53
  13.4 36.1 %collective-permute-done.15.refs_2_ = bf16[4096,256]{1,0:T(8,128)(2,1)S(1)} collective-permute-done((bf16[4096,256]{1,0:T(8,128)(2,1)}, bf16[4096,256]{1,0:T(8,128)(2,1)S(1)}, u32[]{:S(2)}, u32[]{:S(2)}) %collective-permute-start.15) | collective-permute-done | bytes 2097184 | tf_op jit(solution)/shard_map/ppermute | solution.py:21
  52.9 2.9 collective-permute-start.3
  57.3 3.6 collective-permute-start.5
  60.9 19.3 %collective-permute-done.3.refs_4_.refs_12_ = bf16[4,8,16,256]{3,2,1,0:T(8,128)(2,1)} collective-permute-done((bf16[4,8,16,256]{3,2,1,0:T(8,128)(2,1)}, bf16[4,8,16,256]{3,2,1,0:T(8,128)(2,1)}, u32[]{:S(2)}, u32[]{:S(2)}) %collective-permute-start.3) | collective-permute-done | bytes 262176 | tf_op jit(solution)/shard_map/ppermute | solution.py:21
  80.2 4.2 %collective-permute-start.6 = (bf16[4,8,16,256]{3,2,1,0:T(8,128)(2,1)}, bf16[4,8,16,256]{3,2,1,0:T(8,128)(2,1)}, u32[]{:S(2)}, u32[]{:S(2)}) collective-permute-start(bf16[4,8,16,256]{3,2,1,0:T(8,128)(2,1)} %get-tuple-element.52), channel_id=1, source_target_pairs={{0,28},{4,24},{8,20},{12,16},{16,12},{20,8},{24,4},{28,0},{1,29},{... | collective-permute-start | bytes 786440 | tf_op jit(solution)/shard_map/ppermute | solution.py:21
  85.2 1.8 fusion.refs_9_
  87.0 5.6 %collective-permute-done.4.refs_5_.refs_13_ = bf16[4,8,16,256]{3,2,1,0:T(8,128)(2,1)} collective-permute-done((bf16[4,8,16,256]{3,2,1,0:T(8,128)(2,1)}, bf16[4,8,16,256]{3,2,1,0:T(8,128)(2,1)}, u32[]{:S(2)}, u32[]{:S(2)}) %collective-permute-start.4) | collective-permute-done | bytes 262176 | tf_op jit(solution)/shard_map/ppermute | solution.py:21
  92.7 6.0 %shard_map.110 = (bf16[32,8,16,256]{3,2,1,0:T(8,128)(2,1)}, bf16[4,8,16,256]{3,2,1,0:T(8,128)(2,1)}, bf16[4,8,16,256]{3,2,1,0:T(8,128)(2,1)}, bf16[4,8,16,256]{3...) custom-call(s32[2]{0:T(128)} %pad_add_fusion.index, ...), custom_call_target="tpu_custom_call" | custom-call | flops 805306368 | bytes 6848512 | tf_op jit(solution)/shard_map/pallas_call | solution.py:53
  98.7 13.3 %collective-permute-start.10 = (bf16[4,8,16,256]{3,2,1,0:T(8,128)(2,1)}, bf16[4,8,16,256]{3,2,1,0:T(8,128)(2,1)S(1)}, u32[]{:S(2)}, u32[]{:S(2)}) collective-permute-start(bf16[4,8,16,256]{3,2,1,0:T(8,128)(2,1)} %get-tuple-element.57), channel_id=1, source_target_pairs={{0,16},{4,20},{8,24},{12,28},{16,0},{20,4},{24,8},{28,12},{1,17},{... | collective-permute-start | bytes 786440 | tf_op jit(solution)/shard_map/ppermute | solution.py:21
  112.5 22.7 %collective-permute-done.10.refs_4_ = bf16[4,8,16,256]{3,2,1,0:T(8,128)(2,1)S(1)} collective-permute-done((bf16[4,8,16,256]{3,2,1,0:T(8,128)(2,1)}, bf16[4,8,16,256]{3,2,1,0:T(8,128)(2,1)S(1)}, u32[]{:S(2)}, u32[]{:S(2)}) %collective-permute-start.10) | collective-permute-done | bytes 262176 | tf_op jit(solution)/shard_map/ppermute | solution.py:21
  136.6 10.4 %collective-permute-done.11.refs_5_ = bf16[4,8,16,256]{3,2,1,0:T(8,128)(2,1)S(1)} collective-permute-done((bf16[4,8,16,256]{3,2,1,0:T(8,128)(2,1)}, bf16[4,8,16,256]{3,2,1,0:T(8,128)(2,1)S(1)}, u32[]{:S(2)}, u32[]{:S(2)}) %collective-permute-start.11) | collective-permute-done | bytes 262176 | tf_op jit(solution)/shard_map/ppermute | solution.py:21
  147.9 2.6 collective-permute-start.9
  150.6 9.4 %shard_map.111 = (f32[4096,256]{1,0:T(8,128)}, bf16[4,8,16,256]{3,2,1,0:T(8,128)(2,1)}, bf16[4,8,16,256]{3,2,1,0:T(8,128)(2,1)}, bf16[4,8,16,256]{3,2,1,0:T(8,12...) custom-call(s32[2]{0:T(128)} %pad_add_fusion.index, ...), custom_call_target="tpu_custom_call" | custom-call | flops 2147483648 | bytes 17301504 | tf_op jit(solution)/shard_map/pallas_call | solution.py:53
  160.1 1.7 collective-permute-done.9.refs_3_
  162.6 8.1 %shard_map.112 = (bf16[4096,256]{1,0:T(8,128)(2,1)}, bf16[4096,256]{1,0:T(8,128)(2,1)}) custom-call(s32[2]{0:T(128)} %pad_add_fusion.index, bf16[4,8,16,256]{3,2,1,0:T(8,128)(2,1)} %get-tuple-element.53.refs_0_, bf16[4,8,16,256]{3,2,1,0:T(8,128)(2,1)} %copy-done.26, bf16[4,8,16,256]{3,2,1,0:T(8,128)(2,1)} %copy-done.27, bf16[4,8,16,256]{3,2,1,0:T(8,128)(2,1)} %copy-done.28, ...), custom_call_target="tpu_custom_call" | custom-call | flops 16777216 | bytes 14680064 | tf_op jit(solution)/shard_map/pallas_call | solution.py:53
  173.8 2.1 collective-permute-start.18
  178.6 3.7 %collective-permute-start.20 = (bf16[4,8,16,256]{3,2,1,0:T(8,128)(2,1)S(1)}, bf16[4,8,16,256]{3,2,1,0:T(8,128)(2,1)S(1)}, u32[]{:S(2)}, u32[]{:S(2)}) collective-permute-start(bf16[4,8,16,256]{3,2,1,0:T(8,128)(2,1)S(1)} %copy-done.35), channel_id=1, source_target_pairs={{0,16},{4,20},{8,24},{12,28},{16,0},{20,4},{24,8},{28,12},{1,17},{... | collective-permute-start | bytes 786440 | tf_op jit(solution)/shard_map/ppermute | solution.py:21
  182.3 2.3 collective-permute-start.21
  184.5 6.3 %collective-permute-done.18.refs_2_ = bf16[4,8,16,256]{3,2,1,0:T(8,128)(2,1)S(1)} collective-permute-done((bf16[4,8,16,256]{3,2,1,0:T(8,128)(2,1)}, bf16[4,8,16,256]{3,2,1,0:T(8,128)(2,1)S(1)}, u32[]{:S(2)}, u32[]{:S(2)}) %collective-permute-start.18) | collective-permute-done | bytes 262176 | tf_op jit(solution)/shard_map/ppermute | solution.py:21
  192.2 3.4 collective-permute-done.19.refs_3_
  197.0 7.6 %shard_map.118 = f32[1024,256]{1,0:T(8,128)} custom-call(s32[2]{0:T(128)} %pad_add_fusion.index, bf16[4096,256]{1,0:T(8,128)(2,1)} %refs_0_.3, bf16[4096,256]{1,0:T(8,128)(2,1)} %collective-permute-done.14.refs_1_, bf16[4096,256]{1,0:T(8,128)(2,1)} %copy-done.2, bf16[4096,256]{1,0:T(8,128)(2,1)} %collective-permute-done.16.refs_3_, ...), custom_call_target="tpu_custom_call" | custom-call | flops 2147483648 | bytes 11534336 | tf_op jit(solution)/shard_map/pallas_call | solution.py:53
  205.6 6.3 %collective-permute-done.20.refs_4_ = bf16[4,8,16,256]{3,2,1,0:T(8,128)(2,1)S(1)} collective-permute-done((bf16[4,8,16,256]{3,2,1,0:T(8,128)(2,1)S(1)}, bf16[4,8,16,256]{3,2,1,0:T(8,128)(2,1)S(1)}, u32[]{:S(2)}, u32[]{:S(2)}) %collective-permute-start.20) | collective-permute-done | bytes 262176 | tf_op jit(solution)/shard_map/ppermute | solution.py:21
  212.0 4.9 %collective-permute-done.21.refs_5_ = bf16[4,8,16,256]{3,2,1,0:T(8,128)(2,1)S(1)} collective-permute-done((bf16[4,8,16,256]{3,2,1,0:T(8,128)(2,1)S(1)}, bf16[4,8,16,256]{3,2,1,0:T(8,128)(2,1)S(1)}, u32[]{:S(2)}, u32[]{:S(2)}) %collective-permute-start.21) | collective-permute-done | bytes 262176 | tf_op jit(solution)/shard_map/ppermute | solution.py:21
  217.8 5.6 %shard_map.113 = (bf16[32,8,16,256]{3,2,1,0:T(8,128)(2,1)}, bf16[4,8,16,256]{3,2,1,0:T(8,128)(2,1)}, bf16[4,8,16,256]{3,2,1,0:T(8,128)(2,1)}, bf16[4,8,16,256]{3...) custom-call(s32[2]{0:T(128)} %pad_add_fusion.index, ...), custom_call_target="tpu_custom_call" | custom-call | flops 805306368 | bytes 6848512 | tf_op jit(solution)/shard_map/pallas_call | solution.py:53
  223.4 8.0 %shard_map.117 = f32[80,128]{1,0:T(8,128)} custom-call(s32[2]{0:T(128)} %pad_add_fusion.index, bf16[4,8,16,256]{3,2,1,0:T(8,128)(2,1)} %get-tuple-element.63.refs_0_, bf16[4,8,16,256]{3,2,1,0:T(8,128)(2,1)} %copy-done.12, bf16[4,8,16,256]{3,2,1,0:T(8,128)(2,1)} %copy-done.13, bf16[4,8,16,256]{3,2,1,0:T(8,128)(2,1)} %copy-done.14, ...), custom_call_target="tpu_custom_call" | custom-call | flops 1342177280 | bytes 8429568 | tf_op jit(solution)/shard_map/pallas_call | solution.py:53
  231.9 3.7 %collective-permute-done.37 = f32[80,128]{1,0:T(8,128)S(1)} collective-permute-done((f32[80,128]{1,0:T(8,128)}, f32[80,128]{1,0:T(8,128)S(1)}, u32[]{:S(2)}, u32[]{:S(2)}) %collective-permute-start.37) | collective-permute-done | bytes 40992 | tf_op jit(solution)/shard_map/ppermute | solution.py:21
  236.9 2.1 collective-permute-start.24
  239.8 6.2 %collective-permute-done.39 = bf16[1,80,128]{2,1,0:T(8,128)(2,1)S(1)} collective-permute-done((bf16[1,80,128]{2,1,0:T(8,128)(2,1)S(1)}, bf16[1,80,128]{2,1,0:T(8,128)(2,1)S(1)}, u32[]{:S(2)}, u32[]{:S(2)}) %collective-permute-start.39) | collective-permute-done | bytes 20512 | tf_op jit(solution)/shard_map/ppermute | solution.py:21
  246.0 9.1 %collective-permute-start.40 = (bf16[2,80,128]{2,1,0:T(8,128)(2,1)S(1)}, bf16[2,80,128]{2,1,0:T(8,128)(2,1)S(1)}, u32[]{:S(2)}, u32[]{:S(2)}) collective-permute-start(bf16[2,80,128]{2,1,0:T(8,128)(2,1)S(1)} %maximum_select_fusion.2), channel_id=1, source_target_pairs={{0,8},{4,12},{8,0},{12,4},{16,24},{20,28},{24,16},{28,20},{1,9},{5... | collective-permute-start | bytes 122888 | tf_op jit(solution)/shard_map/ppermute | solution.py:21
  255.1 2.0 collective-permute-done.40
  257.0 2.0 collective-permute-start.25
  260.1 2.9 collective-permute-start.27
  263.0 9.2 %collective-permute-done.25.refs_2_ = bf16[4,8,16,256]{3,2,1,0:T(8,128)(2,1)} collective-permute-done((bf16[4,8,16,256]{3,2,1,0:T(8,128)(2,1)}, bf16[4,8,16,256]{3,2,1,0:T(8,128)(2,1)}, u32[]{:S(2)}, u32[]{:S(2)}) %collective-permute-start.25) | collective-permute-done | bytes 262176 | tf_op jit(solution)/shard_map/ppermute | solution.py:21
  272.2 4.2 %collective-permute-start.28 = (bf16[4,8,16,256]{3,2,1,0:T(8,128)(2,1)}, bf16[4,8,16,256]{3,2,1,0:T(8,128)(2,1)S(1)}, u32[]{:S(2)}, u32[]{:S(2)}) collective-permute-start(bf16[4,8,16,256]{3,2,1,0:T(8,128)(2,1)} %get-tuple-element.76), channel_id=1, source_target_pairs={{0,20},{4,16},{8,28},{12,24},{16,4},{20,0},{24,12},{28,8},{1,21},{... | collective-permute-start | bytes 786440 | tf_op jit(solution)/shard_map/ppermute | solution.py:21
  276.4 2.7 collective-permute-done.26.refs_3_
  279.1 2.4 collective-permute-start.29
  283.5 17.2 %collective-permute-done.28.refs_5_ = bf16[4,8,16,256]{3,2,1,0:T(8,128)(2,1)S(1)} collective-permute-done((bf16[4,8,16,256]{3,2,1,0:T(8,128)(2,1)}, bf16[4,8,16,256]{3,2,1,0:T(8,128)(2,1)S(1)}, u32[]{:S(2)}, u32[]{:S(2)}) %collective-permute-start.28) | collective-permute-done | bytes 262176 | tf_op jit(solution)/shard_map/ppermute | solution.py:21
  300.7 5.6 %collective-permute-start.41 = (bf16[4,80,128]{2,1,0:T(8,128)(2,1)S(1)}, bf16[4,80,128]{2,1,0:T(8,128)(2,1)}, u32[]{:S(2)}, u32[]{:S(2)}) collective-permute-start(bf16[4,80,128]{2,1,0:T(8,128)(2,1)S(1)} %maximum_select_fusion.1), channel_id=1, source_target_pairs={{0,16},{4,20},{8,24},{12,28},{16,0},{20,4},{24,8},{28,12},{1,17},{... | collective-permute-start | bytes 245768 | tf_op jit(solution)/shard_map/ppermute | solution.py:21
  307.1 5.9 %shard_map.114 = (bf16[4096,256]{1,0:T(8,128)(2,1)}, f32[8,8,8,128]{3,2,1,0:T(8,128)}) custom-call(s32[2]{0:T(128)} %pad_add_fusion.index, bf16[4,8,16,256]{3,2,1,0:T(8,128)(2,1)} %get-tuple-element.71.refs_0_, bf16[4,8,16,256]{3,2,1,0:T(8,128)(2,1)} %collective-permute-done.24.refs_1_, bf16[4,8,16,256]{3,2,1,0:T(8,128)(2,1)} %collective-permute-done.25.refs_2_, ...), custom_call_target="tpu_custom_call" | custom-call | flops 134217728 | bytes 6553600 | tf_op jit(solution)/shard_map/pallas_call | solution.py:53
  313.0 8.4 %all-to-all-start = ((f32[32,16,128]{2,1,0:T(8,128)}), f32[32,16,128]{2,1,0:T(8,128)}, u32[]{:S(2)}, u32[]{:S(2)}) async-start(f32[32,16,128]{2,1,0:T(8,128)} %bitcast.69), calls=%async_computation | async-start | bytes 524288 | tf_op jit(solution)/shard_map/all_to_all | solution.py:413
  322.5 1.6 collective-permute-start.35
  326.8 2.4 collective-permute-start.44
  329.2 3.1 all-to-all-done
  333.9 4.6 %all-to-all-start.1 = ((bf16[32,16,128]{2,1,0:T(8,128)(2,1)}), bf16[32,16,128]{2,1,0:T(8,128)(2,1)S(1)}, u32[]{:S(2)}, u32[]{:S(2)}) async-start(bf16[32,16,128]{2,1,0:T(8,128)(2,1)} %broadcast_in_dim.35), calls=%async_computation.1 | async-start | bytes 262144 | tf_op jit(solution)/shard_map/all_to_all | solution.py:415
  348.9 8.6 %shard_map.115.partial = f32[4096,256]{1,0:T(8,128)} custom-call(s32[2]{0:T(128)} %pad_add_fusion.index, bf16[4096,256]{1,0:T(8,128)(2,1)} %get-tuple-element.80.refs_0_.refs_4_, bf16[4096,256]{1,0:T(8,128)(2,1)} %collective-permute-done.31.refs_1_, bf16[4096,256]{1,0:T(8,128)(2,1)} %collective-permute-done.32.refs_2_, ...), custom_call_target="tpu_custom_call" | custom-call | flops 2147483648 | bytes 15204352 | tf_op jit(solution)/shard_map/pallas_call | solution.py:53
  357.6 5.9 %shard_map.116 = bf16[4096,256]{1,0:T(8,128)(2,1)} custom-call(s32[2]{0:T(128)} %pad_add_fusion.index, bf16[4096,256]{1,0:T(8,128)(2,1)} %get-tuple-element.79.back, bf16[16,64,64]{2,1,0:T(8,128)(2,1)} %factor.3, f32[4096,256]{1,0:T(8,128)} %shard_map.115.partial), custom_call_target="tpu_custom_call" | custom-call | flops 134217728 | bytes 8519680 | tf_op jit(solution)/shard_map/pallas_call | solution.py:53
  (205 shorter events, 46.2 us)
Async XLA Ops:
  0.7 48.9 %collective-permute-start.15 = (bf16[4096,256]{1,0:T(8,128)(2,1)}, bf16[4096,256]{1,0:T(8,128)(2,1)S(1)}, u32[]{:S(2)}, u32[]{:S(2)}) collective-permute-start(bf16[4096,256]{1,0:T(8,128)(2,1)} %refs_0_.3), channel_id=1, source_target_pairs={{0,2},{1,3},{2,0},{3,1},{4,6},{5,7},{6,4},{7,5},{8,10},{9,11},{10,... | collective-permute-start | bytes 6291464 | tf_op jit(solution)/shard_map/ppermute | solution.py:21
  3.7 144.2 %collective-permute-start.14 = (bf16[4096,256]{1,0:T(8,128)(2,1)}, bf16[4096,256]{1,0:T(8,128)(2,1)}, u32[]{:S(2)}, u32[]{:S(2)}) collective-permute-start(bf16[4096,256]{1,0:T(8,128)(2,1)} %refs_0_.3), channel_id=1, source_target_pairs={{0,1},{1,0},{2,3},{3,2},{4,5},{5,4},{6,7},{7,6},{8,9},{9,8},{10,11... | collective-permute-start | bytes 6291464 | tf_op jit(solution)/shard_map/ppermute | solution.py:21
  9.3 43.5 %collective-permute-start = (bf16[4,8,16,256]{3,2,1,0:T(8,128)(2,1)}, bf16[4,8,16,256]{3,2,1,0:T(8,128)(2,1)S(1)}, u32[]{:S(2)}, u32[]{:S(2)}) collective-permute-start(bf16[4,8,16,256]{3,2,1,0:T(8,128)(2,1)} %get-tuple-element.46), channel_id=1, source_target_pairs={{0,4},{4,0},{8,12},{12,8},{16,20},{20,16},{24,28},{28,24},{1,5},{5... | collective-permute-start | bytes 786440 | tf_op jit(solution)/shard_map/ppermute | solution.py:21
  10.9 45.1 %collective-permute-start.1 = (bf16[4,8,16,256]{3,2,1,0:T(8,128)(2,1)}, bf16[4,8,16,256]{3,2,1,0:T(8,128)(2,1)S(1)}, u32[]{:S(2)}, u32[]{:S(2)}) collective-permute-start(bf16[4,8,16,256]{3,2,1,0:T(8,128)(2,1)} %get-tuple-element.47), channel_id=1, source_target_pairs={{0,8},{4,12},{8,0},{12,4},{16,24},{20,28},{24,16},{28,20},{1,9},{5... | collective-permute-start | bytes 786440 | tf_op jit(solution)/shard_map/ppermute | solution.py:21
  12.5 44.9 %collective-permute-start.2 = (bf16[4,8,16,256]{3,2,1,0:T(8,128)(2,1)}, bf16[4,8,16,256]{3,2,1,0:T(8,128)(2,1)S(1)}, u32[]{:S(2)}, u32[]{:S(2)}) collective-permute-start(bf16[4,8,16,256]{3,2,1,0:T(8,128)(2,1)} %get-tuple-element.48), channel_id=1, source_target_pairs={{0,12},{4,8},{8,4},{12,0},{16,28},{20,24},{24,20},{28,16},{1,13},{... | collective-permute-start | bytes 786440 | tf_op jit(solution)/shard_map/ppermute | solution.py:21
  49.5 98.4 %collective-permute-start.16 = (bf16[4096,256]{1,0:T(8,128)(2,1)S(1)}, bf16[4096,256]{1,0:T(8,128)(2,1)}, u32[]{:S(2)}, u32[]{:S(2)}) collective-permute-start(bf16[4096,256]{1,0:T(8,128)(2,1)S(1)} %collective-permute-done.15.refs_2_), channel_id=1, source_target_pairs={{0,1},{1,0},{2,3},{3,2},{4,5},{5,4},{6,7},{7,6},{8,9},{9,8},{10,11... | collective-permute-start | bytes 6291464 | tf_op jit(solution)/shard_map/ppermute | solution.py:21
  52.9 27.3 %collective-permute-start.3 = (bf16[4,8,16,256]{3,2,1,0:T(8,128)(2,1)}, bf16[4,8,16,256]{3,2,1,0:T(8,128)(2,1)}, u32[]{:S(2)}, u32[]{:S(2)}) collective-permute-start(bf16[4,8,16,256]{3,2,1,0:T(8,128)(2,1)} %get-tuple-element.49), channel_id=1, source_target_pairs={{0,16},{4,20},{8,24},{12,28},{16,0},{20,4},{24,8},{28,12},{1,17},{... | collective-permute-start | bytes 786440 | tf_op jit(solution)/shard_map/ppermute | solution.py:21
  56.0 36.7 %collective-permute-start.4 = (bf16[4,8,16,256]{3,2,1,0:T(8,128)(2,1)}, bf16[4,8,16,256]{3,2,1,0:T(8,128)(2,1)}, u32[]{:S(2)}, u32[]{:S(2)}) collective-permute-start(bf16[4,8,16,256]{3,2,1,0:T(8,128)(2,1)} %get-tuple-element.50), channel_id=1, source_target_pairs={{0,20},{4,16},{8,28},{12,24},{16,4},{20,0},{24,12},{28,8},{1,21},{... | collective-permute-start | bytes 786440 | tf_op jit(solution)/shard_map/ppermute | solution.py:21
  57.3 35.3 %collective-permute-start.5 = (bf16[4,8,16,256]{3,2,1,0:T(8,128)(2,1)}, bf16[4,8,16,256]{3,2,1,0:T(8,128)(2,1)}, u32[]{:S(2)}, u32[]{:S(2)}) collective-permute-start(bf16[4,8,16,256]{3,2,1,0:T(8,128)(2,1)} %get-tuple-element.51), channel_id=1, source_target_pairs={{0,24},{4,28},{8,16},{12,20},{16,8},{20,12},{24,0},{28,4},{1,25},{... | collective-permute-start | bytes 786440 | tf_op jit(solution)/shard_map/ppermute | solution.py:21
  80.2 12.4 %collective-permute-start.6 = (bf16[4,8,16,256]{3,2,1,0:T(8,128)(2,1)}, bf16[4,8,16,256]{3,2,1,0:T(8,128)(2,1)}, u32[]{:S(2)}, u32[]{:S(2)}) collective-permute-start(bf16[4,8,16,256]{3,2,1,0:T(8,128)(2,1)} %get-tuple-element.52), channel_id=1, source_target_pairs={{0,28},{4,24},{8,20},{12,16},{16,12},{20,8},{24,4},{28,0},{1,29},{... | collective-permute-start | bytes 786440 | tf_op jit(solution)/shard_map/ppermute | solution.py:21
  98.7 36.5 %collective-permute-start.10 = (bf16[4,8,16,256]{3,2,1,0:T(8,128)(2,1)}, bf16[4,8,16,256]{3,2,1,0:T(8,128)(2,1)S(1)}, u32[]{:S(2)}, u32[]{:S(2)}) collective-permute-start(bf16[4,8,16,256]{3,2,1,0:T(8,128)(2,1)} %get-tuple-element.57), channel_id=1, source_target_pairs={{0,16},{4,20},{8,24},{12,28},{16,0},{20,4},{24,8},{28,12},{1,17},{... | collective-permute-start | bytes 786440 | tf_op jit(solution)/shard_map/ppermute | solution.py:21
  112.0 35.1 %collective-permute-start.11 = (bf16[4,8,16,256]{3,2,1,0:T(8,128)(2,1)}, bf16[4,8,16,256]{3,2,1,0:T(8,128)(2,1)S(1)}, u32[]{:S(2)}, u32[]{:S(2)}) collective-permute-start(bf16[4,8,16,256]{3,2,1,0:T(8,128)(2,1)} %get-tuple-element.58), channel_id=1, source_target_pairs={{0,20},{4,16},{8,28},{12,24},{16,4},{20,0},{24,12},{28,8},{1,21},{... | collective-permute-start | bytes 786440 | tf_op jit(solution)/shard_map/ppermute | solution.py:21
  112.0 48.0 %collective-permute-start.12 = (bf16[4,8,16,256]{3,2,1,0:T(8,128)(2,1)}, bf16[4,8,16,256]{3,2,1,0:T(8,128)(2,1)S(1)}, u32[]{:S(2)}, u32[]{:S(2)}) collective-permute-start(bf16[4,8,16,256]{3,2,1,0:T(8,128)(2,1)} %get-tuple-element.59), channel_id=1, source_target_pairs={{0,24},{4,28},{8,16},{12,20},{16,8},{20,12},{24,0},{28,4},{1,25},{... | collective-permute-start | bytes 786440 | tf_op jit(solution)/shard_map/ppermute | solution.py:21
  135.2 24.8 %collective-permute-start.13 = (bf16[4,8,16,256]{3,2,1,0:T(8,128)(2,1)}, bf16[4,8,16,256]{3,2,1,0:T(8,128)(2,1)S(1)}, u32[]{:S(2)}, u32[]{:S(2)}) collective-permute-start(bf16[4,8,16,256]{3,2,1,0:T(8,128)(2,1)} %get-tuple-element.60), channel_id=1, source_target_pairs={{0,28},{4,24},{8,20},{12,16},{16,12},{20,8},{24,4},{28,0},{1,29},{... | collective-permute-start | bytes 786440 | tf_op jit(solution)/shard_map/ppermute | solution.py:21
  147.1 13.0 %collective-permute-start.7 = (bf16[4,8,16,256]{3,2,1,0:T(8,128)(2,1)}, bf16[4,8,16,256]{3,2,1,0:T(8,128)(2,1)S(1)}, u32[]{:S(2)}, u32[]{:S(2)}) collective-permute-start(bf16[4,8,16,256]{3,2,1,0:T(8,128)(2,1)} %get-tuple-element.54), channel_id=1, source_target_pairs={{0,4},{4,0},{8,12},{12,8},{16,20},{20,16},{24,28},{28,24},{1,5},{5... | collective-permute-start | bytes 786440 | tf_op jit(solution)/shard_map/ppermute | solution.py:21
  147.9 12.1 %collective-permute-start.8 = (bf16[4,8,16,256]{3,2,1,0:T(8,128)(2,1)}, bf16[4,8,16,256]{3,2,1,0:T(8,128)(2,1)S(1)}, u32[]{:S(2)}, u32[]{:S(2)}) collective-permute-start(bf16[4,8,16,256]{3,2,1,0:T(8,128)(2,1)} %get-tuple-element.55), channel_id=1, source_target_pairs={{0,8},{4,12},{8,0},{12,4},{16,24},{20,28},{24,16},{28,20},{1,9},{5... | collective-permute-start | bytes 786440 | tf_op jit(solution)/shard_map/ppermute | solution.py:21
  147.9 13.9 %collective-permute-start.9 = (bf16[4,8,16,256]{3,2,1,0:T(8,128)(2,1)}, bf16[4,8,16,256]{3,2,1,0:T(8,128)(2,1)S(1)}, u32[]{:S(2)}, u32[]{:S(2)}) collective-permute-start(bf16[4,8,16,256]{3,2,1,0:T(8,128)(2,1)} %get-tuple-element.56), channel_id=1, source_target_pairs={{0,12},{4,8},{8,4},{12,0},{16,28},{20,24},{24,20},{28,16},{1,13},{... | collective-permute-start | bytes 786440 | tf_op jit(solution)/shard_map/ppermute | solution.py:21
  170.7 68.3 %collective-permute-start.32 = (bf16[4096,256]{1,0:T(8,128)(2,1)}, bf16[4096,256]{1,0:T(8,128)(2,1)}, u32[]{:S(2)}, u32[]{:S(2)}) collective-permute-start(bf16[4096,256]{1,0:T(8,128)(2,1)} %get-tuple-element.80.refs_0_.refs_4_), channel_id=1, source_target_pairs={{0,2},{1,3},{2,0},{3,1},{4,6},{5,7},{6,4},{7,5},{8,10},{9,11},{10,... | collective-permute-start | bytes 6291464 | tf_op jit(solution)/shard_map/ppermute | solution.py:21
  172.4 9.9 %collective-permute-start.17 = (bf16[4,8,16,256]{3,2,1,0:T(8,128)(2,1)}, bf16[4,8,16,256]{3,2,1,0:T(8,128)(2,1)S(1)}, u32[]{:S(2)}, u32[]{:S(2)}) collective-permute-start(bf16[4,8,16,256]{3,2,1,0:T(8,128)(2,1)} %get-tuple-element.64), channel_id=1, source_target_pairs={{0,4},{4,0},{8,12},{12,8},{16,20},{20,16},{24,28},{28,24},{1,5},{5... | collective-permute-start | bytes 786440 | tf_op jit(solution)/shard_map/ppermute | solution.py:21
  173.8 17.0 %collective-permute-start.18 = (bf16[4,8,16,256]{3,2,1,0:T(8,128)(2,1)}, bf16[4,8,16,256]{3,2,1,0:T(8,128)(2,1)S(1)}, u32[]{:S(2)}, u32[]{:S(2)}) collective-permute-start(bf16[4,8,16,256]{3,2,1,0:T(8,128)(2,1)} %get-tuple-element.65), channel_id=1, source_target_pairs={{0,8},{4,12},{8,0},{12,4},{16,24},{20,28},{24,16},{28,20},{1,9},{5... | collective-permute-start | bytes 786440 | tf_op jit(solution)/shard_map/ppermute | solution.py:21
  175.9 19.7 %collective-permute-start.19 = (bf16[4,8,16,256]{3,2,1,0:T(8,128)(2,1)S(1)}, bf16[4,8,16,256]{3,2,1,0:T(8,128)(2,1)S(1)}, u32[]{:S(2)}, u32[]{:S(2)}) collective-permute-start(bf16[4,8,16,256]{3,2,1,0:T(8,128)(2,1)S(1)} %copy-done.36), channel_id=1, source_target_pairs={{0,12},{4,8},{8,4},{12,0},{16,28},{20,24},{24,20},{28,16},{1,13},{... | collective-permute-start | bytes 786440 | tf_op jit(solution)/shard_map/ppermute | solution.py:21
  178.6 33.3 %collective-permute-start.20 = (bf16[4,8,16,256]{3,2,1,0:T(8,128)(2,1)S(1)}, bf16[4,8,16,256]{3,2,1,0:T(8,128)(2,1)S(1)}, u32[]{:S(2)}, u32[]{:S(2)}) collective-permute-start(bf16[4,8,16,256]{3,2,1,0:T(8,128)(2,1)S(1)} %copy-done.35), channel_id=1, source_target_pairs={{0,16},{4,20},{8,24},{12,28},{16,0},{20,4},{24,8},{28,12},{1,17},{... | collective-permute-start | bytes 786440 | tf_op jit(solution)/shard_map/ppermute | solution.py:21
  182.3 34.6 %collective-permute-start.21 = (bf16[4,8,16,256]{3,2,1,0:T(8,128)(2,1)S(1)}, bf16[4,8,16,256]{3,2,1,0:T(8,128)(2,1)S(1)}, u32[]{:S(2)}, u32[]{:S(2)}) collective-permute-start(bf16[4,8,16,256]{3,2,1,0:T(8,128)(2,1)S(1)} %copy-done.34), channel_id=1, source_target_pairs={{0,20},{4,16},{8,28},{12,24},{16,4},{20,0},{24,12},{28,8},{1,21},{... | collective-permute-start | bytes 786440 | tf_op jit(solution)/shard_map/ppermute | solution.py:21
  190.8 26.0 %collective-permute-start.22 = (bf16[4,8,16,256]{3,2,1,0:T(8,128)(2,1)S(1)}, bf16[4,8,16,256]{3,2,1,0:T(8,128)(2,1)S(1)}, u32[]{:S(2)}, u32[]{:S(2)}) collective-permute-start(bf16[4,8,16,256]{3,2,1,0:T(8,128)(2,1)S(1)} %copy-done.33), channel_id=1, source_target_pairs={{0,24},{4,28},{8,16},{12,20},{16,8},{20,12},{24,0},{28,4},{1,25},{... | collective-permute-start | bytes 786440 | tf_op jit(solution)/shard_map/ppermute | solution.py:21
  195.7 21.2 %collective-permute-start.23 = (bf16[4,8,16,256]{3,2,1,0:T(8,128)(2,1)S(1)}, bf16[4,8,16,256]{3,2,1,0:T(8,128)(2,1)S(1)}, u32[]{:S(2)}, u32[]{:S(2)}) collective-permute-start(bf16[4,8,16,256]{3,2,1,0:T(8,128)(2,1)S(1)} %copy-done.32), channel_id=1, source_target_pairs={{0,28},{4,24},{8,20},{12,16},{16,12},{20,8},{24,4},{28,0},{1,29},{... | collective-permute-start | bytes 786440 | tf_op jit(solution)/shard_map/ppermute | solution.py:21
  212.0 47.1 %collective-permute-start.42 = (f32[4,128,256]{2,1,0:T(8,128)S(1)}, f32[4,128,256]{2,1,0:T(8,128)}, u32[]{:S(2)}, u32[]{:S(2)}) collective-permute-start(f32[4,128,256]{2,1,0:T(8,128)S(1)} %dynamic-slice_bitcast_fusion), channel_id=1, source_target_pairs={{0,4},{4,0},{8,12},{12,8},{16,20},{20,16},{24,28},{28,24},{1,5},{5... | collective-permute-start | bytes 1572872 | tf_op jit(solution)/shard_map/ppermute | solution.py:21
  223.3 58.2 %copy-start.3 = (f32[1024,256]{1,0:T(8,128)S(1)}, f32[1024,256]{1,0:T(8,128)}, u32[]{:S(2)}) copy-start(f32[1024,256]{1,0:T(8,128)} %shard_map.118) | copy-start | bytes 3145732
  231.3 4.2 %collective-permute-start.37 = (f32[80,128]{1,0:T(8,128)}, f32[80,128]{1,0:T(8,128)S(1)}, u32[]{:S(2)}, u32[]{:S(2)}) collective-permute-start(f32[80,128]{1,0:T(8,128)} %shard_map.117), channel_id=1, source_target_pairs={{0,2},{1,3},{2,0},{3,1},{4,6},{5,7},{6,4},{7,5},{8,10},{9,11},{10,... | collective-permute-start | bytes 122888 | tf_op jit(solution)/shard_map/ppermute | solution.py:21
  236.3 2.7 collective-permute-start.38
  236.4 111.9 %collective-permute-start.31 = (bf16[4096,256]{1,0:T(8,128)(2,1)S(1)}, bf16[4096,256]{1,0:T(8,128)(2,1)}, u32[]{:S(2)}, u32[]{:S(2)}) collective-permute-start(bf16[4096,256]{1,0:T(8,128)(2,1)S(1)} %copy-done.1), channel_id=1, source_target_pairs={{0,1},{1,0},{2,3},{3,2},{4,5},{5,4},{6,7},{7,6},{8,9},{9,8},{10,11... | collective-permute-start | bytes 6291464 | tf_op jit(solution)/shard_map/ppermute | solution.py:21
  236.9 23.2 %collective-permute-start.24 = (bf16[4,8,16,256]{3,2,1,0:T(8,128)(2,1)S(1)}, bf16[4,8,16,256]{3,2,1,0:T(8,128)(2,1)}, u32[]{:S(2)}, u32[]{:S(2)}) collective-permute-start(bf16[4,8,16,256]{3,2,1,0:T(8,128)(2,1)S(1)} %copy-done.37), channel_id=1, source_target_pairs={{0,4},{4,0},{8,12},{12,8},{16,20},{20,16},{24,28},{28,24},{1,5},{5... | collective-permute-start | bytes 786440 | tf_op jit(solution)/shard_map/ppermute | solution.py:21
  239.0 109.3 %collective-permute-start.33 = (bf16[4096,256]{1,0:T(8,128)(2,1)}, bf16[4096,256]{1,0:T(8,128)(2,1)}, u32[]{:S(2)}, u32[]{:S(2)}) collective-permute-start(bf16[4096,256]{1,0:T(8,128)(2,1)} %collective-permute-done.32.refs_2_), channel_id=1, source_target_pairs={{0,1},{1,0},{2,3},{3,2},{4,5},{5,4},{6,7},{7,6},{8,9},{9,8},{10,11... | collective-permute-start | bytes 6291464 | tf_op jit(solution)/shard_map/ppermute | solution.py:21
  239.0 7.0 %collective-permute-start.39 = (bf16[1,80,128]{2,1,0:T(8,128)(2,1)S(1)}, bf16[1,80,128]{2,1,0:T(8,128)(2,1)S(1)}, u32[]{:S(2)}, u32[]{:S(2)}) collective-permute-start(bf16[1,80,128]{2,1,0:T(8,128)(2,1)S(1)} %fusion.12), channel_id=1, source_target_pairs={{0,4},{4,0},{8,12},{12,8},{16,20},{20,16},{24,28},{28,24},{1,5},{5... | collective-permute-start | bytes 61448 | tf_op jit(solution)/shard_map/ppermute | solution.py:21
  246.0 11.0 %collective-permute-start.40 = (bf16[2,80,128]{2,1,0:T(8,128)(2,1)S(1)}, bf16[2,80,128]{2,1,0:T(8,128)(2,1)S(1)}, u32[]{:S(2)}, u32[]{:S(2)}) collective-permute-start(bf16[2,80,128]{2,1,0:T(8,128)(2,1)S(1)} %maximum_select_fusion.2), channel_id=1, source_target_pairs={{0,8},{4,12},{8,0},{12,4},{16,24},{20,28},{24,16},{28,20},{1,9},{5... | collective-permute-start | bytes 122888 | tf_op jit(solution)/shard_map/ppermute | solution.py:21
  257.0 15.2 %collective-permute-start.25 = (bf16[4,8,16,256]{3,2,1,0:T(8,128)(2,1)}, bf16[4,8,16,256]{3,2,1,0:T(8,128)(2,1)}, u32[]{:S(2)}, u32[]{:S(2)}) collective-permute-start(bf16[4,8,16,256]{3,2,1,0:T(8,128)(2,1)} %get-tuple-element.73), channel_id=1, source_target_pairs={{0,8},{4,12},{8,0},{12,4},{16,24},{20,28},{24,16},{28,20},{1,9},{5... | collective-permute-start | bytes 786440 | tf_op jit(solution)/shard_map/ppermute | solution.py:21
  259.1 20.1 %collective-permute-start.26 = (bf16[4,8,16,256]{3,2,1,0:T(8,128)(2,1)}, bf16[4,8,16,256]{3,2,1,0:T(8,128)(2,1)}, u32[]{:S(2)}, u32[]{:S(2)}) collective-permute-start(bf16[4,8,16,256]{3,2,1,0:T(8,128)(2,1)} %get-tuple-element.74), channel_id=1, source_target_pairs={{0,12},{4,8},{8,4},{12,0},{16,28},{20,24},{24,20},{28,16},{1,13},{... | collective-permute-start | bytes 786440 | tf_op jit(solution)/shard_map/ppermute | solution.py:21
  260.1 21.4 %collective-permute-start.27 = (bf16[4,8,16,256]{3,2,1,0:T(8,128)(2,1)}, bf16[4,8,16,256]{3,2,1,0:T(8,128)(2,1)}, u32[]{:S(2)}, u32[]{:S(2)}) collective-permute-start(bf16[4,8,16,256]{3,2,1,0:T(8,128)(2,1)} %get-tuple-element.75), channel_id=1, source_target_pairs={{0,16},{4,20},{8,24},{12,28},{16,0},{20,4},{24,8},{28,12},{1,17},{... | collective-permute-start | bytes 786440 | tf_op jit(solution)/shard_map/ppermute | solution.py:21
  272.2 28.4 %collective-permute-start.28 = (bf16[4,8,16,256]{3,2,1,0:T(8,128)(2,1)}, bf16[4,8,16,256]{3,2,1,0:T(8,128)(2,1)S(1)}, u32[]{:S(2)}, u32[]{:S(2)}) collective-permute-start(bf16[4,8,16,256]{3,2,1,0:T(8,128)(2,1)} %get-tuple-element.76), channel_id=1, source_target_pairs={{0,20},{4,16},{8,28},{12,24},{16,4},{20,0},{24,12},{28,8},{1,21},{... | collective-permute-start | bytes 786440 | tf_op jit(solution)/shard_map/ppermute | solution.py:21
  279.1 21.6 %collective-permute-start.29 = (bf16[4,8,16,256]{3,2,1,0:T(8,128)(2,1)}, bf16[4,8,16,256]{3,2,1,0:T(8,128)(2,1)S(1)}, u32[]{:S(2)}, u32[]{:S(2)}) collective-permute-start(bf16[4,8,16,256]{3,2,1,0:T(8,128)(2,1)} %get-tuple-element.77), channel_id=1, source_target_pairs={{0,24},{4,28},{8,16},{12,20},{16,8},{20,12},{24,0},{28,4},{1,25},{... | collective-permute-start | bytes 786440 | tf_op jit(solution)/shard_map/ppermute | solution.py:21
  281.5 24.9 %collective-permute-start.30 = (bf16[4,8,16,256]{3,2,1,0:T(8,128)(2,1)}, bf16[4,8,16,256]{3,2,1,0:T(8,128)(2,1)S(1)}, u32[]{:S(2)}, u32[]{:S(2)}) collective-permute-start(bf16[4,8,16,256]{3,2,1,0:T(8,128)(2,1)} %get-tuple-element.78), channel_id=1, source_target_pairs={{0,28},{4,24},{8,20},{12,16},{16,12},{20,8},{24,4},{28,0},{1,29},{... | collective-permute-start | bytes 786440 | tf_op jit(solution)/shard_map/ppermute | solution.py:21
  300.7 24.4 %collective-permute-start.43 = (f32[2,128,256]{2,1,0:T(8,128)}, f32[2,128,256]{2,1,0:T(8,128)}, u32[]{:S(2)}, u32[]{:S(2)}) collective-permute-start(f32[2,128,256]{2,1,0:T(8,128)} %dynamic-slice_bitcast_fusion.1), channel_id=1, source_target_pairs={{0,8},{4,12},{8,0},{12,4},{16,24},{20,28},{24,16},{28,20},{1,9},{5... | collective-permute-start | bytes 786440 | tf_op jit(solution)/shard_map/ppermute | solution.py:21
  300.7 21.7 %collective-permute-start.41 = (bf16[4,80,128]{2,1,0:T(8,128)(2,1)S(1)}, bf16[4,80,128]{2,1,0:T(8,128)(2,1)}, u32[]{:S(2)}, u32[]{:S(2)}) collective-permute-start(bf16[4,80,128]{2,1,0:T(8,128)(2,1)S(1)} %maximum_select_fusion.1), channel_id=1, source_target_pairs={{0,16},{4,20},{8,24},{12,28},{16,0},{20,4},{24,8},{28,12},{1,17},{... | collective-permute-start | bytes 245768 | tf_op jit(solution)/shard_map/ppermute | solution.py:21
  313.0 19.2 %all-to-all-start = ((f32[32,16,128]{2,1,0:T(8,128)}), f32[32,16,128]{2,1,0:T(8,128)}, u32[]{:S(2)}, u32[]{:S(2)}) async-start(f32[32,16,128]{2,1,0:T(8,128)} %bitcast.69), calls=%async_computation | async-start | bytes 524288 | tf_op jit(solution)/shard_map/all_to_all | solution.py:413
  322.3 25.4 %collective-permute-start.34 = (bf16[256,256]{1,0:T(8,128)(2,1)}, bf16[256,256]{1,0:T(8,128)(2,1)S(1)}, u32[]{:S(2)}, u32[]{:S(2)}) collective-permute-start(bf16[256,256]{1,0:T(8,128)(2,1)} %get-tuple-element.97), channel_id=1, source_target_pairs={{0,1},{1,0},{2,3},{3,2},{4,5},{5,4},{6,7},{7,6},{8,9},{9,8},{10,11... | collective-permute-start | bytes 393224 | tf_op jit(solution)/shard_map/ppermute | solution.py:21
  322.5 25.2 %collective-permute-start.35 = (bf16[256,256]{1,0:T(8,128)(2,1)}, bf16[256,256]{1,0:T(8,128)(2,1)}, u32[]{:S(2)}, u32[]{:S(2)}) collective-permute-start(bf16[256,256]{1,0:T(8,128)(2,1)} %get-tuple-element.99), channel_id=1, source_target_pairs={{0,2},{1,3},{2,0},{3,1},{4,6},{5,7},{6,4},{7,5},{8,10},{9,11},{10,... | collective-permute-start | bytes 393224 | tf_op jit(solution)/shard_map/ppermute | solution.py:21
  326.8 15.7 %collective-permute-start.44 = (f32[1,128,256]{2,1,0:T(8,128)}, f32[1,128,256]{2,1,0:T(8,128)}, u32[]{:S(2)}, u32[]{:S(2)}) collective-permute-start(f32[1,128,256]{2,1,0:T(8,128)} %constant_dynamic-slice_fusion), channel_id=1, source_target_pairs={{0,16},{4,20},{8,24},{12,28},{16,0},{20,4},{24,8},{28,12},{1,17},{... | collective-permute-start | bytes 393224 | tf_op jit(solution)/shard_map/ppermute | solution.py:21
  333.9 12.8 %all-to-all-start.1 = ((bf16[32,16,128]{2,1,0:T(8,128)(2,1)}), bf16[32,16,128]{2,1,0:T(8,128)(2,1)S(1)}, u32[]{:S(2)}, u32[]{:S(2)}) async-start(bf16[32,16,128]{2,1,0:T(8,128)(2,1)} %broadcast_in_dim.35), calls=%async_computation.1 | async-start | bytes 262144 | tf_op jit(solution)/shard_map/all_to_all | solution.py:415
  342.5 5.7 %collective-permute-start.36 = (bf16[256,256]{1,0:T(8,128)(2,1)}, bf16[256,256]{1,0:T(8,128)(2,1)S(1)}, u32[]{:S(2)}, u32[]{:S(2)}) collective-permute-start(bf16[256,256]{1,0:T(8,128)(2,1)} %get-tuple-element.96), channel_id=1, source_target_pairs={{0,3},{1,2},{2,1},{3,0},{4,7},{5,6},{6,5},{7,4},{8,11},{9,10},{10,... | collective-permute-start | bytes 393224 | tf_op jit(solution)/shard_map/ppermute | solution.py:21
  (49 other events, 735.5 us)
where the time goes:
time: 365 us; the launch traced here: 363 us
  waiting for transfers between devices  163 us (45%)
  starting transfers between devices  101 us (28%)
  Pallas kernels  70.1 us (19%)
  local copies, waits for them, and re-layouts  13.7 us (4%)
  other arithmetic  9.07 us (2%)
  matrix products  5.23 us (1%)
    ppermute x45, waiting for transfers between devices, swap(): return lax.ppermute(values, axis, [(i, i ^ step) for i in range(count)])  159 us
    ppermute x45, starting transfers between devices, swap(): return lax.ppermute(values, axis, [(i, i ^ step) for i in range(count)])  88.2 us
    pallas_call x10, Pallas kernels, call(): pl.pallas_call(kernel, grid_spec=pltpu.PrefetchScalarGridSpec(num_scalar_...  70.1 us
    all_to_all x1, starting transfers between devices, resident(): lax.all_to_all(parts, ('seq', 'ch'), split_axis=0, concat_axis=0, tiled=T...  8.38 us
  transfers between devices with their start and end apart: 47, of which 19 were waited for; matrix products, arithmetic and copies ran while one was open for 7% of the time, Pallas kernels for 13%

commit v1 on v0

--- a/solution.py
+++ b/solution.py
@@ -13,24 +13,14 @@
 PER = 8
 F32 = jnp.float32
 BF16 = jnp.bfloat16
+HALVES = 2
+BACK_HALVES = 1
 VMEM_BYTES = 56 * 1024 * 1024
 
 
 def swap(values, axis, step):
     count = lax.axis_size(axis)
     return lax.ppermute(values, axis, [(i, i ^ step) for i in range(count)])
-
-
-def flip_blocks(values, dim, index):
-    count = values.shape[dim]
-    bit = 1
-    while bit < count:
-        shape = values.shape[:dim] + (count // (2 * bit), 2, bit) + values.shape[dim + 1 :]
-        split = values.reshape(shape)
-        turned = jnp.flip(split, dim + 1)
-        values = jnp.where((index // bit) % 2 == 1, turned, split).reshape(values.shape)
-        bit *= 2
-    return values
 
 
 def exchange(pieces):
@@ -81,18 +71,18 @@
     return pl.BlockSpec(dims, lambda i, *_: (i,) + (0,) * (len(dims) - 1))
 
 
-def scatter_rows(source, pieces, me, pair):
+def scatter_rows(source, pieces, me, pair, columns=slice(None)):
     for j, piece in enumerate(pieces):
-        low = source[0, rows_of(me ^ j, PER), :]
-        high = source[1, rows_of(me ^ j, PER), :]
+        low = source[0, rows_of(me ^ j, PER), columns]
+        high = source[1, rows_of(me ^ j, PER), columns]
         piece[0, pair] = jnp.concatenate([low, high], 0).astype(BF16)
 
 
-def gather_rows(target, pieces, me, pair):
+def gather_rows(target, pieces, me, pair, columns=slice(None)):
     for j, piece in enumerate(pieces):
         both = piece[0, pair].astype(F32)
-        target[0, rows_of(me ^ j, PER), :] = both[:PER]
-        target[1, rows_of(me ^ j, PER), :] = both[PER:]
+        target[0, rows_of(me ^ j, PER), columns] = both[:PER]
+        target[1, rows_of(me ^ j, PER), columns] = both[PER:]
 
 
 def first_kernel(index, tokens, factor, *rest):
@@ -133,14 +123,22 @@
         gate_out[rows, :] = gate
         grad = upstream[rows, :].astype(F32) * (gate * jax.nn.sigmoid(gate))
         held[pair % 2] = grad.reshape(2, C, width)
-        scatter_rows(held.at[pair % 2], pieces, index[0], pair)
+        count = len(pieces) // BACK_HALVES
+        for h in range(BACK_HALVES):
+            columns = slice(h * width // BACK_HALVES, (h + 1) * width // BACK_HALVES)
+            some = pieces[h * count : (h + 1) * count]
+            scatter_rows(held.at[pair % 2], some, index[0], pair, columns)
 
 
 def output_kernel(n, index, *refs):
-    pieces, (gate_in, tokens, upstream, output, pre_grad, held) = refs[:n], refs[n:]
+    pieces, (gate_in, tokens, upstream, output, pre_grad, held) = refs[:-6], refs[-6:]
     for pair in range(B // 2):
         rows = slice(pair * 2 * C, (pair + 1) * 2 * C)
-        gather_rows(held.at[pair % 2], pieces, index[0], pair)
+        for h in range(len(pieces) // n):
+            some = pieces[h * n : (h + 1) * n]
+            step = some[0].shape[-1]
+            columns = slice(h * step, (h + 1) * step)
+            gather_rows(held.at[pair % 2], some, index[0], pair, columns)
         mixed = held[pair % 2].reshape(2 * C, -1)
         gate = gate_in[rows, :]
         sig = jax.nn.sigmoid(gate)
@@ -171,18 +169,32 @@
 
 
 def far_grad_kernel(n, own_a, index, *refs):
-    grads, first = refs[:n], refs[n : 2 * n]
-    second_val, back_second, sums, third_acc, second_acc = refs[2 * n :]
+    cuts = [BACK_HALVES * n, HALVES * n, HALVES, BACK_HALVES]
+    ends = [sum(cuts[: k + 1]) for k in range(4)]
+    grads, first = refs[: ends[0]], refs[ends[0] : ends[1]]
+    second_vals, back_vals = refs[ends[1] : ends[2]], refs[ends[2] : ends[3]]
+    sums, third_acc, second_acc = refs[ends[3] :]
     big = 2 * A * PER
     small = B * PER
+
+    def wide(blocks):
+        return blocks[0] if len(blocks) == 1 else jnp.concatenate(blocks, 1)
+
     for pair in range(B // 2):
-        block = jnp.concatenate([g[:, pair].reshape(own_a * 2 * PER, -1) for g in grads], 0)
-        part = dot(block, second_val[:, pair].reshape(big, -1), ((1,), (1,)))
+        sides = []
+        for h in range(BACK_HALVES):
+            some = grads[h * n : (h + 1) * n]
+            sides.append(
+                jnp.concatenate([g[:, pair].reshape(own_a * 2 * PER, -1) for g in some], 0)
+            )
+        other = wide([v[:, pair].reshape(big, -1) for v in second_vals])
+        part = dot(wide(sides), other, ((1,), (1,)))
         third_acc[...] = part if pair == 0 else third_acc[...] + part
     for j in range(n):
         for i in range(own_a):
-            block = back_second[j * own_a + i].reshape(small, -1)
-            part = dot(block, first[j][i].reshape(small, -1), ((1,), (1,)))
+            block = wide([v[j * own_a + i].reshape(small, -1) for v in back_vals])
+            other = wide([first[h * n + j][i].reshape(small, -1) for h in range(HALVES)])
+            part = dot(block, other, ((1,), (1,)))
             second_acc[...] = part if j + i == 0 else second_acc[...] + part
     tall = own_a * 2 * PER
     row = lax.broadcasted_iota(jnp.int32, (tall, big), 0)
@@ -234,11 +246,11 @@
 
 
 def first_grad_kernel(n, index, *refs):
-    pieces, (tokens, back, out, held) = refs[:n], refs[n:]
+    pieces, (tokens, back, out, held, total) = refs[:n], refs[n:]
 
     @pl.when(pl.program_id(0) == 0)
     def _():
-        out[...] = jnp.zeros_like(out)
+        total[...] = jnp.zeros_like(total)
 
     for pair in range(B // 2):
         gather_rows(held.at[pair % 2], pieces, index[0], pair)
@@ -249,31 +261,56 @@
             back[rows, :] = value
             sides.append(dot(value, tokens[rows, :], ((1,), (1,))))
         both = jnp.concatenate(sides, 1).reshape(C // PER, PER, 2 * C)
-        out[:, pair] += both
-
-
-def input_grad_kernel(index, back, factor, partial, out):
+        total[:, pair] += both
+
+    @pl.when(pl.program_id(0) == pl.num_programs(0) - 1)
+    def _():
+        out[...] = total[...].reshape(out.shape).astype(out.dtype)
+
+
+def input_grad_kernel(index, *refs):
+    back, (factor, partial, out) = refs[:-3], refs[-3:]
     for b in range(B):
         rows = slice(b * C, (b + 1) * C)
-        mixed = dot(factor[b], back[rows, :], ((0,), (0,)))
+        value = [x[rows, :] for x in back]
+        value = value[0] if len(value) == 1 else jnp.concatenate(value, 1)
+        mixed = dot(factor[b], value, ((0,), (0,)))
         out[rows, :] = (partial[rows, :] + mixed).astype(BF16)
 
 
-def spread_diagonal(values, copies):
-    rows, c, cols = values.shape
-    tall = jnp.broadcast_to(values[:, None], (rows, copies, c, cols))
-    tall = tall.reshape(rows * copies * c, cols)
-    wide = cols * copies * c
-    expand = (
-        lax.broadcasted_iota(jnp.int32, (cols, wide), 1) // (copies * c)
-        == lax.broadcasted_iota(jnp.int32, (cols, wide), 0)
+def one_hot(dims, test):
+    return test(
+        lax.broadcasted_iota(jnp.int32, dims, 0), lax.broadcasted_iota(jnp.int32, dims, 1)
     ).astype(BF16)
-    dims = (tall.shape[0], wide)
-    keep = (
-        lax.broadcasted_iota(jnp.int32, dims, 0) % (copies * c)
-        == lax.broadcasted_iota(jnp.int32, dims, 1) % (copies * c)
-    )
-    return jnp.where(keep, dot(tall, expand), 0.0).astype(BF16)
+
+
+def spread_kernel(own_a, back, index, third, second, third_big, second_big):
+    me = index[0]
+
+    def place(slot):
+        return ((slot // own_a) ^ me) * own_a + slot % own_a
+
+    def fill(values, copies, count, big, where):
+        fast = copies * PER
+        size = count * fast
+        rows = one_hot(
+            (size, PER * count), lambda r, k: k == (r % PER) * count + where(r // fast)
+        )
+        columns = one_hot((size, count), lambda r, k: k == where(r // fast))
+        if back:
+            picked = dot(columns, values, ((1,), (1,))).astype(BF16)
+            wide = dot(picked, rows, ((1,), (1,)))
+        else:
+            picked = dot(rows, values).astype(BF16)
+            wide = dot(picked, columns, ((1,), (1,)))
+        row = lax.broadcasted_iota(jnp.int32, (size, size), 0)
+        col = lax.broadcasted_iota(jnp.int32, (size, size), 1)
+        big[...] = jnp.where(row % fast == col % fast, wide, 0.0).astype(BF16)
+
+    own = third[pl.ds(pl.multiple_of(me * PER, PER), PER)].reshape(PER * A, A)
+    fill(own, 2, A, third_big, place)
+    own = second[pl.ds(pl.multiple_of(me * PER, PER), PER)].reshape(PER * B, B)
+    fill(own, 1, B, second_big, lambda slot: slot)
 
 
 def resident(tokens, cotangent, first_factor, second_factor, third_factor, gate_weight):
@@ -284,71 +321,94 @@
     rows, width = tokens.shape
     own_a = rows // (B * C)
     index = jnp.stack([s, q]).astype(jnp.int32)
-    piece = shape((own_a, B // 2, 2 * PER, width), BF16)
-    piece_rows = [by_row(piece, own_a)] * n
     row_blocks = by_row(tokens, own_a)
     pair_rows = pltpu.VMEM((2, 2, C, width), F32)
 
     far_tokens = swap(tokens, "ch", 2)
-    sent = call(
-        first_kernel, (own_a,), index, (tokens, first_factor),
-        [row_blocks, whole(first_factor)], [piece] * n, piece_rows, [pair_rows],
-        2 * rows * width * C,
-    )
-    first_far = exchange(sent)
+    half_width = width // HALVES
+    half = shape((own_a, B // 2, 2 * PER, half_width), BF16)
+    half_rows = [by_row(half, own_a)] * n
+    part_width = width // BACK_HALVES
+    part = shape((own_a, B // 2, 2 * PER, part_width), BF16)
+    part_rows = [by_row(part, own_a)] * n
+    far_part = shape((A, B // 2, 2 * PER, part_width), BF16)
+    first_far = []
+    for h in range(HALVES):
+        columns = pl.BlockSpec((B * C, half_width), lambda i, *_, h=h: (i, h))
+        sent = call(
+            first_kernel, (own_a,), index, (tokens, first_factor),
+            [columns, whole(first_factor)], [half] * n, half_rows,
+            [pltpu.VMEM((2, 2, C, half_width), F32)],
+            2 * rows * half_width * C,
+        )
+        first_far.append(exchange(sent))
     gathered = [tokens, swap(tokens, "ch", 1), far_tokens, swap(far_tokens, "ch", 1)]
     weight_rows = [
         lax.dynamic_slice_in_dim(gate_weight, (q ^ j) * width, width, 0) for j in range(m)
     ]
     back_weight = [weight_rows[0]] + [swap(weight_rows[j], "ch", j) for j in range(1, m)]
 
-    second_own = lax.dynamic_slice_in_dim(second_factor, s * PER, PER, 0)
-    third_own = lax.dynamic_slice_in_dim(third_factor, s * PER, PER, 0)
-    third_own = third_own.reshape(PER, n, own_a, n, own_a)
-    third_own = flip_blocks(flip_blocks(third_own, 1, s), 3, s).reshape(PER, A, A)
-    second_big = spread_diagonal(second_own.transpose(1, 0, 2), 1)
-    third_big = spread_diagonal(third_own.transpose(1, 0, 2), 2)
-    second_back = spread_diagonal(second_own.transpose(2, 0, 1), 1)
-    third_back = spread_diagonal(third_own.transpose(2, 0, 1), 2)
-
-    far = shape((A, B // 2, 2 * PER, width), BF16)
-    ins = (*first_far, second_big, third_big)
-    outs = [far] + [piece] * n
-    second_far, *sent = call(
-        functools.partial(far_kernel, n, own_a), (1,), index, ins,
-        [whole(x) for x in ins], outs, [whole(x) for x in outs],
-        (), 2 * rows * width * 6 * C,
-    )
-    mixed_home = exchange(sent)
+    spread = []
+    for back in (False, True):
+        ins = (third_factor, second_factor)
+        outs = [shape((2 * A * PER,) * 2, BF16), shape((B * PER,) * 2, BF16)]
+        spread += call(
+            functools.partial(spread_kernel, own_a, back), (1,), index, ins,
+            [whole(x) for x in ins], outs, [whole(x) for x in outs], (),
+            0,
+        )
+    third_big, second_big, third_back, second_back = spread
+
+    far_half = shape((A, B // 2, 2 * PER, half_width), BF16)
+    second_far, mixed_home = [], []
+    for h in range(HALVES):
+        ins = (*first_far[h], second_big, third_big)
+        outs = [far_half] + [half] * n
+        second_val, *sent = call(
+            functools.partial(far_kernel, n, own_a), (1,), index, ins,
+            [whole(x) for x in ins], outs, [whole(x) for x in outs],
+            (), 2 * rows * half_width * 6 * C,
+        )
+        second_far.append(second_val)
+        mixed_home += exchange(sent)
 
     gate_shape = shape((rows, width), F32)
     ins = (*gathered, gate_weight, cotangent)
     gate_pre, *sent = call(
         functools.partial(gate_kernel, m), (own_a,), index, ins,
         [row_blocks] * m + [whole(gate_weight), row_blocks],
-        [gate_shape] + [piece] * n, [row_blocks] + piece_rows, [pair_rows],
+        [gate_shape] + [part] * (n * BACK_HALVES),
+        [row_blocks] + part_rows * BACK_HALVES, [pair_rows],
         2 * rows * width * m * width,
     )
-    grad_far = exchange(sent)
+    grad_far = [exchange(sent[h * n : (h + 1) * n]) for h in range(BACK_HALVES)]
 
     ins = (*mixed_home, gate_pre, tokens, cotangent)
     output, pre_grad = call(
         functools.partial(output_kernel, n), (own_a,), index, ins,
-        piece_rows + [row_blocks] * 3, [shape((rows, width), BF16)] * 2, [row_blocks] * 2,
+        half_rows * HALVES + [row_blocks] * 3,
+        [shape((rows, width), BF16)] * 2, [row_blocks] * 2,
         [pair_rows], rows * width * 16,
     )
     far_pre = swap(pre_grad, "ch", 2)
     all_pre = [pre_grad, swap(pre_grad, "ch", 1), far_pre, swap(far_pre, "ch", 1)]
 
-    ins = (*grad_far, second_back, third_back)
-    outs = [far] + [piece] * n
-    back_second, *sent = call(
-        functools.partial(back_kernel, n, own_a), (1,), index, ins,
-        [whole(x) for x in ins], outs, [whole(x) for x in outs], (),
-        2 * rows * width * 6 * C,
-    )
-    back_home = exchange(sent)
-    ins = (*grad_far, *first_far, second_far, back_second)
+    back_home, back_far = [], []
+    for h in range(BACK_HALVES):
+        ins = (*grad_far[h], second_back, third_back)
+        outs = [far_part] + [part] * n
+        back_second, *sent = call(
+            functools.partial(back_kernel, n, own_a), (1,), index, ins,
+            [whole(x) for x in ins], outs, [whole(x) for x in outs], (),
+            2 * rows * part_width * 6 * C,
+        )
+        back_far.append(back_second)
+        back_home.append(exchange(sent))
+
+    def flat(halves):
+        return [x for half_pieces in halves for x in half_pieces]
+
+    ins = (*flat(grad_far), *flat(first_far), *second_far, *back_far)
     outs = [shape((n * PER + 2 * PER, 128), F32)]
     sums = call(
         functools.partial(far_grad_kernel, n, own_a), (1,), index, ins,
@@ -387,31 +447,24 @@
     while bit:
         sums = sums + swap(sums, "ch", bit)
         bit //= 2
-    every = sums.astype(BF16)[None]
-    bit = 1
-    while bit < n:
-        other = swap(every, "seq", bit)
-        every = jnp.where(
-            (s // bit) % 2 == 1,
-            jnp.concatenate([other, every], 0),
-            jnp.concatenate([every, other], 0),
-        )
-        bit *= 2
+    every = jnp.broadcast_to(sums.astype(BF16)[None], (n, *sums.shape))
+    every = lax.all_to_all(every, "seq", split_axis=0, concat_axis=0, tiled=True)
     third_all = every[:, : n * PER].reshape(n, n, PER, 128).transpose(0, 2, 1, 3)
     third_grad = third_all.reshape(C, A, A)
     second_all = every[:, n * PER :].reshape(n, 2, PER, B // 2, B)
     second_grad = second_all.transpose(0, 2, 3, 1, 4).reshape(C, B, B)
 
-    ins = (*back_home, tokens)
-    first_out = shape((n, B // 2, PER, 2 * C), F32)
-    back_rows, first_part = call(
+    first_out = shape((n * m, B * C // (2 * n * m), 2 * C), BF16)
+    ins = (*back_home[0], tokens)
+    back_rows, parts = call(
         functools.partial(first_grad_kernel, n), (own_a,), index, ins,
-        piece_rows + [row_blocks], [shape((rows, width), BF16), first_out],
-        [row_blocks, whole(first_out)], [pair_rows], 2 * rows * width * C,
-    )
-    parts = first_part.reshape(n * m, -1, 128)
+        part_rows + [row_blocks], [shape((rows, width), BF16), first_out],
+        [row_blocks, whole(first_out)],
+        [pair_rows, pltpu.VMEM((n, B // 2, PER, 2 * C), F32)],
+        2 * rows * width * C,
+    )
     parts = lax.all_to_all(parts, ("seq", "ch"), split_axis=0, concat_axis=0, tiled=True)
-    first_sum = parts.sum(0).astype(BF16)
+    first_sum = parts.astype(F32).sum(0).astype(BF16)
     first_sum = lax.all_to_all(
         jnp.broadcast_to(first_sum[None], (n * m, *first_sum.shape)),
         ("seq", "ch"), split_axis=0, concat_axis=0, tiled=True,

time: 365 us -> 364 us (level)
  waiting for transfers between devices: 163 us -> 132 us
  starting transfers between devices: 101 us -> 126 us
  Pallas kernels: 70.1 us -> 83.3 us
  matrix products: 5.23 us -> 0 us
  other arithmetic: 9.07 us -> 4.28 us
    ppermute x45 -> x56, waiting for transfers between devices: 159 us -> 117 us  [swap(): return lax.ppermute(values, axis, [(i, i ^ step) for i in range(count)])]
    ppermute x45 -> x56, starting transfers between devices: 88.2 us -> 115 us  [swap(): return lax.ppermute(values, axis, [(i, i ^ step) for i in range(count)])]
    pallas_call x10 -> x14, Pallas kernels: 70.1 us -> 83.3 us  [call(): pl.pallas_call(kernel, grid_spec=pltpu.PrefetchScalarGridSpec(num_scalar_...]
    all_to_all x0 -> x1, waiting for transfers between devices: none -> 5.88 us  [resident(): lax.all_to_all(every, 'seq', split_axis=0, concat_axis=0, tiled=True)]
    dot_general x4 -> x0, matrix products: 5.23 us -> none  [dot(): lax.dot_general(left, right, (dims, ((), ())), preferred_element_type=F32)]
    unnamed x102 -> x104, local copies, waits for them, and re-layouts: 5.15 us -> 9.24 us
    all_to_all x1, starting transfers between devices: 8.38 us -> 4.67 us  [resident(): lax.all_to_all(parts, ('seq', 'ch'), split_axis=0, concat_axis=0, tiled=T...]
  transfers between devices with their start and end apart: 47 -> 59, of which waited for: 19 -> 21; matrix products, arithmetic and copies ran while one was open for 7% -> 5% of each run, Pallas kernels for 13% -> 17%
where the time goes in v1:
time: 364 us; the launch traced here: 362 us
  waiting for transfers between devices  132 us (36%)
  starting transfers between devices  126 us (35%)
  Pallas kernels  83.3 us (23%)
  local copies, waits for them, and re-layouts  15.4 us (4%)
  other arithmetic  4.28 us (1%)
    ppermute x56, waiting for transfers between devices, swap(): return lax.ppermute(values, axis, [(i, i ^ step) for i in range(count)])  117 us
    ppermute x56, starting transfers between devices, swap(): return lax.ppermute(values, axis, [(i, i ^ step) for i in range(count)])  115 us
    pallas_call x14, Pallas kernels, call(): pl.pallas_call(kernel, grid_spec=pltpu.PrefetchScalarGridSpec(num_scalar_...  83.3 us
    unnamed x104, local copies, waits for them, and re-layouts  9.24 us
  transfers between devices with their start and end apart: 59, of which 21 were waited for; matrix products, arithmetic and copies ran while one was open for 5% of the time, Pallas kernels for 17%

profile of v1, /device:TPU:0, one launch (start us, length us, event | category | flops | bytes accessed | tf_op | source)
XLA Modules:
  0.0 362.2 jit_solution(5985652408578297871)
XLA Ops:
  0.6 3.0 collective-permute-start.29
  3.7 45.8 %collective-permute-done.29.refs_2_ = bf16[4096,256]{1,0:T(8,128)(2,1)S(1)} collective-permute-done((bf16[4096,256]{1,0:T(8,128)(2,1)}, bf16[4096,256]{1,0:T(8,128)(2,1)S(1)}, u32[]{:S(2)}, u32[]{:S(2)}) %collective-permute-start.29) | collective-permute-done | bytes 2097184 | tf_op jit(solution)/shard_map/ppermute | solution.py:23
  50.2 4.6 %shard_map.112 = (bf16[4,8,16,128]{3,2,1,0:T(8,128)(2,1)}, bf16[4,8,16,128]{3,2,1,0:T(8,128)(2,1)}, bf16[4,8,16,128]{3,2,1,0:T(8,128)(2,1)}, bf16[4,8,16,128]{3,...) custom-call(s32[2]{0:T(128)} %pad_add_fusion.index, ...), custom_call_target="tpu_custom_call" | custom-call | flops 67108864 | bytes 3276800 | tf_op jit(solution)/shard_map/pallas_call | solution.py:43
  58.3 2.6 collective-permute-done.14.refs_1_.refs_17_
  60.9 2.8 collective-permute-start.17
  65.5 4.6 %shard_map.109 = (bf16[4,8,16,128]{3,2,1,0:T(8,128)(2,1)}, bf16[4,8,16,128]{3,2,1,0:T(8,128)(2,1)}, bf16[4,8,16,128]{3,2,1,0:T(8,128)(2,1)}, bf16[4,8,16,128]{3,...) custom-call(s32[2]{0:T(128)} %pad_add_fusion.index, ...), custom_call_target="tpu_custom_call" | custom-call | flops 67108864 | bytes 3276800 | tf_op jit(solution)/shard_map/pallas_call | solution.py:43
  70.1 3.2 collective-permute-start.19
  73.3 6.9 %collective-permute-start.20 = (bf16[4,8,16,128]{3,2,1,0:T(8,128)(2,1)S(1)}, bf16[4,8,16,128]{3,2,1,0:T(8,128)(2,1)S(1)}, u32[]{:S(2)}, u32[]{:S(2)}) collective-permute-start(bf16[4,8,16,128]{3,2,1,0:T(8,128)(2,1)S(1)} %copy-done.48), channel_id=1, source_target_pairs={{0,28},{4,24},{8,20},{12,16},{16,12},{20,8},{24,4},{28,0},{1,29},{... | collective-permute-start | bytes 393224 | tf_op jit(solution)/shard_map/ppermute | solution.py:23
  81.9 3.6 collective-permute-start.1
  85.5 3.0 collective-permute-start.2
  90.5 2.7 collective-permute-start.4
  96.1 8.3 %collective-permute-done.3.refs_4_.refs_12_ = bf16[4,8,16,128]{3,2,1,0:T(8,128)(2,1)S(1)} collective-permute-done((bf16[4,8,16,128]{3,2,1,0:T(8,128)(2,1)}, bf16[4,8,16,128]{3,2,1,0:T(8,128)(2,1)S(1)}, u32[]{:S(2)}, u32[]{:S(2)}) %collective-permute-start.3) | collective-permute-done | bytes 131104 | tf_op jit(solution)/shard_map/ppermute | solution.py:23
  104.4 3.1 collective-permute-start.6
  111.7 3.0 shard_map.110
  114.8 4.5 %shard_map.113 = (bf16[32,8,16,128]{3,2,1,0:T(8,128)(2,1)}, bf16[4,8,16,128]{3,2,1,0:T(8,128)(2,1)}, bf16[4,8,16,128]{3,2,1,0:T(8,128)(2,1)}, bf16[4,8,16,128]{3...) custom-call(s32[2]{0:T(128)} %pad_add_fusion.index, ...), custom_call_target="tpu_custom_call" | custom-call | flops 402653184 | bytes 3702784 | tf_op jit(solution)/shard_map/pallas_call | solution.py:43
  122.9 3.1 collective-permute-done.21.refs_9_
  126.0 2.9 collective-permute-start.25
  130.5 4.5 %shard_map.111 = (bf16[32,8,16,128]{3,2,1,0:T(8,128)(2,1)}, bf16[4,8,16,128]{3,2,1,0:T(8,128)(2,1)}, bf16[4,8,16,128]{3,2,1,0:T(8,128)(2,1)}, bf16[4,8,16,128]{3...) custom-call(s32[2]{0:T(128)} %pad_add_fusion.index, ...), custom_call_target="tpu_custom_call" | custom-call | flops 402653184 | bytes 3702784 | tf_op jit(solution)/shard_map/pallas_call | solution.py:43
  135.1 5.2 %collective-permute-done.24.refs_12_ = bf16[4,8,16,128]{3,2,1,0:T(8,128)(2,1)S(1)} collective-permute-done((bf16[4,8,16,128]{3,2,1,0:T(8,128)(2,1)}, bf16[4,8,16,128]{3,2,1,0:T(8,128)(2,1)S(1)}, u32[]{:S(2)}, u32[]{:S(2)}) %collective-permute-start.24) | collective-permute-done | bytes 131104 | tf_op jit(solution)/shard_map/ppermute | solution.py:23
  143.1 10.5 %collective-permute-start.11 = (bf16[4,8,16,128]{3,2,1,0:T(8,128)(2,1)}, bf16[4,8,16,128]{3,2,1,0:T(8,128)(2,1)S(1)}, u32[]{:S(2)}, u32[]{:S(2)}) collective-permute-start(bf16[4,8,16,128]{3,2,1,0:T(8,128)(2,1)} %get-tuple-element.81), channel_id=1, source_target_pairs={{0,20},{4,16},{8,28},{12,24},{16,4},{20,0},{24,12},{28,8},{1,21},{... | collective-permute-start | bytes 393224 | tf_op jit(solution)/shard_map/ppermute | solution.py:23
  154.2 4.3 %collective-permute-done.10.refs_4_ = bf16[4,8,16,128]{3,2,1,0:T(8,128)(2,1)S(1)} collective-permute-done((bf16[4,8,16,128]{3,2,1,0:T(8,128)(2,1)}, bf16[4,8,16,128]{3,2,1,0:T(8,128)(2,1)S(1)}, u32[]{:S(2)}, u32[]{:S(2)}) %collective-permute-start.10) | collective-permute-done | bytes 131104 | tf_op jit(solution)/shard_map/ppermute | solution.py:23
  158.6 5.8 %collective-permute-start.13 = (bf16[4,8,16,128]{3,2,1,0:T(8,128)(2,1)}, bf16[4,8,16,128]{3,2,1,0:T(8,128)(2,1)S(1)}, u32[]{:S(2)}, u32[]{:S(2)}) collective-permute-start(bf16[4,8,16,128]{3,2,1,0:T(8,128)(2,1)} %get-tuple-element.83), channel_id=1, source_target_pairs={{0,28},{4,24},{8,20},{12,16},{16,12},{20,8},{24,4},{28,0},{1,29},{... | collective-permute-start | bytes 393224 | tf_op jit(solution)/shard_map/ppermute | solution.py:23
  167.8 9.4 %shard_map.114 = (f32[4096,256]{1,0:T(8,128)}, bf16[4,8,16,256]{3,2,1,0:T(8,128)(2,1)}, bf16[4,8,16,256]{3,2,1,0:T(8,128)(2,1)}, bf16[4,8,16,256]{3,2,1,0:T(8,12...) custom-call(s32[2]{0:T(128)} %pad_add_fusion.index, ...), custom_call_target="tpu_custom_call" | custom-call | flops 2147483648 | bytes 17301504 | tf_op jit(solution)/shard_map/pallas_call | solution.py:43
  178.2 8.2 %shard_map.115 = (bf16[4096,256]{1,0:T(8,128)(2,1)}, bf16[4096,256]{1,0:T(8,128)(2,1)}) custom-call(s32[2]{0:T(128)} %pad_add_fusion.index, bf16[4,8,16,128]{3,2,1,0:T(8,128)(2,1)} %get-tuple-element.76.refs_0_, bf16[4,8,16,128]{3,2,1,0:T(8,128)(2,1)} %copy-done.39, bf16[4,8,16,128]{3,2,1,0:T(8,128)(2,1)} %copy-done.40, bf16[4,8,16,128]{3,2,1,0:T(8,128)(2,1)} %copy-done.41, ...), custom_call_target="tpu_custom_call" | custom-call | flops 16777216 | bytes 14680064 | tf_op jit(solution)/shard_map/pallas_call | solution.py:43
  192.6 7.6 %shard_map.122 = f32[1024,256]{1,0:T(8,128)} custom-call(s32[2]{0:T(128)} %pad_add_fusion.index, bf16[4096,256]{1,0:T(8,128)(2,1)} %refs_0_.3, bf16[4096,256]{1,0:T(8,128)(2,1)} %collective-permute-done.28.refs_1_, bf16[4096,256]{1,0:T(8,128)(2,1)} %copy-done.1, bf16[4096,256]{1,0:T(8,128)(2,1)} %collective-permute-done.30.refs_3_, ...), custom_call_target="tpu_custom_call" | custom-call | flops 2147483648 | bytes 11534336 | tf_op jit(solution)/shard_map/pallas_call | solution.py:43
  200.2 2.6 collective-permute-start.35
  202.9 2.5 collective-permute-start.36
  208.1 12.4 %collective-permute-done.34.refs_4_ = bf16[4,8,16,256]{3,2,1,0:T(8,128)(2,1)S(1)} collective-permute-done((bf16[4,8,16,256]{3,2,1,0:T(8,128)(2,1)S(1)}, bf16[4,8,16,256]{3,2,1,0:T(8,128)(2,1)S(1)}, u32[]{:S(2)}, u32[]{:S(2)}) %collective-permute-start.34) | collective-permute-done | bytes 262176 | tf_op jit(solution)/shard_map/ppermute | solution.py:23
  222.5 3.0 shard_map.116
  228.9 5.6 %shard_map.117 = (bf16[32,8,16,256]{3,2,1,0:T(8,128)(2,1)}, bf16[4,8,16,256]{3,2,1,0:T(8,128)(2,1)}, bf16[4,8,16,256]{3,2,1,0:T(8,128)(2,1)}, bf16[4,8,16,256]{3...) custom-call(s32[2]{0:T(128)} %pad_add_fusion.index, ...), custom_call_target="tpu_custom_call" | custom-call | flops 805306368 | bytes 6848512 | tf_op jit(solution)/shard_map/pallas_call | solution.py:43
  235.8 7.9 %shard_map.121 = f32[80,128]{1,0:T(8,128)} custom-call(s32[2]{0:T(128)} %pad_add_fusion.index, bf16[4,8,16,256]{3,2,1,0:T(8,128)(2,1)} %get-tuple-element.102.refs_0_, bf16[4,8,16,256]{3,2,1,0:T(8,128)(2,1)} %copy-done.18, bf16[4,8,16,256]{3,2,1,0:T(8,128)(2,1)} %copy-done.19, bf16[4,8,16,256]{3,2,1,0:T(8,128)(2,1)} %copy-done.20, ...), custom_call_target="tpu_custom_call" | custom-call | flops 1342177280 | bytes 8429568 | tf_op jit(solution)/shard_map/pallas_call | solution.py:43
  245.2 2.7 collective-permute-done.51
  248.0 7.8 %collective-permute-start.39 = (bf16[4,8,16,256]{3,2,1,0:T(8,128)(2,1)}, bf16[4,8,16,256]{3,2,1,0:T(8,128)(2,1)}, u32[]{:S(2)}, u32[]{:S(2)}) collective-permute-start(bf16[4,8,16,256]{3,2,1,0:T(8,128)(2,1)} %get-tuple-element.114), channel_id=1, source_target_pairs={{0,8},{4,12},{8,0},{12,4},{16,24},{20,28},{24,16},{28,20},{1,9},{5... | collective-permute-start | bytes 786440 | tf_op jit(solution)/shard_map/ppermute | solution.py:23
  259.6 9.8 %collective-permute-done.39.refs_2_ = bf16[4,8,16,256]{3,2,1,0:T(8,128)(2,1)} collective-permute-done((bf16[4,8,16,256]{3,2,1,0:T(8,128)(2,1)}, bf16[4,8,16,256]{3,2,1,0:T(8,128)(2,1)}, u32[]{:S(2)}, u32[]{:S(2)}) %collective-permute-start.39) | collective-permute-done | bytes 262176 | tf_op jit(solution)/shard_map/ppermute | solution.py:23
  269.4 2.9 collective-permute-done.40.refs_3_
  274.1 4.6 %collective-permute-start.44 = (bf16[4,8,16,256]{3,2,1,0:T(8,128)(2,1)}, bf16[4,8,16,256]{3,2,1,0:T(8,128)(2,1)S(1)}, u32[]{:S(2)}, u32[]{:S(2)}) collective-permute-start(bf16[4,8,16,256]{3,2,1,0:T(8,128)(2,1)} %get-tuple-element.119), channel_id=1, source_target_pairs={{0,28},{4,24},{8,20},{12,16},{16,12},{20,8},{24,4},{28,0},{1,29},{... | collective-permute-start | bytes 786440 | tf_op jit(solution)/shard_map/ppermute | solution.py:23
  280.6 13.5 %collective-permute-done.42.refs_5_ = bf16[4,8,16,256]{3,2,1,0:T(8,128)(2,1)S(1)} collective-permute-done((bf16[4,8,16,256]{3,2,1,0:T(8,128)(2,1)}, bf16[4,8,16,256]{3,2,1,0:T(8,128)(2,1)S(1)}, u32[]{:S(2)}, u32[]{:S(2)}) %collective-permute-start.42) | collective-permute-done | bytes 262176 | tf_op jit(solution)/shard_map/ppermute | solution.py:23
  294.2 6.3 %collective-permute-start.54 = (f32[2,128,256]{2,1,0:T(8,128)}, f32[2,128,256]{2,1,0:T(8,128)}, u32[]{:S(2)}, u32[]{:S(2)}) collective-permute-start(f32[2,128,256]{2,1,0:T(8,128)} %dynamic-slice_bitcast_fusion.1), channel_id=1, source_target_pairs={{0,8},{4,12},{8,0},{12,4},{16,24},{20,28},{24,16},{28,20},{1,9},{5... | collective-permute-start | bytes 786440 | tf_op jit(solution)/shard_map/ppermute | solution.py:23
  301.2 5.9 %shard_map.118 = (bf16[4096,256]{1,0:T(8,128)(2,1)}, bf16[32,16,128]{2,1,0:T(8,128)(2,1)}) custom-call(s32[2]{0:T(128)} %pad_add_fusion.index, bf16[4,8,16,256]{3,2,1,0:T(8,128)(2,1)} %get-tuple-element.112.refs_0_, bf16[4,8,16,256]{3,2,1,0:T(8,128)(2,1)} %copy-done.17, bf16[4,8,16,256]{3,2,1,0:T(8,128)(2,1)} %collective-permute-done.39.refs_2_, ...), custom_call_target="tpu_custom_call" | custom-call | flops 134217728 | bytes 6422528 | tf_op jit(solution)/shard_map/pallas_call | solution.py:43
  307.2 4.7 %all-to-all-start = ((bf16[32,16,128]{2,1,0:T(8,128)(2,1)}), bf16[32,16,128]{2,1,0:T(8,128)(2,1)S(1)}, u32[]{:S(2)}, u32[]{:S(2)}) async-start(bf16[32,16,128]{2,1,0:T(8,128)(2,1)} %get-tuple-element.122), calls=%async_computation | async-start | bytes 262144 | tf_op jit(solution)/shard_map/all_to_all | solution.py:466
  314.6 5.5 %all-to-all-done = bf16[32,16,128]{2,1,0:T(8,128)(2,1)S(1)} async-done(((bf16[32,16,128]{2,1,0:T(8,128)(2,1)}), bf16[32,16,128]{2,1,0:T(8,128)(2,1)S(1)}, u32[]{:S(2)}, u32[]{:S(2)}) %all-to-all-start) | async-done | bytes 131104 | tf_op jit(solution)/shard_map/all_to_all | solution.py:466
  320.8 3.4 all-to-all-start.2
  325.9 2.8 collective-permute-start.55
  328.7 5.9 %all-to-all-done.2 = bf16[8,80,128]{2,1,0:T(8,128)(2,1)S(1)} async-done(((bf16[8,80,128]{2,1,0:T(8,128)(2,1)}), bf16[8,80,128]{2,1,0:T(8,128)(2,1)S(1)}, u32[]{:S(2)}, u32[]{:S(2)}) %all-to-all-start.2) | async-done | bytes 163872 | tf_op jit(solution)/shard_map/all_to_all | solution.py:451
  335.3 2.6 all-to-all-start.1
  342.5 3.6 %all-to-all-done.1 = bf16[32,16,128]{2,1,0:T(8,128)(2,1)S(1)} async-done(((bf16[32,16,128]{2,1,0:T(8,128)(2,1)}), bf16[32,16,128]{2,1,0:T(8,128)(2,1)S(1)}, u32[]{:S(2)}, u32[]{:S(2)}) %all-to-all-start.1) | async-done | bytes 131104 | tf_op jit(solution)/shard_map/all_to_all | solution.py:468
  347.7 8.6 %shard_map.119.refs_2_ = f32[4096,256]{1,0:T(8,128)} custom-call(s32[2]{0:T(128)} %pad_add_fusion.index, bf16[4096,256]{1,0:T(8,128)(2,1)} %get-tuple-element.121.refs_0_.refs_4_, bf16[4096,256]{1,0:T(8,128)(2,1)} %collective-permute-done.45.refs_1_, bf16[4096,256]{1,0:T(8,128)(2,1)} %collective-permute-done.46.refs_2_, ...), custom_call_target="tpu_custom_call" | custom-call | flops 2147483648 | bytes 15204352 | tf_op jit(solution)/shard_map/pallas_call | solution.py:43
  356.3 5.9 %shard_map.120 = bf16[4096,256]{1,0:T(8,128)(2,1)} custom-call(s32[2]{0:T(128)} %pad_add_fusion.index, bf16[4096,256]{1,0:T(8,128)(2,1)} %get-tuple-element.120.refs_0_, bf16[16,64,64]{2,1,0:T(8,128)(2,1)} %refs_1_.1, f32[4096,256]{1,0:T(8,128)} %shard_map.119.refs_2_), custom_call_target="tpu_custom_call" | custom-call | flops 134217728 | bytes 8519680 | tf_op jit(solution)/shard_map/pallas_call | solution.py:43
  (209 shorter events, 66.8 us)
Async XLA Ops:
  0.6 48.9 %collective-permute-start.29 = (bf16[4096,256]{1,0:T(8,128)(2,1)}, bf16[4096,256]{1,0:T(8,128)(2,1)S(1)}, u32[]{:S(2)}, u32[]{:S(2)}) collective-permute-start(bf16[4096,256]{1,0:T(8,128)(2,1)} %refs_0_.3), channel_id=1, source_target_pairs={{0,2},{1,3},{2,0},{3,1},{4,6},{5,7},{6,4},{7,5},{8,10},{9,11},{10,... | collective-permute-start | bytes 6291464 | tf_op jit(solution)/shard_map/ppermute | solution.py:23
  3.7 162.0 %collective-permute-start.28 = (bf16[4096,256]{1,0:T(8,128)(2,1)}, bf16[4096,256]{1,0:T(8,128)(2,1)}, u32[]{:S(2)}, u32[]{:S(2)}) collective-permute-start(bf16[4096,256]{1,0:T(8,128)(2,1)} %refs_0_.3), channel_id=1, source_target_pairs={{0,1},{1,0},{2,3},{3,2},{4,5},{5,4},{6,7},{7,6},{8,9},{9,8},{10,11... | collective-permute-start | bytes 6291464 | tf_op jit(solution)/shard_map/ppermute | solution.py:23
  49.5 116.1 %collective-permute-start.30 = (bf16[4096,256]{1,0:T(8,128)(2,1)S(1)}, bf16[4096,256]{1,0:T(8,128)(2,1)}, u32[]{:S(2)}, u32[]{:S(2)}) collective-permute-start(bf16[4096,256]{1,0:T(8,128)(2,1)S(1)} %collective-permute-done.29.refs_2_), channel_id=1, source_target_pairs={{0,1},{1,0},{2,3},{3,2},{4,5},{5,4},{6,7},{7,6},{8,9},{9,8},{10,11... | collective-permute-start | bytes 6291464 | tf_op jit(solution)/shard_map/ppermute | solution.py:23
  58.2 11.9 %collective-permute-start.16 = (bf16[4,8,16,128]{3,2,1,0:T(8,128)(2,1)}, bf16[4,8,16,128]{3,2,1,0:T(8,128)(2,1)S(1)}, u32[]{:S(2)}, u32[]{:S(2)}) collective-permute-start(bf16[4,8,16,128]{3,2,1,0:T(8,128)(2,1)} %get-tuple-element.87), channel_id=1, source_target_pairs={{0,12},{4,8},{8,4},{12,0},{16,28},{20,24},{24,20},{28,16},{1,13},{... | collective-permute-start | bytes 393224 | tf_op jit(solution)/shard_map/ppermute | solution.py:23
  60.9 12.4 %collective-permute-start.17 = (bf16[4,8,16,128]{3,2,1,0:T(8,128)(2,1)}, bf16[4,8,16,128]{3,2,1,0:T(8,128)(2,1)S(1)}, u32[]{:S(2)}, u32[]{:S(2)}) collective-permute-start(bf16[4,8,16,128]{3,2,1,0:T(8,128)(2,1)} %get-tuple-element.88), channel_id=1, source_target_pairs={{0,16},{4,20},{8,24},{12,28},{16,0},{20,4},{24,8},{28,12},{1,17},{... | collective-permute-start | bytes 393224 | tf_op jit(solution)/shard_map/ppermute | solution.py:23
  63.8 18.1 %collective-permute-start.18 = (bf16[4,8,16,128]{3,2,1,0:T(8,128)(2,1)}, bf16[4,8,16,128]{3,2,1,0:T(8,128)(2,1)S(1)}, u32[]{:S(2)}, u32[]{:S(2)}) collective-permute-start(bf16[4,8,16,128]{3,2,1,0:T(8,128)(2,1)} %get-tuple-element.89), channel_id=1, source_target_pairs={{0,20},{4,16},{8,28},{12,24},{16,4},{20,0},{24,12},{28,8},{1,21},{... | collective-permute-start | bytes 393224 | tf_op jit(solution)/shard_map/ppermute | solution.py:23
  70.1 11.8 %collective-permute-start.19 = (bf16[4,8,16,128]{3,2,1,0:T(8,128)(2,1)S(1)}, bf16[4,8,16,128]{3,2,1,0:T(8,128)(2,1)S(1)}, u32[]{:S(2)}, u32[]{:S(2)}) collective-permute-start(bf16[4,8,16,128]{3,2,1,0:T(8,128)(2,1)S(1)} %copy-done.49), channel_id=1, source_target_pairs={{0,24},{4,28},{8,16},{12,20},{16,8},{20,12},{24,0},{28,4},{1,25},{... | collective-permute-start | bytes 393224 | tf_op jit(solution)/shard_map/ppermute | solution.py:23
  73.3 12.2 %collective-permute-start.20 = (bf16[4,8,16,128]{3,2,1,0:T(8,128)(2,1)S(1)}, bf16[4,8,16,128]{3,2,1,0:T(8,128)(2,1)S(1)}, u32[]{:S(2)}, u32[]{:S(2)}) collective-permute-start(bf16[4,8,16,128]{3,2,1,0:T(8,128)(2,1)S(1)} %copy-done.48), channel_id=1, source_target_pairs={{0,28},{4,24},{8,20},{12,16},{16,12},{20,8},{24,4},{28,0},{1,29},{... | collective-permute-start | bytes 393224 | tf_op jit(solution)/shard_map/ppermute | solution.py:23
  88.5 15.9 %collective-permute-start.3 = (bf16[4,8,16,128]{3,2,1,0:T(8,128)(2,1)}, bf16[4,8,16,128]{3,2,1,0:T(8,128)(2,1)S(1)}, u32[]{:S(2)}, u32[]{:S(2)}) collective-permute-start(bf16[4,8,16,128]{3,2,1,0:T(8,128)(2,1)} %get-tuple-element.70), channel_id=1, source_target_pairs={{0,16},{4,20},{8,24},{12,28},{16,0},{20,4},{24,8},{28,12},{1,17},{... | collective-permute-start | bytes 393224 | tf_op jit(solution)/shard_map/ppermute | solution.py:23
  90.5 28.8 %collective-permute-start.4 = (bf16[4,8,16,128]{3,2,1,0:T(8,128)(2,1)}, bf16[4,8,16,128]{3,2,1,0:T(8,128)(2,1)}, u32[]{:S(2)}, u32[]{:S(2)}) collective-permute-start(bf16[4,8,16,128]{3,2,1,0:T(8,128)(2,1)} %get-tuple-element.71), channel_id=1, source_target_pairs={{0,20},{4,16},{8,28},{12,24},{16,4},{20,0},{24,12},{28,8},{1,21},{... | collective-permute-start | bytes 393224 | tf_op jit(solution)/shard_map/ppermute | solution.py:23
  94.0 26.4 %collective-permute-start.5 = (bf16[4,8,16,128]{3,2,1,0:T(8,128)(2,1)}, bf16[4,8,16,128]{3,2,1,0:T(8,128)(2,1)}, u32[]{:S(2)}, u32[]{:S(2)}) collective-permute-start(bf16[4,8,16,128]{3,2,1,0:T(8,128)(2,1)} %get-tuple-element.72), channel_id=1, source_target_pairs={{0,24},{4,28},{8,16},{12,20},{16,8},{20,12},{24,0},{28,4},{1,25},{... | collective-permute-start | bytes 393224 | tf_op jit(solution)/shard_map/ppermute | solution.py:23
  104.4 16.0 %collective-permute-start.6 = (bf16[4,8,16,128]{3,2,1,0:T(8,128)(2,1)}, bf16[4,8,16,128]{3,2,1,0:T(8,128)(2,1)}, u32[]{:S(2)}, u32[]{:S(2)}) collective-permute-start(bf16[4,8,16,128]{3,2,1,0:T(8,128)(2,1)} %get-tuple-element.73), channel_id=1, source_target_pairs={{0,28},{4,24},{8,20},{12,16},{16,12},{20,8},{24,4},{28,0},{1,29},{... | collective-permute-start | bytes 393224 | tf_op jit(solution)/shard_map/ppermute | solution.py:23
  126.0 14.3 %collective-permute-start.24 = (bf16[4,8,16,128]{3,2,1,0:T(8,128)(2,1)}, bf16[4,8,16,128]{3,2,1,0:T(8,128)(2,1)S(1)}, u32[]{:S(2)}, u32[]{:S(2)}) collective-permute-start(bf16[4,8,16,128]{3,2,1,0:T(8,128)(2,1)} %get-tuple-element.96), channel_id=1, source_target_pairs={{0,16},{4,20},{8,24},{12,28},{16,0},{20,4},{24,8},{28,12},{1,17},{... | collective-permute-start | bytes 393224 | tf_op jit(solution)/shard_map/ppermute | solution.py:23
  126.0 17.1 %collective-permute-start.25 = (bf16[4,8,16,128]{3,2,1,0:T(8,128)(2,1)}, bf16[4,8,16,128]{3,2,1,0:T(8,128)(2,1)S(1)}, u32[]{:S(2)}, u32[]{:S(2)}) collective-permute-start(bf16[4,8,16,128]{3,2,1,0:T(8,128)(2,1)} %get-tuple-element.97), channel_id=1, source_target_pairs={{0,20},{4,16},{8,28},{12,24},{16,4},{20,0},{24,12},{28,8},{1,21},{... | collective-permute-start | bytes 393224 | tf_op jit(solution)/shard_map/ppermute | solution.py:23
  129.1 14.0 %collective-permute-start.26 = (bf16[4,8,16,128]{3,2,1,0:T(8,128)(2,1)}, bf16[4,8,16,128]{3,2,1,0:T(8,128)(2,1)S(1)}, u32[]{:S(2)}, u32[]{:S(2)}) collective-permute-start(bf16[4,8,16,128]{3,2,1,0:T(8,128)(2,1)} %get-tuple-element.98), channel_id=1, source_target_pairs={{0,24},{4,28},{8,16},{12,20},{16,8},{20,12},{24,0},{28,4},{1,25},{... | collective-permute-start | bytes 393224 | tf_op jit(solution)/shard_map/ppermute | solution.py:23
  140.3 13.4 %collective-permute-start.27 = (bf16[4,8,16,128]{3,2,1,0:T(8,128)(2,1)}, bf16[4,8,16,128]{3,2,1,0:T(8,128)(2,1)S(1)}, u32[]{:S(2)}, u32[]{:S(2)}) collective-permute-start(bf16[4,8,16,128]{3,2,1,0:T(8,128)(2,1)} %get-tuple-element.99), channel_id=1, source_target_pairs={{0,28},{4,24},{8,20},{12,16},{16,12},{20,8},{24,4},{28,0},{1,29},{... | collective-permute-start | bytes 393224 | tf_op jit(solution)/shard_map/ppermute | solution.py:23
  143.1 15.4 %collective-permute-start.10 = (bf16[4,8,16,128]{3,2,1,0:T(8,128)(2,1)}, bf16[4,8,16,128]{3,2,1,0:T(8,128)(2,1)S(1)}, u32[]{:S(2)}, u32[]{:S(2)}) collective-permute-start(bf16[4,8,16,128]{3,2,1,0:T(8,128)(2,1)} %get-tuple-element.80), channel_id=1, source_target_pairs={{0,16},{4,20},{8,24},{12,28},{16,0},{20,4},{24,8},{28,12},{1,17},{... | collective-permute-start | bytes 393224 | tf_op jit(solution)/shard_map/ppermute | solution.py:23
  143.1 21.2 %collective-permute-start.11 = (bf16[4,8,16,128]{3,2,1,0:T(8,128)(2,1)}, bf16[4,8,16,128]{3,2,1,0:T(8,128)(2,1)S(1)}, u32[]{:S(2)}, u32[]{:S(2)}) collective-permute-start(bf16[4,8,16,128]{3,2,1,0:T(8,128)(2,1)} %get-tuple-element.81), channel_id=1, source_target_pairs={{0,20},{4,16},{8,28},{12,24},{16,4},{20,0},{24,12},{28,8},{1,21},{... | collective-permute-start | bytes 393224 | tf_op jit(solution)/shard_map/ppermute | solution.py:23
  153.7 23.6 %collective-permute-start.12 = (bf16[4,8,16,128]{3,2,1,0:T(8,128)(2,1)}, bf16[4,8,16,128]{3,2,1,0:T(8,128)(2,1)S(1)}, u32[]{:S(2)}, u32[]{:S(2)}) collective-permute-start(bf16[4,8,16,128]{3,2,1,0:T(8,128)(2,1)} %get-tuple-element.82), channel_id=1, source_target_pairs={{0,24},{4,28},{8,16},{12,20},{16,8},{20,12},{24,0},{28,4},{1,25},{... | collective-permute-start | bytes 393224 | tf_op jit(solution)/shard_map/ppermute | solution.py:23
  158.6 18.8 %collective-permute-start.13 = (bf16[4,8,16,128]{3,2,1,0:T(8,128)(2,1)}, bf16[4,8,16,128]{3,2,1,0:T(8,128)(2,1)S(1)}, u32[]{:S(2)}, u32[]{:S(2)}) collective-permute-start(bf16[4,8,16,128]{3,2,1,0:T(8,128)(2,1)} %get-tuple-element.83), channel_id=1, source_target_pairs={{0,28},{4,24},{8,20},{12,16},{16,12},{20,8},{24,4},{28,0},{1,29},{... | collective-permute-start | bytes 393224 | tf_op jit(solution)/shard_map/ppermute | solution.py:23
  164.3 13.0 %collective-permute-start.7 = (bf16[4,8,16,128]{3,2,1,0:T(8,128)(2,1)}, bf16[4,8,16,128]{3,2,1,0:T(8,128)(2,1)S(1)}, u32[]{:S(2)}, u32[]{:S(2)}) collective-permute-start(bf16[4,8,16,128]{3,2,1,0:T(8,128)(2,1)} %get-tuple-element.77), channel_id=1, source_target_pairs={{0,4},{4,0},{8,12},{12,8},{16,20},{20,16},{24,28},{28,24},{1,5},{5... | collective-permute-start | bytes 393224 | tf_op jit(solution)/shard_map/ppermute | solution.py:23
  165.6 11.7 %collective-permute-start.8 = (bf16[4,8,16,128]{3,2,1,0:T(8,128)(2,1)}, bf16[4,8,16,128]{3,2,1,0:T(8,128)(2,1)S(1)}, u32[]{:S(2)}, u32[]{:S(2)}) collective-permute-start(bf16[4,8,16,128]{3,2,1,0:T(8,128)(2,1)} %get-tuple-element.78), channel_id=1, source_target_pairs={{0,8},{4,12},{8,0},{12,4},{16,24},{20,28},{24,16},{28,20},{1,9},{5... | collective-permute-start | bytes 393224 | tf_op jit(solution)/shard_map/ppermute | solution.py:23
  165.7 11.7 %collective-permute-start.9 = (bf16[4,8,16,128]{3,2,1,0:T(8,128)(2,1)}, bf16[4,8,16,128]{3,2,1,0:T(8,128)(2,1)S(1)}, u32[]{:S(2)}, u32[]{:S(2)}) collective-permute-start(bf16[4,8,16,128]{3,2,1,0:T(8,128)(2,1)} %get-tuple-element.79), channel_id=1, source_target_pairs={{0,12},{4,8},{8,4},{12,0},{16,28},{20,24},{24,20},{28,16},{1,13},{... | collective-permute-start | bytes 393224 | tf_op jit(solution)/shard_map/ppermute | solution.py:23
  186.4 41.4 %collective-permute-start.46 = (bf16[4096,256]{1,0:T(8,128)(2,1)}, bf16[4096,256]{1,0:T(8,128)(2,1)}, u32[]{:S(2)}, u32[]{:S(2)}) collective-permute-start(bf16[4096,256]{1,0:T(8,128)(2,1)} %get-tuple-element.121.refs_0_.refs_4_), channel_id=1, source_target_pairs={{0,2},{1,3},{2,0},{3,1},{4,6},{5,7},{6,4},{7,5},{8,10},{9,11},{10,... | collective-permute-start | bytes 6291464 | tf_op jit(solution)/shard_map/ppermute | solution.py:23
  188.0 12.2 %collective-permute-start.31 = (bf16[4,8,16,256]{3,2,1,0:T(8,128)(2,1)}, bf16[4,8,16,256]{3,2,1,0:T(8,128)(2,1)S(1)}, u32[]{:S(2)}, u32[]{:S(2)}) collective-permute-start(bf16[4,8,16,256]{3,2,1,0:T(8,128)(2,1)} %get-tuple-element.103), channel_id=1, source_target_pairs={{0,4},{4,0},{8,12},{12,8},{16,20},{20,16},{24,28},{28,24},{1,5},{5... | collective-permute-start | bytes 786440 | tf_op jit(solution)/shard_map/ppermute | solution.py:23
  189.3 13.6 %collective-permute-start.32 = (bf16[4,8,16,256]{3,2,1,0:T(8,128)(2,1)}, bf16[4,8,16,256]{3,2,1,0:T(8,128)(2,1)S(1)}, u32[]{:S(2)}, u32[]{:S(2)}) collective-permute-start(bf16[4,8,16,256]{3,2,1,0:T(8,128)(2,1)} %get-tuple-element.104), channel_id=1, source_target_pairs={{0,8},{4,12},{8,0},{12,4},{16,24},{20,28},{24,16},{28,20},{1,9},{5... | collective-permute-start | bytes 786440 | tf_op jit(solution)/shard_map/ppermute | solution.py:23
  189.3 16.0 %collective-permute-start.33 = (bf16[4,8,16,256]{3,2,1,0:T(8,128)(2,1)S(1)}, bf16[4,8,16,256]{3,2,1,0:T(8,128)(2,1)S(1)}, u32[]{:S(2)}, u32[]{:S(2)}) collective-permute-start(bf16[4,8,16,256]{3,2,1,0:T(8,128)(2,1)S(1)} %copy-done.47), channel_id=1, source_target_pairs={{0,12},{4,8},{8,4},{12,0},{16,28},{20,24},{24,20},{28,16},{1,13},{... | collective-permute-start | bytes 786440 | tf_op jit(solution)/shard_map/ppermute | solution.py:23
  191.5 29.0 %collective-permute-start.34 = (bf16[4,8,16,256]{3,2,1,0:T(8,128)(2,1)S(1)}, bf16[4,8,16,256]{3,2,1,0:T(8,128)(2,1)S(1)}, u32[]{:S(2)}, u32[]{:S(2)}) collective-permute-start(bf16[4,8,16,256]{3,2,1,0:T(8,128)(2,1)S(1)} %copy-done.46), channel_id=1, source_target_pairs={{0,16},{4,20},{8,24},{12,28},{16,0},{20,4},{24,8},{28,12},{1,17},{... | collective-permute-start | bytes 786440 | tf_op jit(solution)/shard_map/ppermute | solution.py:23
  200.2 27.4 %collective-permute-start.35 = (bf16[4,8,16,256]{3,2,1,0:T(8,128)(2,1)S(1)}, bf16[4,8,16,256]{3,2,1,0:T(8,128)(2,1)S(1)}, u32[]{:S(2)}, u32[]{:S(2)}) collective-permute-start(bf16[4,8,16,256]{3,2,1,0:T(8,128)(2,1)S(1)} %copy-done.45), channel_id=1, source_target_pairs={{0,20},{4,16},{8,28},{12,24},{16,4},{20,0},{24,12},{28,8},{1,21},{... | collective-permute-start | bytes 786440 | tf_op jit(solution)/shard_map/ppermute | solution.py:23
  202.9 25.2 %collective-permute-start.36 = (bf16[4,8,16,256]{3,2,1,0:T(8,128)(2,1)S(1)}, bf16[4,8,16,256]{3,2,1,0:T(8,128)(2,1)S(1)}, u32[]{:S(2)}, u32[]{:S(2)}) collective-permute-start(bf16[4,8,16,256]{3,2,1,0:T(8,128)(2,1)S(1)} %copy-done.44), channel_id=1, source_target_pairs={{0,24},{4,28},{8,16},{12,20},{16,8},{20,12},{24,0},{28,4},{1,25},{... | collective-permute-start | bytes 786440 | tf_op jit(solution)/shard_map/ppermute | solution.py:23
  205.4 22.7 %collective-permute-start.37 = (bf16[4,8,16,256]{3,2,1,0:T(8,128)(2,1)S(1)}, bf16[4,8,16,256]{3,2,1,0:T(8,128)(2,1)S(1)}, u32[]{:S(2)}, u32[]{:S(2)}) collective-permute-start(bf16[4,8,16,256]{3,2,1,0:T(8,128)(2,1)S(1)} %copy-done.43), channel_id=1, source_target_pairs={{0,28},{4,24},{8,20},{12,16},{16,12},{20,8},{24,4},{28,0},{1,29},{... | collective-permute-start | bytes 786440 | tf_op jit(solution)/shard_map/ppermute | solution.py:23
  220.5 35.3 %collective-permute-start.53 = (f32[4,128,256]{2,1,0:T(8,128)S(1)}, f32[4,128,256]{2,1,0:T(8,128)}, u32[]{:S(2)}, u32[]{:S(2)}) collective-permute-start(f32[4,128,256]{2,1,0:T(8,128)S(1)} %dynamic-slice_bitcast_fusion), channel_id=1, source_target_pairs={{0,4},{4,0},{8,12},{12,8},{16,20},{20,16},{24,28},{28,24},{1,5},{5... | collective-permute-start | bytes 1572872 | tf_op jit(solution)/shard_map/ppermute | solution.py:23
  227.6 119.5 %collective-permute-start.45 = (bf16[4096,256]{1,0:T(8,128)(2,1)S(1)}, bf16[4096,256]{1,0:T(8,128)(2,1)}, u32[]{:S(2)}, u32[]{:S(2)}) collective-permute-start(bf16[4096,256]{1,0:T(8,128)(2,1)S(1)} %copy-done), channel_id=1, source_target_pairs={{0,1},{1,0},{2,3},{3,2},{4,5},{5,4},{6,7},{7,6},{8,9},{9,8},{10,11... | collective-permute-start | bytes 6291464 | tf_op jit(solution)/shard_map/ppermute | solution.py:23
  227.8 119.3 %collective-permute-start.47 = (bf16[4096,256]{1,0:T(8,128)(2,1)}, bf16[4096,256]{1,0:T(8,128)(2,1)}, u32[]{:S(2)}, u32[]{:S(2)}) collective-permute-start(bf16[4096,256]{1,0:T(8,128)(2,1)} %collective-permute-done.46.refs_2_), channel_id=1, source_target_pairs={{0,1},{1,0},{2,3},{3,2},{4,5},{5,4},{6,7},{7,6},{8,9},{9,8},{10,11... | collective-permute-start | bytes 6291464 | tf_op jit(solution)/shard_map/ppermute | solution.py:23
  234.5 21.9 %collective-permute-start.38 = (bf16[4,8,16,256]{3,2,1,0:T(8,128)(2,1)}, bf16[4,8,16,256]{3,2,1,0:T(8,128)(2,1)S(1)}, u32[]{:S(2)}, u32[]{:S(2)}) collective-permute-start(bf16[4,8,16,256]{3,2,1,0:T(8,128)(2,1)} %get-tuple-element.113), channel_id=1, source_target_pairs={{0,4},{4,0},{8,12},{12,8},{16,20},{20,16},{24,28},{28,24},{1,5},{5... | collective-permute-start | bytes 786440 | tf_op jit(solution)/shard_map/ppermute | solution.py:23
  248.0 21.5 %collective-permute-start.39 = (bf16[4,8,16,256]{3,2,1,0:T(8,128)(2,1)}, bf16[4,8,16,256]{3,2,1,0:T(8,128)(2,1)}, u32[]{:S(2)}, u32[]{:S(2)}) collective-permute-start(bf16[4,8,16,256]{3,2,1,0:T(8,128)(2,1)} %get-tuple-element.114), channel_id=1, source_target_pairs={{0,8},{4,12},{8,0},{12,4},{16,24},{20,28},{24,16},{28,20},{1,9},{5... | collective-permute-start | bytes 786440 | tf_op jit(solution)/shard_map/ppermute | solution.py:23
  255.8 16.5 %collective-permute-start.40 = (bf16[4,8,16,256]{3,2,1,0:T(8,128)(2,1)}, bf16[4,8,16,256]{3,2,1,0:T(8,128)(2,1)}, u32[]{:S(2)}, u32[]{:S(2)}) collective-permute-start(bf16[4,8,16,256]{3,2,1,0:T(8,128)(2,1)} %get-tuple-element.115), channel_id=1, source_target_pairs={{0,12},{4,8},{8,4},{12,0},{16,28},{20,24},{24,20},{28,16},{1,13},{... | collective-permute-start | bytes 786440 | tf_op jit(solution)/shard_map/ppermute | solution.py:23
  256.4 17.6 %collective-permute-start.41 = (bf16[4,8,16,256]{3,2,1,0:T(8,128)(2,1)}, bf16[4,8,16,256]{3,2,1,0:T(8,128)(2,1)}, u32[]{:S(2)}, u32[]{:S(2)}) collective-permute-start(bf16[4,8,16,256]{3,2,1,0:T(8,128)(2,1)} %get-tuple-element.116), channel_id=1, source_target_pairs={{0,16},{4,20},{8,24},{12,28},{16,0},{20,4},{24,8},{28,12},{1,17},{... | collective-permute-start | bytes 786440 | tf_op jit(solution)/shard_map/ppermute | solution.py:23
  269.4 24.7 %collective-permute-start.42 = (bf16[4,8,16,256]{3,2,1,0:T(8,128)(2,1)}, bf16[4,8,16,256]{3,2,1,0:T(8,128)(2,1)S(1)}, u32[]{:S(2)}, u32[]{:S(2)}) collective-permute-start(bf16[4,8,16,256]{3,2,1,0:T(8,128)(2,1)} %get-tuple-element.117), channel_id=1, source_target_pairs={{0,20},{4,16},{8,28},{12,24},{16,4},{20,0},{24,12},{28,8},{1,21},{... | collective-permute-start | bytes 786440 | tf_op jit(solution)/shard_map/ppermute | solution.py:23
  272.3 21.8 %collective-permute-start.43 = (bf16[4,8,16,256]{3,2,1,0:T(8,128)(2,1)}, bf16[4,8,16,256]{3,2,1,0:T(8,128)(2,1)S(1)}, u32[]{:S(2)}, u32[]{:S(2)}) collective-permute-start(bf16[4,8,16,256]{3,2,1,0:T(8,128)(2,1)} %get-tuple-element.118), channel_id=1, source_target_pairs={{0,24},{4,28},{8,16},{12,20},{16,8},{20,12},{24,0},{28,4},{1,25},{... | collective-permute-start | bytes 786440 | tf_op jit(solution)/shard_map/ppermute | solution.py:23
  274.1 26.4 %collective-permute-start.44 = (bf16[4,8,16,256]{3,2,1,0:T(8,128)(2,1)}, bf16[4,8,16,256]{3,2,1,0:T(8,128)(2,1)S(1)}, u32[]{:S(2)}, u32[]{:S(2)}) collective-permute-start(bf16[4,8,16,256]{3,2,1,0:T(8,128)(2,1)} %get-tuple-element.119), channel_id=1, source_target_pairs={{0,28},{4,24},{8,20},{12,16},{16,12},{20,8},{24,4},{28,0},{1,29},{... | collective-permute-start | bytes 786440 | tf_op jit(solution)/shard_map/ppermute | solution.py:23
  294.2 18.8 %collective-permute-start.52 = (f32[80,128]{1,0:T(8,128)S(1)}, f32[80,128]{1,0:T(8,128)S(1)}, u32[]{:S(2)}, u32[]{:S(2)}) collective-permute-start(f32[80,128]{1,0:T(8,128)S(1)} %add.68), channel_id=1, source_target_pairs={{0,1},{1,0},{2,3},{3,2},{4,5},{5,4},{6,7},{7,6},{8,9},{9,8},{10,11... | collective-permute-start | bytes 122888 | tf_op jit(solution)/shard_map/ppermute | solution.py:23
  294.2 30.0 %collective-permute-start.54 = (f32[2,128,256]{2,1,0:T(8,128)}, f32[2,128,256]{2,1,0:T(8,128)}, u32[]{:S(2)}, u32[]{:S(2)}) collective-permute-start(f32[2,128,256]{2,1,0:T(8,128)} %dynamic-slice_bitcast_fusion.1), channel_id=1, source_target_pairs={{0,8},{4,12},{8,0},{12,4},{16,24},{20,28},{24,16},{28,20},{1,9},{5... | collective-permute-start | bytes 786440 | tf_op jit(solution)/shard_map/ppermute | solution.py:23
  307.2 12.9 %all-to-all-start = ((bf16[32,16,128]{2,1,0:T(8,128)(2,1)}), bf16[32,16,128]{2,1,0:T(8,128)(2,1)S(1)}, u32[]{:S(2)}, u32[]{:S(2)}) async-start(bf16[32,16,128]{2,1,0:T(8,128)(2,1)} %get-tuple-element.122), calls=%async_computation | async-start | bytes 262144 | tf_op jit(solution)/shard_map/all_to_all | solution.py:466
  312.7 34.4 %collective-permute-start.48 = (bf16[256,256]{1,0:T(8,128)(2,1)}, bf16[256,256]{1,0:T(8,128)(2,1)}, u32[]{:S(2)}, u32[]{:S(2)}) collective-permute-start(bf16[256,256]{1,0:T(8,128)(2,1)} %get-tuple-element.139), channel_id=1, source_target_pairs={{0,1},{1,0},{2,3},{3,2},{4,5},{5,4},{6,7},{7,6},{8,9},{9,8},{10,11... | collective-permute-start | bytes 393224 | tf_op jit(solution)/shard_map/ppermute | solution.py:23
  312.9 34.1 %collective-permute-start.49 = (bf16[256,256]{1,0:T(8,128)(2,1)}, bf16[256,256]{1,0:T(8,128)(2,1)}, u32[]{:S(2)}, u32[]{:S(2)}) collective-permute-start(bf16[256,256]{1,0:T(8,128)(2,1)} %get-tuple-element.141), channel_id=1, source_target_pairs={{0,2},{1,3},{2,0},{3,1},{4,6},{5,7},{6,4},{7,5},{8,10},{9,11},{10,... | collective-permute-start | bytes 393224 | tf_op jit(solution)/shard_map/ppermute | solution.py:23
  320.8 13.8 %all-to-all-start.2 = ((bf16[8,80,128]{2,1,0:T(8,128)(2,1)}), bf16[8,80,128]{2,1,0:T(8,128)(2,1)S(1)}, u32[]{:S(2)}, u32[]{:S(2)}) async-start(bf16[8,80,128]{2,1,0:T(8,128)(2,1)} %broadcast_in_dim.5), calls=%async_computation.2 | async-start | bytes 327680 | tf_op jit(solution)/shard_map/all_to_all | solution.py:451
  325.9 14.6 %collective-permute-start.55 = (f32[1,128,256]{2,1,0:T(8,128)}, f32[1,128,256]{2,1,0:T(8,128)S(1)}, u32[]{:S(2)}, u32[]{:S(2)}) collective-permute-start(f32[1,128,256]{2,1,0:T(8,128)} %constant_dynamic-slice_fusion), channel_id=1, source_target_pairs={{0,16},{4,20},{8,24},{12,28},{16,0},{20,4},{24,8},{28,12},{1,17},{... | collective-permute-start | bytes 393224 | tf_op jit(solution)/shard_map/ppermute | solution.py:23
  (61 other events, 1208.8 us)

commit v2 on v1

--- a/solution.py
+++ b/solution.py
@@ -15,6 +15,7 @@
 BF16 = jnp.bfloat16
 HALVES = 2
 BACK_HALVES = 1
+STEPS = 2
 VMEM_BYTES = 56 * 1024 * 1024
 
 
@@ -71,27 +72,33 @@
     return pl.BlockSpec(dims, lambda i, *_: (i,) + (0,) * (len(dims) - 1))
 
 
-def scatter_rows(source, pieces, me, pair, columns=slice(None)):
+def blocks_of(ref):
+    for i in range(ref.shape[0] // (B * C)):
+        for pair in range(B // 2):
+            yield (i * B + 2 * pair) * C, i, pair
+
+
+def scatter_rows(source, pieces, me, i, pair, columns=slice(None)):
     for j, piece in enumerate(pieces):
         low = source[0, rows_of(me ^ j, PER), columns]
         high = source[1, rows_of(me ^ j, PER), columns]
-        piece[0, pair] = jnp.concatenate([low, high], 0).astype(BF16)
-
-
-def gather_rows(target, pieces, me, pair, columns=slice(None)):
+        piece[i, pair] = jnp.concatenate([low, high], 0).astype(BF16)
+
+
+def gather_rows(target, pieces, me, i, pair, columns=slice(None)):
     for j, piece in enumerate(pieces):
-        both = piece[0, pair].astype(F32)
+        both = piece[i, pair].astype(F32)
         target[0, rows_of(me ^ j, PER), columns] = both[:PER]
         target[1, rows_of(me ^ j, PER), columns] = both[PER:]
 
 
 def first_kernel(index, tokens, factor, *rest):
     pieces, held = rest[:-1], rest[-1]
-    for pair in range(B // 2):
+    for row, i, pair in blocks_of(tokens):
         for side in range(2):
-            b = 2 * pair + side
-            held[pair % 2, side] = dot(factor[b], tokens[b * C : (b + 1) * C, :])
-        scatter_rows(held.at[pair % 2], pieces, index[0], pair)
+            rows = slice(row + side * C, row + (side + 1) * C)
+            held[pair % 2, side] = dot(factor[2 * pair + side], tokens[rows, :])
+        scatter_rows(held.at[pair % 2], pieces, index[0], i, pair)
 
 
 def far_kernel(n, own_a, index, *refs):
@@ -115,8 +122,8 @@
         refs[:m], refs[m : m + 3], refs[m + 3 : -1], refs[-1]
     )
     width = weight.shape[1]
-    for pair in range(B // 2):
-        rows = slice(pair * 2 * C, (pair + 1) * 2 * C)
+    for row, i, pair in blocks_of(gate_out):
+        rows = slice(row, row + 2 * C)
         gate = 0.0
         for j in range(m):
             gate += dot(gathered[j][rows, :], weight[rows_of(index[1] ^ j, width), :])
@@ -127,18 +134,18 @@
         for h in range(BACK_HALVES):
             columns = slice(h * width // BACK_HALVES, (h + 1) * width // BACK_HALVES)
             some = pieces[h * count : (h + 1) * count]
-            scatter_rows(held.at[pair % 2], some, index[0], pair, columns)
+            scatter_rows(held.at[pair % 2], some, index[0], i, pair, columns)
 
 
 def output_kernel(n, index, *refs):
     pieces, (gate_in, tokens, upstream, output, pre_grad, held) = refs[:-6], refs[-6:]
-    for pair in range(B // 2):
-        rows = slice(pair * 2 * C, (pair + 1) * 2 * C)
+    for row, i, pair in blocks_of(output):
+        rows = slice(row, row + 2 * C)
         for h in range(len(pieces) // n):
             some = pieces[h * n : (h + 1) * n]
             step = some[0].shape[-1]
             columns = slice(h * step, (h + 1) * step)
-            gather_rows(held.at[pair % 2], some, index[0], pair, columns)
+            gather_rows(held.at[pair % 2], some, index[0], i, pair, columns)
         mixed = held[pair % 2].reshape(2 * C, -1)
         gate = gate_in[rows, :]
         sig = jax.nn.sigmoid(gate)
@@ -245,37 +252,49 @@
     out[...] = total
 
 
-def first_grad_kernel(n, index, *refs):
-    pieces, (tokens, back, out, held, total) = refs[:n], refs[n:]
+def first_grad_kernel(n, last, index, *refs):
+    pieces, (tokens, *other, out, held, total) = refs[: n // 2], refs[n // 2 :]
+    me = index[0]
+    slots = range(n // 2, n) if last else range(n // 2)
 
     @pl.when(pl.program_id(0) == 0)
     def _():
         total[...] = jnp.zeros_like(total)
 
-    for pair in range(B // 2):
-        gather_rows(held.at[pair % 2], pieces, index[0], pair)
+    for row, i, pair in blocks_of(tokens):
+        for piece, j in zip(pieces, slots):
+            place = rows_of((me ^ j) % (n // 2), PER)
+            both = piece[i, pair].astype(F32)
+            held[pair % 2, 0, place, :] = both[:PER]
+            held[pair % 2, 1, place, :] = both[PER:]
         sides = []
         for side in range(2):
-            rows = slice((2 * pair + side) * C, (2 * pair + side + 1) * C)
+            rows = slice(row + side * C, row + (side + 1) * C)
             value = held[pair % 2, side].astype(BF16)
-            back[rows, :] = value
             sides.append(dot(value, tokens[rows, :], ((1,), (1,))))
-        both = jnp.concatenate(sides, 1).reshape(C // PER, PER, 2 * C)
-        total[:, pair] += both
+        total[:, pair] += jnp.concatenate(sides, 1).reshape(n // 2, PER, 2 * C)
 
     @pl.when(pl.program_id(0) == pl.num_programs(0) - 1)
     def _():
-        out[...] = total[...].reshape(out.shape).astype(out.dtype)
-
-
-def input_grad_kernel(index, *refs):
-    back, (factor, partial, out) = refs[:-3], refs[-3:]
-    for b in range(B):
-        rows = slice(b * C, (b + 1) * C)
-        value = [x[rows, :] for x in back]
-        value = value[0] if len(value) == 1 else jnp.concatenate(value, 1)
-        mixed = dot(factor[b], value, ((0,), (0,)))
-        out[rows, :] = (partial[rows, :] + mixed).astype(BF16)
+        count = out.shape[0] // 2 if last else out.shape[0]
+        mine = total[...].reshape(count, -1, 2 * C).astype(out.dtype)
+        if last:
+            half = me // (n // 2)
+            out[pl.ds(half * count, count)] = other[0][...]
+            out[pl.ds((1 - half) * count, count)] = mine
+        else:
+            out[...] = mine
+
+
+def input_grad_kernel(n, index, *refs):
+    pieces, (factor, partial, out, held) = refs[:n], refs[n:]
+    for row, i, pair in blocks_of(out):
+        gather_rows(held.at[pair % 2], pieces, index[0], i, pair)
+        for side in range(2):
+            rows = slice(row + side * C, row + (side + 1) * C)
+            value = held[pair % 2, side].astype(BF16)
+            mixed = dot(factor[2 * pair + side], value, ((0,), (0,)))
+            out[rows, :] = (partial[rows, :] + mixed).astype(BF16)
 
 
 def one_hot(dims, test):
@@ -321,22 +340,22 @@
     rows, width = tokens.shape
     own_a = rows // (B * C)
     index = jnp.stack([s, q]).astype(jnp.int32)
-    row_blocks = by_row(tokens, own_a)
+    row_blocks = by_row(tokens, STEPS)
     pair_rows = pltpu.VMEM((2, 2, C, width), F32)
 
     far_tokens = swap(tokens, "ch", 2)
     half_width = width // HALVES
     half = shape((own_a, B // 2, 2 * PER, half_width), BF16)
-    half_rows = [by_row(half, own_a)] * n
+    half_rows = [by_row(half, STEPS)] * n
     part_width = width // BACK_HALVES
     part = shape((own_a, B // 2, 2 * PER, part_width), BF16)
-    part_rows = [by_row(part, own_a)] * n
+    part_rows = [by_row(part, STEPS)] * n
     far_part = shape((A, B // 2, 2 * PER, part_width), BF16)
     first_far = []
     for h in range(HALVES):
-        columns = pl.BlockSpec((B * C, half_width), lambda i, *_, h=h: (i, h))
+        columns = pl.BlockSpec((rows // STEPS, half_width), lambda i, *_, h=h: (i, h))
         sent = call(
-            first_kernel, (own_a,), index, (tokens, first_factor),
+            first_kernel, (STEPS,), index, (tokens, first_factor),
             [columns, whole(first_factor)], [half] * n, half_rows,
             [pltpu.VMEM((2, 2, C, half_width), F32)],
             2 * rows * half_width * C,
@@ -375,7 +394,7 @@
     gate_shape = shape((rows, width), F32)
     ins = (*gathered, gate_weight, cotangent)
     gate_pre, *sent = call(
-        functools.partial(gate_kernel, m), (own_a,), index, ins,
+        functools.partial(gate_kernel, m), (STEPS,), index, ins,
         [row_blocks] * m + [whole(gate_weight), row_blocks],
         [gate_shape] + [part] * (n * BACK_HALVES),
         [row_blocks] + part_rows * BACK_HALVES, [pair_rows],
@@ -385,7 +404,7 @@
 
     ins = (*mixed_home, gate_pre, tokens, cotangent)
     output, pre_grad = call(
-        functools.partial(output_kernel, n), (own_a,), index, ins,
+        functools.partial(output_kernel, n), (STEPS,), index, ins,
         half_rows * HALVES + [row_blocks] * 3,
         [shape((rows, width), BF16)] * 2, [row_blocks] * 2,
         [pair_rows], rows * width * 16,
@@ -422,7 +441,7 @@
 
     out = shape((m * width, width), F32)
     gate_part = call(
-        functools.partial(gate_grad_kernel, m), (own_a,), index, (*gathered, pre_grad),
+        functools.partial(gate_grad_kernel, m), (STEPS,), index, (*gathered, pre_grad),
         [row_blocks] * (m + 1), [out], [whole(out)], (),
         2 * rows * width * m * width,
     )[0].reshape(n, m * width // n, width)
@@ -438,7 +457,7 @@
 
     ins = (*all_pre, *back_weight, cotangent)
     partial = call(
-        functools.partial(gate_input_kernel, m), (own_a,), index, ins,
+        functools.partial(gate_input_kernel, m), (STEPS,), index, ins,
         [row_blocks] * m + [whole(w) for w in back_weight] + [row_blocks],
         [gate_shape], [row_blocks], (), 2 * rows * width * m * width,
     )[0]
@@ -455,14 +474,21 @@
     second_grad = second_all.transpose(0, 2, 3, 1, 4).reshape(C, B, B)
 
     first_out = shape((n * m, B * C // (2 * n * m), 2 * C), BF16)
-    ins = (*back_home[0], tokens)
-    back_rows, parts = call(
-        functools.partial(first_grad_kernel, n), (own_a,), index, ins,
-        part_rows + [row_blocks], [shape((rows, width), BF16), first_out],
-        [row_blocks, whole(first_out)],
-        [pair_rows, pltpu.VMEM((n, B // 2, PER, 2 * C), F32)],
-        2 * rows * width * C,
-    )
+    near_out = shape((n * m // 2, *first_out.shape[1:]), BF16)
+    home = back_home[0]
+    held_half = pltpu.VMEM((2, 2, n // 2 * PER, width), F32)
+    total_half = pltpu.VMEM((n // 2, B // 2, PER, 2 * C), F32)
+    parts = ()
+    for last in (False, True):
+        ins = (*(home[n // 2 :] if last else home[: n // 2]), tokens, *parts)
+        outs = [first_out if last else near_out]
+        parts = call(
+            functools.partial(first_grad_kernel, n, last), (STEPS,), index, ins,
+            part_rows[: n // 2] + [row_blocks] + [whole(x) for x in parts],
+            outs, [whole(outs[0])], [held_half, total_half],
+            rows * width * C,
+        )
+    parts = parts[0]
     parts = lax.all_to_all(parts, ("seq", "ch"), split_axis=0, concat_axis=0, tiled=True)
     first_sum = parts.astype(F32).sum(0).astype(BF16)
     first_sum = lax.all_to_all(
@@ -472,11 +498,11 @@
     first_grad = first_sum.reshape(n, B // 2, PER, 2, C).transpose(1, 3, 0, 2, 4)
     first_grad = first_grad.reshape(B, C, C)
 
-    ins = (back_rows, first_factor, partial)
+    ins = (*home, first_factor, partial)
     input_grad = call(
-        input_grad_kernel, (own_a,), index, ins,
-        [row_blocks, whole(first_factor), row_blocks],
-        [shape((rows, width), BF16)], [row_blocks], (), 2 * rows * width * C,
+        functools.partial(input_grad_kernel, n), (STEPS,), index, ins,
+        part_rows + [whole(first_factor), row_blocks],
+        [shape((rows, width), BF16)], [row_blocks], [pair_rows], 2 * rows * width * C,
     )[0]
     return output, input_grad, first_grad, second_grad, third_grad, gate_grad
 

time: 364 us -> 358 us (0.984)
  starting transfers between devices: 126 us -> 120 us
    ppermute x56, starting transfers between devices: 115 us -> 108 us  [swap(): return lax.ppermute(values, axis, [(i, i ^ step) for i in range(count)])]
    pallas_call x14 -> x15, Pallas kernels: 83.3 us -> 80.1 us  [call(): pl.pallas_call(kernel, grid_spec=pltpu.PrefetchScalarGridSpec(num_scalar_...]
where the time goes in v2:
time: 358 us; the launch traced here: 357 us
  waiting for transfers between devices  134 us (37%)
  starting transfers between devices  120 us (34%)
  Pallas kernels  80.1 us (22%)
  local copies, waits for them, and re-layouts  15.4 us (4%)
  other arithmetic  5.69 us (2%)
    ppermute x56, waiting for transfers between devices, swap(): return lax.ppermute(values, axis, [(i, i ^ step) for i in range(count)])  120 us
    ppermute x56, starting transfers between devices, swap(): return lax.ppermute(values, axis, [(i, i ^ step) for i in range(count)])  108 us
    pallas_call x15, Pallas kernels, call(): pl.pallas_call(kernel, grid_spec=pltpu.PrefetchScalarGridSpec(num_scalar_...  80.1 us
    unnamed x104, local copies, waits for them, and re-layouts  9.98 us
  transfers between devices with their start and end apart: 59, of which 21 were waited for; matrix products, arithmetic and copies ran while one was open for 5% of the time, Pallas kernels for 17%

profile of v2, /device:TPU:0, one launch (start us, length us, event | category | flops | bytes accessed | tf_op | source)
XLA Modules:
  0.0 357.0 jit_solution(6975593016001017489)
XLA Ops:
  0.6 3.0 collective-permute-start.29
  3.7 45.8 %collective-permute-done.29.refs_2_ = bf16[4096,256]{1,0:T(8,128)(2,1)S(1)} collective-permute-done((bf16[4096,256]{1,0:T(8,128)(2,1)}, bf16[4096,256]{1,0:T(8,128)(2,1)S(1)}, u32[]{:S(2)}, u32[]{:S(2)}) %collective-permute-start.29) | collective-permute-done | bytes 2097184 | tf_op jit(solution)/shard_map/ppermute | solution.py:24
  50.2 3.4 shard_map.112
  57.1 2.6 collective-permute-done.14.refs_1_.refs_17_
  59.7 2.9 collective-permute-start.17
  64.3 3.4 shard_map.109
  67.7 3.3 collective-permute-start.19
  71.0 3.6 %collective-permute-done.17.refs_4_.refs_20_ = bf16[4,8,16,128]{3,2,1,0:T(8,128)(2,1)S(1)} collective-permute-done((bf16[4,8,16,128]{3,2,1,0:T(8,128)(2,1)}, bf16[4,8,16,128]{3,2,1,0:T(8,128)(2,1)S(1)}, u32[]{:S(2)}, u32[]{:S(2)}) %collective-permute-start.17) | collective-permute-done | bytes 131104 | tf_op jit(solution)/shard_map/ppermute | solution.py:24
  74.7 4.4 %collective-permute-start.20 = (bf16[4,8,16,128]{3,2,1,0:T(8,128)(2,1)S(1)}, bf16[4,8,16,128]{3,2,1,0:T(8,128)(2,1)S(1)}, u32[]{:S(2)}, u32[]{:S(2)}) collective-permute-start(bf16[4,8,16,128]{3,2,1,0:T(8,128)(2,1)S(1)} %copy-done.48), channel_id=1, source_target_pairs={{0,28},{4,24},{8,20},{12,16},{16,12},{20,8},{24,4},{28,0},{1,29},{... | collective-permute-start | bytes 393224 | tf_op jit(solution)/shard_map/ppermute | solution.py:24
  80.4 4.0 %collective-permute-start.1 = (bf16[4,8,16,128]{3,2,1,0:T(8,128)(2,1)}, bf16[4,8,16,128]{3,2,1,0:T(8,128)(2,1)S(1)}, u32[]{:S(2)}, u32[]{:S(2)}) collective-permute-start(bf16[4,8,16,128]{3,2,1,0:T(8,128)(2,1)} %get-tuple-element.66), channel_id=1, source_target_pairs={{0,8},{4,12},{8,0},{12,4},{16,24},{20,28},{24,16},{28,20},{1,9},{5... | collective-permute-start | bytes 393224 | tf_op jit(solution)/shard_map/ppermute | solution.py:24
  84.3 3.1 collective-permute-start.2
  89.4 2.7 collective-permute-start.4
  95.0 8.4 %collective-permute-done.3.refs_4_.refs_12_ = bf16[4,8,16,128]{3,2,1,0:T(8,128)(2,1)S(1)} collective-permute-done((bf16[4,8,16,128]{3,2,1,0:T(8,128)(2,1)}, bf16[4,8,16,128]{3,2,1,0:T(8,128)(2,1)S(1)}, u32[]{:S(2)}, u32[]{:S(2)}) %collective-permute-start.3) | collective-permute-done | bytes 131104 | tf_op jit(solution)/shard_map/ppermute | solution.py:24
  103.3 3.1 collective-permute-start.6
  110.7 3.0 shard_map.110
  113.7 4.5 %shard_map.113 = (bf16[32,8,16,128]{3,2,1,0:T(8,128)(2,1)}, bf16[4,8,16,128]{3,2,1,0:T(8,128)(2,1)}, bf16[4,8,16,128]{3,2,1,0:T(8,128)(2,1)}, bf16[4,8,16,128]{3...) custom-call(s32[2]{0:T(128)} %pad_add_fusion.index, ...), custom_call_target="tpu_custom_call" | custom-call | flops 402653184 | bytes 3702784 | tf_op jit(solution)/shard_map/pallas_call | solution.py:44
  121.8 3.1 collective-permute-done.21.refs_9_
  124.9 2.9 collective-permute-start.25
  129.4 4.5 %shard_map.111 = (bf16[32,8,16,128]{3,2,1,0:T(8,128)(2,1)}, bf16[4,8,16,128]{3,2,1,0:T(8,128)(2,1)}, bf16[4,8,16,128]{3,2,1,0:T(8,128)(2,1)}, bf16[4,8,16,128]{3...) custom-call(s32[2]{0:T(128)} %pad_add_fusion.index, ...), custom_call_target="tpu_custom_call" | custom-call | flops 402653184 | bytes 3702784 | tf_op jit(solution)/shard_map/pallas_call | solution.py:44
  134.0 5.2 %collective-permute-done.24.refs_12_ = bf16[4,8,16,128]{3,2,1,0:T(8,128)(2,1)S(1)} collective-permute-done((bf16[4,8,16,128]{3,2,1,0:T(8,128)(2,1)}, bf16[4,8,16,128]{3,2,1,0:T(8,128)(2,1)S(1)}, u32[]{:S(2)}, u32[]{:S(2)}) %collective-permute-start.24) | collective-permute-done | bytes 131104 | tf_op jit(solution)/shard_map/ppermute | solution.py:24
  142.0 10.5 %collective-permute-start.11 = (bf16[4,8,16,128]{3,2,1,0:T(8,128)(2,1)}, bf16[4,8,16,128]{3,2,1,0:T(8,128)(2,1)S(1)}, u32[]{:S(2)}, u32[]{:S(2)}) collective-permute-start(bf16[4,8,16,128]{3,2,1,0:T(8,128)(2,1)} %get-tuple-element.79), channel_id=1, source_target_pairs={{0,20},{4,16},{8,28},{12,24},{16,4},{20,0},{24,12},{28,8},{1,21},{... | collective-permute-start | bytes 393224 | tf_op jit(solution)/shard_map/ppermute | solution.py:24
  153.1 4.3 %collective-permute-done.10.refs_4_ = bf16[4,8,16,128]{3,2,1,0:T(8,128)(2,1)S(1)} collective-permute-done((bf16[4,8,16,128]{3,2,1,0:T(8,128)(2,1)}, bf16[4,8,16,128]{3,2,1,0:T(8,128)(2,1)S(1)}, u32[]{:S(2)}, u32[]{:S(2)}) %collective-permute-start.10) | collective-permute-done | bytes 131104 | tf_op jit(solution)/shard_map/ppermute | solution.py:24
  157.4 5.8 %collective-permute-start.13 = (bf16[4,8,16,128]{3,2,1,0:T(8,128)(2,1)}, bf16[4,8,16,128]{3,2,1,0:T(8,128)(2,1)S(1)}, u32[]{:S(2)}, u32[]{:S(2)}) collective-permute-start(bf16[4,8,16,128]{3,2,1,0:T(8,128)(2,1)} %get-tuple-element.81), channel_id=1, source_target_pairs={{0,28},{4,24},{8,20},{12,16},{16,12},{20,8},{24,4},{28,0},{1,29},{... | collective-permute-start | bytes 393224 | tf_op jit(solution)/shard_map/ppermute | solution.py:24
  166.7 9.2 %shard_map.114 = (f32[4096,256]{1,0:T(8,128)}, bf16[4,8,16,256]{3,2,1,0:T(8,128)(2,1)}, bf16[4,8,16,256]{3,2,1,0:T(8,128)(2,1)}, bf16[4,8,16,256]{3,2,1,0:T(8,12...) custom-call(s32[2]{0:T(128)} %pad_add_fusion.index, ...), custom_call_target="tpu_custom_call" | custom-call | flops 2147483648 | bytes 17301504 | tf_op jit(solution)/shard_map/pallas_call | solution.py:44
  176.8 7.7 %shard_map.115 = (bf16[4096,256]{1,0:T(8,128)(2,1)}, bf16[4096,256]{1,0:T(8,128)(2,1)}) custom-call(s32[2]{0:T(128)} %pad_add_fusion.index, bf16[4,8,16,128]{3,2,1,0:T(8,128)(2,1)} %get-tuple-element.74.refs_0_, bf16[4,8,16,128]{3,2,1,0:T(8,128)(2,1)} %copy-done.39, bf16[4,8,16,128]{3,2,1,0:T(8,128)(2,1)} %copy-done.40, bf16[4,8,16,128]{3,2,1,0:T(8,128)(2,1)} %copy-done.41, ...), custom_call_target="tpu_custom_call" | custom-call | flops 16777216 | bytes 14680064 | tf_op jit(solution)/shard_map/pallas_call | solution.py:44
  190.8 7.1 %shard_map.123 = f32[1024,256]{1,0:T(8,128)} custom-call(s32[2]{0:T(128)} %pad_add_fusion.index, bf16[4096,256]{1,0:T(8,128)(2,1)} %refs_0_.3, bf16[4096,256]{1,0:T(8,128)(2,1)} %collective-permute-done.28.refs_1_, bf16[4096,256]{1,0:T(8,128)(2,1)} %copy-done.1, bf16[4096,256]{1,0:T(8,128)(2,1)} %collective-permute-done.30.refs_3_, ...), custom_call_target="tpu_custom_call" | custom-call | flops 2147483648 | bytes 11534336 | tf_op jit(solution)/shard_map/pallas_call | solution.py:44
  197.9 2.6 collective-permute-start.35
  205.7 12.7 %collective-permute-done.34.refs_4_ = bf16[4,8,16,256]{3,2,1,0:T(8,128)(2,1)S(1)} collective-permute-done((bf16[4,8,16,256]{3,2,1,0:T(8,128)(2,1)S(1)}, bf16[4,8,16,256]{3,2,1,0:T(8,128)(2,1)S(1)}, u32[]{:S(2)}, u32[]{:S(2)}) %collective-permute-start.34) | collective-permute-done | bytes 262176 | tf_op jit(solution)/shard_map/ppermute | solution.py:24
  220.5 3.0 shard_map.116
  226.9 5.6 %shard_map.117 = (bf16[32,8,16,256]{3,2,1,0:T(8,128)(2,1)}, bf16[4,8,16,256]{3,2,1,0:T(8,128)(2,1)}, bf16[4,8,16,256]{3,2,1,0:T(8,128)(2,1)}, bf16[4,8,16,256]{3...) custom-call(s32[2]{0:T(128)} %pad_add_fusion.index, ...), custom_call_target="tpu_custom_call" | custom-call | flops 805306368 | bytes 6848512 | tf_op jit(solution)/shard_map/pallas_call | solution.py:44
  234.0 7.9 %shard_map.122 = f32[80,128]{1,0:T(8,128)} custom-call(s32[2]{0:T(128)} %pad_add_fusion.index, bf16[4,8,16,256]{3,2,1,0:T(8,128)(2,1)} %get-tuple-element.100.refs_0_, bf16[4,8,16,256]{3,2,1,0:T(8,128)(2,1)} %copy-done.21, bf16[4,8,16,256]{3,2,1,0:T(8,128)(2,1)} %copy-done.22, bf16[4,8,16,256]{3,2,1,0:T(8,128)(2,1)} %copy-done.23, ...), custom_call_target="tpu_custom_call" | custom-call | flops 1342177280 | bytes 8429568 | tf_op jit(solution)/shard_map/pallas_call | solution.py:44
  243.4 2.7 collective-permute-done.51
  246.1 7.8 %collective-permute-start.39 = (bf16[4,8,16,256]{3,2,1,0:T(8,128)(2,1)}, bf16[4,8,16,256]{3,2,1,0:T(8,128)(2,1)}, u32[]{:S(2)}, u32[]{:S(2)}) collective-permute-start(bf16[4,8,16,256]{3,2,1,0:T(8,128)(2,1)} %get-tuple-element.112), channel_id=1, source_target_pairs={{0,8},{4,12},{8,0},{12,4},{16,24},{20,28},{24,16},{28,20},{1,9},{5... | collective-permute-start | bytes 786440 | tf_op jit(solution)/shard_map/ppermute | solution.py:24
  258.0 9.6 %collective-permute-done.39.refs_2_ = bf16[4,8,16,256]{3,2,1,0:T(8,128)(2,1)} collective-permute-done((bf16[4,8,16,256]{3,2,1,0:T(8,128)(2,1)}, bf16[4,8,16,256]{3,2,1,0:T(8,128)(2,1)}, u32[]{:S(2)}, u32[]{:S(2)}) %collective-permute-start.39) | collective-permute-done | bytes 262176 | tf_op jit(solution)/shard_map/ppermute | solution.py:24
  267.5 3.1 collective-permute-done.40.refs_3_
  271.8 14.3 %collective-permute-done.41.refs_4_.refs_0_ = bf16[4,8,16,256]{3,2,1,0:T(8,128)(2,1)} collective-permute-done((bf16[4,8,16,256]{3,2,1,0:T(8,128)(2,1)}, bf16[4,8,16,256]{3,2,1,0:T(8,128)(2,1)}, u32[]{:S(2)}, u32[]{:S(2)}) %collective-permute-start.41) | collective-permute-done | bytes 262176 | tf_op jit(solution)/shard_map/ppermute | solution.py:24
  286.1 3.6 %collective-permute-start.44 = (bf16[4,8,16,256]{3,2,1,0:T(8,128)(2,1)}, bf16[4,8,16,256]{3,2,1,0:T(8,128)(2,1)S(1)}, u32[]{:S(2)}, u32[]{:S(2)}) collective-permute-start(bf16[4,8,16,256]{3,2,1,0:T(8,128)(2,1)} %get-tuple-element.117), channel_id=1, source_target_pairs={{0,28},{4,24},{8,20},{12,16},{16,12},{20,8},{24,4},{28,0},{1,29},{... | collective-permute-start | bytes 786440 | tf_op jit(solution)/shard_map/ppermute | solution.py:24
  291.6 3.9 %shard_map.120.refs_5_ = bf16[16,16,128]{2,1,0:T(8,128)(2,1)} custom-call(s32[2]{0:T(128)} %pad_add_fusion.index, bf16[4,8,16,256]{3,2,1,0:T(8,128)(2,1)} %get-tuple-element.110.refs_0_, bf16[4,8,16,256]{3,2,1,0:T(8,128)(2,1)} %copy-done.6, bf16[4,8,16,256]{3,2,1,0:T(8,128)(2,1)} %collective-permute-done.39.refs_2_, ...), custom_call_target="tpu_custom_call" | custom-call | flops 67108864 | bytes 3211264 | tf_op jit(solution)/shard_map/pallas_call | solution.py:44
  298.4 3.9 %shard_map.121 = bf16[32,16,128]{2,1,0:T(8,128)(2,1)} custom-call(s32[2]{0:T(128)} %pad_add_fusion.index, bf16[4,8,16,256]{3,2,1,0:T(8,128)(2,1)} %collective-permute-done.41.refs_4_.refs_0_, bf16[4,8,16,256]{3,2,1,0:T(8,128)(2,1)} %copy-done.7, bf16[4,8,16,256]{3,2,1,0:T(8,128)(2,1)} %copy-done.8, bf16[4,8,16,256]{3,2,1,0:T(8,128)(2,1)} %copy-done.9, ...), custom_call_target="tpu_custom_call" | custom-call | flops 67108864 | bytes 3342336 | tf_op jit(solution)/shard_map/pallas_call | solution.py:44
  302.3 5.8 %all-to-all-start = ((bf16[32,16,128]{2,1,0:T(8,128)(2,1)}), bf16[32,16,128]{2,1,0:T(8,128)(2,1)S(1)}, u32[]{:S(2)}, u32[]{:S(2)}) async-start(bf16[32,16,128]{2,1,0:T(8,128)(2,1)} %shard_map.121), calls=%async_computation | async-start | bytes 262144 | tf_op jit(solution)/shard_map/all_to_all | solution.py:492
  311.6 4.7 %all-to-all-done = bf16[32,16,128]{2,1,0:T(8,128)(2,1)S(1)} async-done(((bf16[32,16,128]{2,1,0:T(8,128)(2,1)}), bf16[32,16,128]{2,1,0:T(8,128)(2,1)S(1)}, u32[]{:S(2)}, u32[]{:S(2)}) %all-to-all-start) | async-done | bytes 131104 | tf_op jit(solution)/shard_map/all_to_all | solution.py:492
  317.0 3.4 all-to-all-start.2
  322.1 2.8 collective-permute-start.55
  325.0 5.9 %all-to-all-done.2 = bf16[8,80,128]{2,1,0:T(8,128)(2,1)S(1)} async-done(((bf16[8,80,128]{2,1,0:T(8,128)(2,1)}), bf16[8,80,128]{2,1,0:T(8,128)(2,1)S(1)}, u32[]{:S(2)}, u32[]{:S(2)}) %all-to-all-start.2) | async-done | bytes 163872 | tf_op jit(solution)/shard_map/all_to_all | solution.py:470
  331.5 2.8 all-to-all-start.1
  338.7 3.6 %all-to-all-done.1 = bf16[32,16,128]{2,1,0:T(8,128)(2,1)S(1)} async-done(((bf16[32,16,128]{2,1,0:T(8,128)(2,1)}), bf16[32,16,128]{2,1,0:T(8,128)(2,1)S(1)}, u32[]{:S(2)}, u32[]{:S(2)}) %all-to-all-start.1) | async-done | bytes 131104 | tf_op jit(solution)/shard_map/all_to_all | solution.py:494
  343.9 7.8 %shard_map.118.refs_9_ = f32[4096,256]{1,0:T(8,128)} custom-call(s32[2]{0:T(128)} %pad_add_fusion.index, bf16[4096,256]{1,0:T(8,128)(2,1)} %get-tuple-element.118.refs_0_.refs_4_, bf16[4096,256]{1,0:T(8,128)(2,1)} %collective-permute-done.45.refs_1_, bf16[4096,256]{1,0:T(8,128)(2,1)} %collective-permute-done.46.refs_2_, ...), custom_call_target="tpu_custom_call" | custom-call | flops 2147483648 | bytes 15204352 | tf_op jit(solution)/shard_map/pallas_call | solution.py:44
  351.8 5.3 %shard_map.119 = bf16[4096,256]{1,0:T(8,128)(2,1)} custom-call(s32[2]{0:T(128)} %pad_add_fusion.index, bf16[4,8,16,256]{3,2,1,0:T(8,128)(2,1)} %get-tuple-element.110.refs_0_, bf16[4,8,16,256]{3,2,1,0:T(8,128)(2,1)} %copy-done.6, bf16[4,8,16,256]{3,2,1,0:T(8,128)(2,1)} %collective-permute-done.39.refs_2_, ...), custom_call_target="tpu_custom_call" | custom-call | flops 134217728 | bytes 8519680 | tf_op jit(solution)/shard_map/pallas_call | solution.py:44
  (210 shorter events, 71.6 us)
Async XLA Ops:
  0.6 48.9 %collective-permute-start.29 = (bf16[4096,256]{1,0:T(8,128)(2,1)}, bf16[4096,256]{1,0:T(8,128)(2,1)S(1)}, u32[]{:S(2)}, u32[]{:S(2)}) collective-permute-start(bf16[4096,256]{1,0:T(8,128)(2,1)} %refs_0_.3), channel_id=1, source_target_pairs={{0,2},{1,3},{2,0},{3,1},{4,6},{5,7},{6,4},{7,5},{8,10},{9,11},{10,... | collective-permute-start | bytes 6291464 | tf_op jit(solution)/shard_map/ppermute | solution.py:24
  3.7 160.9 %collective-permute-start.28 = (bf16[4096,256]{1,0:T(8,128)(2,1)}, bf16[4096,256]{1,0:T(8,128)(2,1)}, u32[]{:S(2)}, u32[]{:S(2)}) collective-permute-start(bf16[4096,256]{1,0:T(8,128)(2,1)} %refs_0_.3), channel_id=1, source_target_pairs={{0,1},{1,0},{2,3},{3,2},{4,5},{5,4},{6,7},{7,6},{8,9},{9,8},{10,11... | collective-permute-start | bytes 6291464 | tf_op jit(solution)/shard_map/ppermute | solution.py:24
  49.5 115.0 %collective-permute-start.30 = (bf16[4096,256]{1,0:T(8,128)(2,1)S(1)}, bf16[4096,256]{1,0:T(8,128)(2,1)}, u32[]{:S(2)}, u32[]{:S(2)}) collective-permute-start(bf16[4096,256]{1,0:T(8,128)(2,1)S(1)} %collective-permute-done.29.refs_2_), channel_id=1, source_target_pairs={{0,1},{1,0},{2,3},{3,2},{4,5},{5,4},{6,7},{7,6},{8,9},{9,8},{10,11... | collective-permute-start | bytes 6291464 | tf_op jit(solution)/shard_map/ppermute | solution.py:24
  57.0 10.7 %collective-permute-start.16 = (bf16[4,8,16,128]{3,2,1,0:T(8,128)(2,1)}, bf16[4,8,16,128]{3,2,1,0:T(8,128)(2,1)S(1)}, u32[]{:S(2)}, u32[]{:S(2)}) collective-permute-start(bf16[4,8,16,128]{3,2,1,0:T(8,128)(2,1)} %get-tuple-element.85), channel_id=1, source_target_pairs={{0,12},{4,8},{8,4},{12,0},{16,28},{20,24},{24,20},{28,16},{1,13},{... | collective-permute-start | bytes 393224 | tf_op jit(solution)/shard_map/ppermute | solution.py:24
  59.7 14.9 %collective-permute-start.17 = (bf16[4,8,16,128]{3,2,1,0:T(8,128)(2,1)}, bf16[4,8,16,128]{3,2,1,0:T(8,128)(2,1)S(1)}, u32[]{:S(2)}, u32[]{:S(2)}) collective-permute-start(bf16[4,8,16,128]{3,2,1,0:T(8,128)(2,1)} %get-tuple-element.86), channel_id=1, source_target_pairs={{0,16},{4,20},{8,24},{12,28},{16,0},{20,4},{24,8},{28,12},{1,17},{... | collective-permute-start | bytes 393224 | tf_op jit(solution)/shard_map/ppermute | solution.py:24
  62.6 16.7 %collective-permute-start.18 = (bf16[4,8,16,128]{3,2,1,0:T(8,128)(2,1)}, bf16[4,8,16,128]{3,2,1,0:T(8,128)(2,1)S(1)}, u32[]{:S(2)}, u32[]{:S(2)}) collective-permute-start(bf16[4,8,16,128]{3,2,1,0:T(8,128)(2,1)} %get-tuple-element.87), channel_id=1, source_target_pairs={{0,20},{4,16},{8,28},{12,24},{16,4},{20,0},{24,12},{28,8},{1,21},{... | collective-permute-start | bytes 393224 | tf_op jit(solution)/shard_map/ppermute | solution.py:24
  67.7 12.6 %collective-permute-start.19 = (bf16[4,8,16,128]{3,2,1,0:T(8,128)(2,1)S(1)}, bf16[4,8,16,128]{3,2,1,0:T(8,128)(2,1)S(1)}, u32[]{:S(2)}, u32[]{:S(2)}) collective-permute-start(bf16[4,8,16,128]{3,2,1,0:T(8,128)(2,1)S(1)} %copy-done.49), channel_id=1, source_target_pairs={{0,24},{4,28},{8,16},{12,20},{16,8},{20,12},{24,0},{28,4},{1,25},{... | collective-permute-start | bytes 393224 | tf_op jit(solution)/shard_map/ppermute | solution.py:24
  87.4 15.9 %collective-permute-start.3 = (bf16[4,8,16,128]{3,2,1,0:T(8,128)(2,1)}, bf16[4,8,16,128]{3,2,1,0:T(8,128)(2,1)S(1)}, u32[]{:S(2)}, u32[]{:S(2)}) collective-permute-start(bf16[4,8,16,128]{3,2,1,0:T(8,128)(2,1)} %get-tuple-element.68), channel_id=1, source_target_pairs={{0,16},{4,20},{8,24},{12,28},{16,0},{20,4},{24,8},{28,12},{1,17},{... | collective-permute-start | bytes 393224 | tf_op jit(solution)/shard_map/ppermute | solution.py:24
  89.4 28.8 %collective-permute-start.4 = (bf16[4,8,16,128]{3,2,1,0:T(8,128)(2,1)}, bf16[4,8,16,128]{3,2,1,0:T(8,128)(2,1)}, u32[]{:S(2)}, u32[]{:S(2)}) collective-permute-start(bf16[4,8,16,128]{3,2,1,0:T(8,128)(2,1)} %get-tuple-element.69), channel_id=1, source_target_pairs={{0,20},{4,16},{8,28},{12,24},{16,4},{20,0},{24,12},{28,8},{1,21},{... | collective-permute-start | bytes 393224 | tf_op jit(solution)/shard_map/ppermute | solution.py:24
  92.9 26.4 %collective-permute-start.5 = (bf16[4,8,16,128]{3,2,1,0:T(8,128)(2,1)}, bf16[4,8,16,128]{3,2,1,0:T(8,128)(2,1)}, u32[]{:S(2)}, u32[]{:S(2)}) collective-permute-start(bf16[4,8,16,128]{3,2,1,0:T(8,128)(2,1)} %get-tuple-element.70), channel_id=1, source_target_pairs={{0,24},{4,28},{8,16},{12,20},{16,8},{20,12},{24,0},{28,4},{1,25},{... | collective-permute-start | bytes 393224 | tf_op jit(solution)/shard_map/ppermute | solution.py:24
  103.3 16.0 %collective-permute-start.6 = (bf16[4,8,16,128]{3,2,1,0:T(8,128)(2,1)}, bf16[4,8,16,128]{3,2,1,0:T(8,128)(2,1)}, u32[]{:S(2)}, u32[]{:S(2)}) collective-permute-start(bf16[4,8,16,128]{3,2,1,0:T(8,128)(2,1)} %get-tuple-element.71), channel_id=1, source_target_pairs={{0,28},{4,24},{8,20},{12,16},{16,12},{20,8},{24,4},{28,0},{1,29},{... | collective-permute-start | bytes 393224 | tf_op jit(solution)/shard_map/ppermute | solution.py:24
  124.9 14.3 %collective-permute-start.24 = (bf16[4,8,16,128]{3,2,1,0:T(8,128)(2,1)}, bf16[4,8,16,128]{3,2,1,0:T(8,128)(2,1)S(1)}, u32[]{:S(2)}, u32[]{:S(2)}) collective-permute-start(bf16[4,8,16,128]{3,2,1,0:T(8,128)(2,1)} %get-tuple-element.94), channel_id=1, source_target_pairs={{0,16},{4,20},{8,24},{12,28},{16,0},{20,4},{24,8},{28,12},{1,17},{... | collective-permute-start | bytes 393224 | tf_op jit(solution)/shard_map/ppermute | solution.py:24
  124.9 17.1 %collective-permute-start.25 = (bf16[4,8,16,128]{3,2,1,0:T(8,128)(2,1)}, bf16[4,8,16,128]{3,2,1,0:T(8,128)(2,1)S(1)}, u32[]{:S(2)}, u32[]{:S(2)}) collective-permute-start(bf16[4,8,16,128]{3,2,1,0:T(8,128)(2,1)} %get-tuple-element.95), channel_id=1, source_target_pairs={{0,20},{4,16},{8,28},{12,24},{16,4},{20,0},{24,12},{28,8},{1,21},{... | collective-permute-start | bytes 393224 | tf_op jit(solution)/shard_map/ppermute | solution.py:24
  128.0 14.0 %collective-permute-start.26 = (bf16[4,8,16,128]{3,2,1,0:T(8,128)(2,1)}, bf16[4,8,16,128]{3,2,1,0:T(8,128)(2,1)S(1)}, u32[]{:S(2)}, u32[]{:S(2)}) collective-permute-start(bf16[4,8,16,128]{3,2,1,0:T(8,128)(2,1)} %get-tuple-element.96), channel_id=1, source_target_pairs={{0,24},{4,28},{8,16},{12,20},{16,8},{20,12},{24,0},{28,4},{1,25},{... | collective-permute-start | bytes 393224 | tf_op jit(solution)/shard_map/ppermute | solution.py:24
  139.2 13.4 %collective-permute-start.27 = (bf16[4,8,16,128]{3,2,1,0:T(8,128)(2,1)}, bf16[4,8,16,128]{3,2,1,0:T(8,128)(2,1)S(1)}, u32[]{:S(2)}, u32[]{:S(2)}) collective-permute-start(bf16[4,8,16,128]{3,2,1,0:T(8,128)(2,1)} %get-tuple-element.97), channel_id=1, source_target_pairs={{0,28},{4,24},{8,20},{12,16},{16,12},{20,8},{24,4},{28,0},{1,29},{... | collective-permute-start | bytes 393224 | tf_op jit(solution)/shard_map/ppermute | solution.py:24
  142.0 15.4 %collective-permute-start.10 = (bf16[4,8,16,128]{3,2,1,0:T(8,128)(2,1)}, bf16[4,8,16,128]{3,2,1,0:T(8,128)(2,1)S(1)}, u32[]{:S(2)}, u32[]{:S(2)}) collective-permute-start(bf16[4,8,16,128]{3,2,1,0:T(8,128)(2,1)} %get-tuple-element.78), channel_id=1, source_target_pairs={{0,16},{4,20},{8,24},{12,28},{16,0},{20,4},{24,8},{28,12},{1,17},{... | collective-permute-start | bytes 393224 | tf_op jit(solution)/shard_map/ppermute | solution.py:24
  142.0 21.2 %collective-permute-start.11 = (bf16[4,8,16,128]{3,2,1,0:T(8,128)(2,1)}, bf16[4,8,16,128]{3,2,1,0:T(8,128)(2,1)S(1)}, u32[]{:S(2)}, u32[]{:S(2)}) collective-permute-start(bf16[4,8,16,128]{3,2,1,0:T(8,128)(2,1)} %get-tuple-element.79), channel_id=1, source_target_pairs={{0,20},{4,16},{8,28},{12,24},{16,4},{20,0},{24,12},{28,8},{1,21},{... | collective-permute-start | bytes 393224 | tf_op jit(solution)/shard_map/ppermute | solution.py:24
  152.6 23.4 %collective-permute-start.12 = (bf16[4,8,16,128]{3,2,1,0:T(8,128)(2,1)}, bf16[4,8,16,128]{3,2,1,0:T(8,128)(2,1)S(1)}, u32[]{:S(2)}, u32[]{:S(2)}) collective-permute-start(bf16[4,8,16,128]{3,2,1,0:T(8,128)(2,1)} %get-tuple-element.80), channel_id=1, source_target_pairs={{0,24},{4,28},{8,16},{12,20},{16,8},{20,12},{24,0},{28,4},{1,25},{... | collective-permute-start | bytes 393224 | tf_op jit(solution)/shard_map/ppermute | solution.py:24
  157.4 18.6 %collective-permute-start.13 = (bf16[4,8,16,128]{3,2,1,0:T(8,128)(2,1)}, bf16[4,8,16,128]{3,2,1,0:T(8,128)(2,1)S(1)}, u32[]{:S(2)}, u32[]{:S(2)}) collective-permute-start(bf16[4,8,16,128]{3,2,1,0:T(8,128)(2,1)} %get-tuple-element.81), channel_id=1, source_target_pairs={{0,28},{4,24},{8,20},{12,16},{16,12},{20,8},{24,4},{28,0},{1,29},{... | collective-permute-start | bytes 393224 | tf_op jit(solution)/shard_map/ppermute | solution.py:24
  163.2 12.8 %collective-permute-start.7 = (bf16[4,8,16,128]{3,2,1,0:T(8,128)(2,1)}, bf16[4,8,16,128]{3,2,1,0:T(8,128)(2,1)S(1)}, u32[]{:S(2)}, u32[]{:S(2)}) collective-permute-start(bf16[4,8,16,128]{3,2,1,0:T(8,128)(2,1)} %get-tuple-element.75), channel_id=1, source_target_pairs={{0,4},{4,0},{8,12},{12,8},{16,20},{20,16},{24,28},{28,24},{1,5},{5... | collective-permute-start | bytes 393224 | tf_op jit(solution)/shard_map/ppermute | solution.py:24
  164.5 11.5 %collective-permute-start.8 = (bf16[4,8,16,128]{3,2,1,0:T(8,128)(2,1)}, bf16[4,8,16,128]{3,2,1,0:T(8,128)(2,1)S(1)}, u32[]{:S(2)}, u32[]{:S(2)}) collective-permute-start(bf16[4,8,16,128]{3,2,1,0:T(8,128)(2,1)} %get-tuple-element.76), channel_id=1, source_target_pairs={{0,8},{4,12},{8,0},{12,4},{16,24},{20,28},{24,16},{28,20},{1,9},{5... | collective-permute-start | bytes 393224 | tf_op jit(solution)/shard_map/ppermute | solution.py:24
  164.5 11.5 %collective-permute-start.9 = (bf16[4,8,16,128]{3,2,1,0:T(8,128)(2,1)}, bf16[4,8,16,128]{3,2,1,0:T(8,128)(2,1)S(1)}, u32[]{:S(2)}, u32[]{:S(2)}) collective-permute-start(bf16[4,8,16,128]{3,2,1,0:T(8,128)(2,1)} %get-tuple-element.77), channel_id=1, source_target_pairs={{0,12},{4,8},{8,4},{12,0},{16,28},{20,24},{24,20},{28,16},{1,13},{... | collective-permute-start | bytes 393224 | tf_op jit(solution)/shard_map/ppermute | solution.py:24
  184.5 41.4 %collective-permute-start.46 = (bf16[4096,256]{1,0:T(8,128)(2,1)}, bf16[4096,256]{1,0:T(8,128)(2,1)}, u32[]{:S(2)}, u32[]{:S(2)}) collective-permute-start(bf16[4096,256]{1,0:T(8,128)(2,1)} %get-tuple-element.118.refs_0_.refs_4_), channel_id=1, source_target_pairs={{0,2},{1,3},{2,0},{3,1},{4,6},{5,7},{6,4},{7,5},{8,10},{9,11},{10,... | collective-permute-start | bytes 6291464 | tf_op jit(solution)/shard_map/ppermute | solution.py:24
  186.1 11.8 %collective-permute-start.31 = (bf16[4,8,16,256]{3,2,1,0:T(8,128)(2,1)}, bf16[4,8,16,256]{3,2,1,0:T(8,128)(2,1)S(1)}, u32[]{:S(2)}, u32[]{:S(2)}) collective-permute-start(bf16[4,8,16,256]{3,2,1,0:T(8,128)(2,1)} %get-tuple-element.101), channel_id=1, source_target_pairs={{0,4},{4,0},{8,12},{12,8},{16,20},{20,16},{24,28},{28,24},{1,5},{5... | collective-permute-start | bytes 786440 | tf_op jit(solution)/shard_map/ppermute | solution.py:24
  187.3 13.2 %collective-permute-start.32 = (bf16[4,8,16,256]{3,2,1,0:T(8,128)(2,1)}, bf16[4,8,16,256]{3,2,1,0:T(8,128)(2,1)S(1)}, u32[]{:S(2)}, u32[]{:S(2)}) collective-permute-start(bf16[4,8,16,256]{3,2,1,0:T(8,128)(2,1)} %get-tuple-element.102), channel_id=1, source_target_pairs={{0,8},{4,12},{8,0},{12,4},{16,24},{20,28},{24,16},{28,20},{1,9},{5... | collective-permute-start | bytes 786440 | tf_op jit(solution)/shard_map/ppermute | solution.py:24
  187.4 15.7 %collective-permute-start.33 = (bf16[4,8,16,256]{3,2,1,0:T(8,128)(2,1)S(1)}, bf16[4,8,16,256]{3,2,1,0:T(8,128)(2,1)S(1)}, u32[]{:S(2)}, u32[]{:S(2)}) collective-permute-start(bf16[4,8,16,256]{3,2,1,0:T(8,128)(2,1)S(1)} %copy-done.47), channel_id=1, source_target_pairs={{0,12},{4,8},{8,4},{12,0},{16,28},{20,24},{24,20},{28,16},{1,13},{... | collective-permute-start | bytes 786440 | tf_op jit(solution)/shard_map/ppermute | solution.py:24
  189.6 28.8 %collective-permute-start.34 = (bf16[4,8,16,256]{3,2,1,0:T(8,128)(2,1)S(1)}, bf16[4,8,16,256]{3,2,1,0:T(8,128)(2,1)S(1)}, u32[]{:S(2)}, u32[]{:S(2)}) collective-permute-start(bf16[4,8,16,256]{3,2,1,0:T(8,128)(2,1)S(1)} %copy-done.46), channel_id=1, source_target_pairs={{0,16},{4,20},{8,24},{12,28},{16,0},{20,4},{24,8},{28,12},{1,17},{... | collective-permute-start | bytes 786440 | tf_op jit(solution)/shard_map/ppermute | solution.py:24
  197.9 27.6 %collective-permute-start.35 = (bf16[4,8,16,256]{3,2,1,0:T(8,128)(2,1)S(1)}, bf16[4,8,16,256]{3,2,1,0:T(8,128)(2,1)S(1)}, u32[]{:S(2)}, u32[]{:S(2)}) collective-permute-start(bf16[4,8,16,256]{3,2,1,0:T(8,128)(2,1)S(1)} %copy-done.45), channel_id=1, source_target_pairs={{0,20},{4,16},{8,28},{12,24},{16,4},{20,0},{24,12},{28,8},{1,21},{... | collective-permute-start | bytes 786440 | tf_op jit(solution)/shard_map/ppermute | solution.py:24
  200.5 25.6 %collective-permute-start.36 = (bf16[4,8,16,256]{3,2,1,0:T(8,128)(2,1)S(1)}, bf16[4,8,16,256]{3,2,1,0:T(8,128)(2,1)S(1)}, u32[]{:S(2)}, u32[]{:S(2)}) collective-permute-start(bf16[4,8,16,256]{3,2,1,0:T(8,128)(2,1)S(1)} %copy-done.44), channel_id=1, source_target_pairs={{0,24},{4,28},{8,16},{12,20},{16,8},{20,12},{24,0},{28,4},{1,25},{... | collective-permute-start | bytes 786440 | tf_op jit(solution)/shard_map/ppermute | solution.py:24
  203.1 23.0 %collective-permute-start.37 = (bf16[4,8,16,256]{3,2,1,0:T(8,128)(2,1)S(1)}, bf16[4,8,16,256]{3,2,1,0:T(8,128)(2,1)S(1)}, u32[]{:S(2)}, u32[]{:S(2)}) collective-permute-start(bf16[4,8,16,256]{3,2,1,0:T(8,128)(2,1)S(1)} %copy-done.43), channel_id=1, source_target_pairs={{0,28},{4,24},{8,20},{12,16},{16,12},{20,8},{24,4},{28,0},{1,29},{... | collective-permute-start | bytes 786440 | tf_op jit(solution)/shard_map/ppermute | solution.py:24
  218.4 35.5 %collective-permute-start.53 = (f32[4,128,256]{2,1,0:T(8,128)S(1)}, f32[4,128,256]{2,1,0:T(8,128)}, u32[]{:S(2)}, u32[]{:S(2)}) collective-permute-start(f32[4,128,256]{2,1,0:T(8,128)S(1)} %dynamic-slice_bitcast_fusion), channel_id=1, source_target_pairs={{0,4},{4,0},{8,12},{12,8},{16,20},{20,16},{24,28},{28,24},{1,5},{5... | collective-permute-start | bytes 1572872 | tf_op jit(solution)/shard_map/ppermute | solution.py:24
  225.6 117.7 %collective-permute-start.45 = (bf16[4096,256]{1,0:T(8,128)(2,1)S(1)}, bf16[4096,256]{1,0:T(8,128)(2,1)}, u32[]{:S(2)}, u32[]{:S(2)}) collective-permute-start(bf16[4096,256]{1,0:T(8,128)(2,1)S(1)} %copy-done), channel_id=1, source_target_pairs={{0,1},{1,0},{2,3},{3,2},{4,5},{5,4},{6,7},{7,6},{8,9},{9,8},{10,11... | collective-permute-start | bytes 6291464 | tf_op jit(solution)/shard_map/ppermute | solution.py:24
  225.9 117.4 %collective-permute-start.47 = (bf16[4096,256]{1,0:T(8,128)(2,1)}, bf16[4096,256]{1,0:T(8,128)(2,1)}, u32[]{:S(2)}, u32[]{:S(2)}) collective-permute-start(bf16[4096,256]{1,0:T(8,128)(2,1)} %collective-permute-done.46.refs_2_), channel_id=1, source_target_pairs={{0,1},{1,0},{2,3},{3,2},{4,5},{5,4},{6,7},{7,6},{8,9},{9,8},{10,11... | collective-permute-start | bytes 6291464 | tf_op jit(solution)/shard_map/ppermute | solution.py:24
  232.4 22.2 %collective-permute-start.38 = (bf16[4,8,16,256]{3,2,1,0:T(8,128)(2,1)}, bf16[4,8,16,256]{3,2,1,0:T(8,128)(2,1)S(1)}, u32[]{:S(2)}, u32[]{:S(2)}) collective-permute-start(bf16[4,8,16,256]{3,2,1,0:T(8,128)(2,1)} %get-tuple-element.111), channel_id=1, source_target_pairs={{0,4},{4,0},{8,12},{12,8},{16,20},{20,16},{24,28},{28,24},{1,5},{5... | collective-permute-start | bytes 786440 | tf_op jit(solution)/shard_map/ppermute | solution.py:24
  246.1 21.4 %collective-permute-start.39 = (bf16[4,8,16,256]{3,2,1,0:T(8,128)(2,1)}, bf16[4,8,16,256]{3,2,1,0:T(8,128)(2,1)}, u32[]{:S(2)}, u32[]{:S(2)}) collective-permute-start(bf16[4,8,16,256]{3,2,1,0:T(8,128)(2,1)} %get-tuple-element.112), channel_id=1, source_target_pairs={{0,8},{4,12},{8,0},{12,4},{16,24},{20,28},{24,16},{28,20},{1,9},{5... | collective-permute-start | bytes 786440 | tf_op jit(solution)/shard_map/ppermute | solution.py:24
  253.9 16.7 %collective-permute-start.40 = (bf16[4,8,16,256]{3,2,1,0:T(8,128)(2,1)}, bf16[4,8,16,256]{3,2,1,0:T(8,128)(2,1)}, u32[]{:S(2)}, u32[]{:S(2)}) collective-permute-start(bf16[4,8,16,256]{3,2,1,0:T(8,128)(2,1)} %get-tuple-element.113), channel_id=1, source_target_pairs={{0,12},{4,8},{8,4},{12,0},{16,28},{20,24},{24,20},{28,16},{1,13},{... | collective-permute-start | bytes 786440 | tf_op jit(solution)/shard_map/ppermute | solution.py:24
  254.6 31.5 %collective-permute-start.41 = (bf16[4,8,16,256]{3,2,1,0:T(8,128)(2,1)}, bf16[4,8,16,256]{3,2,1,0:T(8,128)(2,1)}, u32[]{:S(2)}, u32[]{:S(2)}) collective-permute-start(bf16[4,8,16,256]{3,2,1,0:T(8,128)(2,1)} %get-tuple-element.114), channel_id=1, source_target_pairs={{0,16},{4,20},{8,24},{12,28},{16,0},{20,4},{24,8},{28,12},{1,17},{... | collective-permute-start | bytes 786440 | tf_op jit(solution)/shard_map/ppermute | solution.py:24
  267.5 27.9 %collective-permute-start.42 = (bf16[4,8,16,256]{3,2,1,0:T(8,128)(2,1)}, bf16[4,8,16,256]{3,2,1,0:T(8,128)(2,1)S(1)}, u32[]{:S(2)}, u32[]{:S(2)}) collective-permute-start(bf16[4,8,16,256]{3,2,1,0:T(8,128)(2,1)} %get-tuple-element.115), channel_id=1, source_target_pairs={{0,20},{4,16},{8,28},{12,24},{16,4},{20,0},{24,12},{28,8},{1,21},{... | collective-permute-start | bytes 786440 | tf_op jit(solution)/shard_map/ppermute | solution.py:24
  270.6 24.9 %collective-permute-start.43 = (bf16[4,8,16,256]{3,2,1,0:T(8,128)(2,1)}, bf16[4,8,16,256]{3,2,1,0:T(8,128)(2,1)S(1)}, u32[]{:S(2)}, u32[]{:S(2)}) collective-permute-start(bf16[4,8,16,256]{3,2,1,0:T(8,128)(2,1)} %get-tuple-element.116), channel_id=1, source_target_pairs={{0,24},{4,28},{8,16},{12,20},{16,8},{20,12},{24,0},{28,4},{1,25},{... | collective-permute-start | bytes 786440 | tf_op jit(solution)/shard_map/ppermute | solution.py:24
  286.1 11.6 %collective-permute-start.44 = (bf16[4,8,16,256]{3,2,1,0:T(8,128)(2,1)}, bf16[4,8,16,256]{3,2,1,0:T(8,128)(2,1)S(1)}, u32[]{:S(2)}, u32[]{:S(2)}) collective-permute-start(bf16[4,8,16,256]{3,2,1,0:T(8,128)(2,1)} %get-tuple-element.117), channel_id=1, source_target_pairs={{0,28},{4,24},{8,20},{12,16},{16,12},{20,8},{24,4},{28,0},{1,29},{... | collective-permute-start | bytes 786440 | tf_op jit(solution)/shard_map/ppermute | solution.py:24
  295.5 13.7 %collective-permute-start.52 = (f32[80,128]{1,0:T(8,128)}, f32[80,128]{1,0:T(8,128)}, u32[]{:S(2)}, u32[]{:S(2)}) collective-permute-start(f32[80,128]{1,0:T(8,128)} %add.68), channel_id=1, source_target_pairs={{0,1},{1,0},{2,3},{3,2},{4,5},{5,4},{6,7},{7,6},{8,9},{9,8},{10,11... | collective-permute-start | bytes 122888 | tf_op jit(solution)/shard_map/ppermute | solution.py:24
  295.6 24.9 %collective-permute-start.54 = (f32[2,128,256]{2,1,0:T(8,128)S(1)}, f32[2,128,256]{2,1,0:T(8,128)}, u32[]{:S(2)}, u32[]{:S(2)}) collective-permute-start(f32[2,128,256]{2,1,0:T(8,128)S(1)} %dynamic-slice_bitcast_fusion.1), channel_id=1, source_target_pairs={{0,8},{4,12},{8,0},{12,4},{16,24},{20,28},{24,16},{28,20},{1,9},{5... | collective-permute-start | bytes 786440 | tf_op jit(solution)/shard_map/ppermute | solution.py:24
  302.3 14.0 %all-to-all-start = ((bf16[32,16,128]{2,1,0:T(8,128)(2,1)}), bf16[32,16,128]{2,1,0:T(8,128)(2,1)S(1)}, u32[]{:S(2)}, u32[]{:S(2)}) async-start(bf16[32,16,128]{2,1,0:T(8,128)(2,1)} %shard_map.121), calls=%async_computation | async-start | bytes 262144 | tf_op jit(solution)/shard_map/all_to_all | solution.py:492
  308.9 34.4 %collective-permute-start.48 = (bf16[256,256]{1,0:T(8,128)(2,1)}, bf16[256,256]{1,0:T(8,128)(2,1)}, u32[]{:S(2)}, u32[]{:S(2)}) collective-permute-start(bf16[256,256]{1,0:T(8,128)(2,1)} %get-tuple-element.135), channel_id=1, source_target_pairs={{0,1},{1,0},{2,3},{3,2},{4,5},{5,4},{6,7},{7,6},{8,9},{9,8},{10,11... | collective-permute-start | bytes 393224 | tf_op jit(solution)/shard_map/ppermute | solution.py:24
  309.2 34.1 %collective-permute-start.49 = (bf16[256,256]{1,0:T(8,128)(2,1)}, bf16[256,256]{1,0:T(8,128)(2,1)}, u32[]{:S(2)}, u32[]{:S(2)}) collective-permute-start(bf16[256,256]{1,0:T(8,128)(2,1)} %get-tuple-element.137), channel_id=1, source_target_pairs={{0,2},{1,3},{2,0},{3,1},{4,6},{5,7},{6,4},{7,5},{8,10},{9,11},{10,... | collective-permute-start | bytes 393224 | tf_op jit(solution)/shard_map/ppermute | solution.py:24
  317.0 13.8 %all-to-all-start.2 = ((bf16[8,80,128]{2,1,0:T(8,128)(2,1)}), bf16[8,80,128]{2,1,0:T(8,128)(2,1)S(1)}, u32[]{:S(2)}, u32[]{:S(2)}) async-start(bf16[8,80,128]{2,1,0:T(8,128)(2,1)} %broadcast_in_dim.5), calls=%async_computation.2 | async-start | bytes 327680 | tf_op jit(solution)/shard_map/all_to_all | solution.py:470
  322.1 14.8 %collective-permute-start.55 = (f32[1,128,256]{2,1,0:T(8,128)}, f32[1,128,256]{2,1,0:T(8,128)S(1)}, u32[]{:S(2)}, u32[]{:S(2)}) collective-permute-start(f32[1,128,256]{2,1,0:T(8,128)} %constant_dynamic-slice_fusion), channel_id=1, source_target_pairs={{0,16},{4,20},{8,24},{12,28},{16,0},{20,4},{24,8},{28,12},{1,17},{... | collective-permute-start | bytes 393224 | tf_op jit(solution)/shard_map/ppermute | solution.py:24
  331.5 10.8 %all-to-all-start.1 = ((bf16[32,16,128]{2,1,0:T(8,128)(2,1)}), bf16[32,16,128]{2,1,0:T(8,128)(2,1)S(1)}, u32[]{:S(2)}, u32[]{:S(2)}) async-start(bf16[32,16,128]{2,1,0:T(8,128)(2,1)} %broadcast_in_dim.4), calls=%async_computation.1 | async-start | bytes 262144 | tf_op jit(solution)/shard_map/all_to_all | solution.py:494
  (61 other events, 1193.5 us)
